TPU v7x, 128 devices: a whole 4x4x4 slice. The times are simulated.
128 devices in a mesh: row: 16 (over y, x), col: 4 (over z), dp: 2 (over core).
Axes of the slice: x: 4, y: 4, z: 4, core: 2. Of those that a mesh axis runs over, the one named last changes fastest.
Arguments:
- inputs: bfloat16 [1024, 8192], P(('col', 'dp'), 'row'), may hold values from -6 to 6
- gate_weight: bfloat16 [8192, 14336], P('row', 'col'), may hold values from -0.0625 to 0.0625
- up_weight: bfloat16 [8192, 14336], P('row', 'col'), may hold values from -0.0625 to 0.0625
- down_weight: bfloat16 [14336, 8192], P('col', 'row'), may hold values from -0.046875 to 0.046875
- reward_head: bfloat16 [8192], P('row'), may hold values from -0.0625 to 0.0625
- upstream: bfloat16 [1024, 8192], P(('col', 'dp'), 'row'), may hold values from -0.59765625 to 0.59765625
- labels: int32 [1024], P(('col', 'dp')), may hold values from 0 to 1
- label_mask: int32 [1024], P(('col', 'dp')), may hold values 0 or 1
Outputs:
- gate_grad: float32 [8192, 14336], P(('row', 'dp'), 'col')
- up_grad: float32 [8192, 14336], P(('row', 'dp'), 'col')
- down_grad: float32 [14336, 8192], P(('col', 'dp'), 'row')
- input_grad: float32 [1024, 8192], P(('col', 'dp'), 'row')
All inputs are finite; a program needn't handle non-finite values. No bound on the sum of `label_mask` on one device may be relied on, other than what follows from the above.
Results may differ from a plain program's by a relative error of at most 0.035.
Values may be sent and summed in bfloat16 or wider, within the bound.
No kernel may reach another device: no remote copies, remote signals or barrier semaphores. Data moves between devices by JAX's collectives and lax.ppermute only.
A program may use at most 128 MiB of HBM per device.

v0:
```python
import jax
import jax.numpy as jnp
from jax import lax
from jax.sharding import PartitionSpec as P

reward_weight = 8.0


def transpose_product(left, right):
    return lax.dot_general(
        left, right, (((0,), (0,)), ((), ())), preferred_element_type=jnp.float32
    )


def right_transpose(left, right):
    return lax.dot_general(
        left, right, (((1,), (1,)), ((), ())), preferred_element_type=jnp.float32
    )


def gather_tokens(block):
    return lax.all_gather(block, "col", axis=0, tiled=True)


def gather_hidden(stacked):
    return lax.all_gather(stacked, "row", axis=1, tiled=True)


def column_total(term_fn, count_rows):
    return lax.psum_scatter(
        term_fn(jnp.int32(0), count_rows * lax.axis_size("col")).astype(jnp.bfloat16),
        "col",
        scatter_dimension=0,
        tiled=True,
    ).astype(jnp.float32)


def per_device(
    inputs, gate_weight, up_weight, down_weight, reward_head, upstream, labels, label_mask
):
    width = gate_weight.shape[1]
    gathered = gather_tokens(inputs)
    rows = gathered
    joined = lax.psum_scatter(
        jnp.concatenate(
            [
                jnp.dot(rows, gate_weight, preferred_element_type=jnp.float32),
                jnp.dot(rows, up_weight, preferred_element_type=jnp.float32),
            ],
            axis=1,
        ).astype(jnp.bfloat16),
        "row",
        scatter_dimension=0,
        tiled=True,
    ).astype(jnp.float32)
    gate = joined[:, :width]
    upper = joined[:, width:]
    sigmoid_gate = jax.nn.sigmoid(gate)
    hidden = (gate * sigmoid_gate * upper).astype(jnp.bfloat16)
    hidden_all = gather_hidden(hidden[None])[0]

    def output_term(start, count):
        return jnp.dot(hidden_all, down_weight, preferred_element_type=jnp.float32)

    mixed = column_total(output_term, inputs.shape[0])
    outcome = inputs.astype(jnp.float32) + mixed
    head_value = reward_head.astype(jnp.float32)
    partial_score = jnp.dot(outcome, head_value, precision=lax.Precision.HIGHEST)
    score = lax.psum(partial_score, "row")
    slope = (
        reward_weight
        * label_mask.astype(jnp.float32)
        * (jax.nn.sigmoid(score) - labels.astype(jnp.float32))
    )
    grad_out = upstream.astype(jnp.float32) + slope[:, None] * head_value[None, :]
    grad_mixed = grad_out.astype(jnp.bfloat16)
    grad_rows = gather_tokens(grad_mixed)
    rows = grad_rows
    grad_hidden = lax.psum_scatter(
        right_transpose(rows, down_weight).astype(jnp.bfloat16),
        "row",
        scatter_dimension=0,
        tiled=True,
    ).astype(jnp.float32)
    grad_gate = (grad_hidden * upper * sigmoid_gate * (1.0 + gate * (1.0 - sigmoid_gate))).astype(
        jnp.bfloat16
    )
    grad_upper = (grad_hidden * gate * sigmoid_gate).astype(jnp.bfloat16)
    grads_all = gather_hidden(jnp.stack([grad_gate, grad_upper]))

    def input_term(start, count):
        return right_transpose(grads_all[0], gate_weight) + right_transpose(grads_all[1], up_weight)

    input_grad = grad_out + column_total(input_term, inputs.shape[0])
    gate_grad, up_grad, down_grad = (
        lax.psum_scatter(
            transpose_product(gathered, grads_all[0]).astype(jnp.bfloat16),
            "dp",
            scatter_dimension=0,
            tiled=True,
        ).astype(jnp.float32),
        lax.psum_scatter(
            transpose_product(gathered, grads_all[1]).astype(jnp.bfloat16),
            "dp",
            scatter_dimension=0,
            tiled=True,
        ).astype(jnp.float32),
        lax.psum_scatter(
            transpose_product(hidden_all, grad_rows).astype(jnp.bfloat16),
            "dp",
            scatter_dimension=0,
            tiled=True,
        ).astype(jnp.float32),
    )
    return (gate_grad, up_grad, down_grad, input_grad)


def solution(mesh):
    in_specs = (
        P(("col", "dp"), "row"),
        P("row", "col"),
        P("row", "col"),
        P("col", "row"),
        P("row"),
        P(("col", "dp"), "row"),
        P(("col", "dp")),
        P(("col", "dp")),
    )
    out_specs = (
        P(("row", "dp"), "col"),
        P(("row", "dp"), "col"),
        P(("col", "dp"), "row"),
        P(("col", "dp"), "row"),
    )
    return jax.shard_map(
        per_device, mesh=mesh, in_specs=in_specs, out_specs=out_specs, check_vma=False
    )
```

profile of v0, /device:TPU:1, one launch (start us, length us, event | category | flops | bytes accessed | tf_op | source)
XLA Modules:
  0.0 488.5 jit_solution(17730826505208931112)
XLA Ops:
  7.2 13.6 %all_gather.12 = bf16[512,512]{1,0:T(8,128)(2,1)S(1)} all-gather(bf16[128,512]{1,0:T(8,128)(2,1)} %param.8), channel_id=1, replica_groups=mesh['row'=16,'col'=4,'dp'=2] {'col'}, dimensions={0}, use_global_device_ids=true | all-gather | bytes 655360 | tf_op jit(solution)/shard_map/all_gather | solution.py:22
  20.8 4.3 convolution_convert_fusion.4
  25.1 3.9 convolution_convert_fusion.5
  29.0 6.0 %pad_maximum_fusion = bf16[512,7168]{1,0:T(8,128)(2,1)} fusion(bf16[512,3584]{1,0:T(8,128)(2,1)S(1)} %convolution_convert_fusion.4, bf16[512,3584]{1,0:T(8,128)(2,1)} %convolution_convert_fusion.5), kind=kLoop, calls=%fused_computation | loop fusion | flops 14680064 | bytes 14680064 | tf_op jit(solution)/shard_map/concatenate | solution.py:45
  35.1 84.9 %reduce-scatter.8.cloned.1.call-done = bf16[32,7168]{1,0:T(8,128)(2,1)} async-done(((bf16[512,7168]{1,0:T(8,128)(2,1)}), bf16[32,7168]{1,0:T(8,128)(2,1)}) %reduce-scatter.8.cloned.1.call-update) | async-done | bytes 458768 | tf_op jit(solution)/shard_map/reduce_scatter | solution.py:44
  122.0 50.6 %all-gather.6.cloned.1.call-done = bf16[512,3584]{1,0:T(8,128)(2,1)} async-done(((bf16[32,3584]{1,0:T(8,128)(2,1)}), bf16[512,3584]{1,0:T(8,128)(2,1)}) %all-gather.6.cloned.1.call-update) | async-done | bytes 3670032 | tf_op jit(solution)/shard_map/all_gather | solution.py:26
  172.7 6.0 %convolution_convert_fusion.6 = bf16[512,512]{1,0:T(8,128)(2,1)} fusion(bf16[512,3584]{1,0:T(8,128)(2,1)} %all-gather.6.cloned.1.call-done, bf16[3584,512]{1,0:T(8,128)(2,1)} %param.11), kind=kOutput, calls=%fused_computation.15 | convolution fusion | flops 1879310336 | bytes 7864320 | tf_op jit(solution)/shard_map/dot_general | solution.py:63
  178.8 19.6 %reduce-scatter.10.cloned.1.call-done = bf16[128,512]{1,0:T(8,128)(2,1)} async-done(((bf16[512,512]{1,0:T(8,128)(2,1)}), bf16[128,512]{1,0:T(8,128)(2,1)}) %reduce-scatter.10.cloned.1.call-update) | async-done | bytes 131088 | tf_op jit(solution)/shard_map/reduce_scatter | solution.py:30
  199.5 33.2 %psum.7 = f32[128]{0:T(128)S(1)} all-reduce(f32[128]{0:T(128)S(1)} %convolution_bitcast_fusion), channel_id=1, replica_groups=mesh['row'=16,'col'=4,'dp'=2] {'row'}, use_global_device_ids=true, to_apply=%region_2.0 | all-reduce | flops 128 | bytes 1024 | tf_op jit(solution)/shard_map/psum | solution.py:69
  232.8 10.2 %all_gather.14 = bf16[512,512]{1,0:T(8,128)(2,1)S(1)} all-gather(bf16[128,512]{1,0:T(8,128)(2,1)S(1)} %fusion.14), channel_id=1, replica_groups=mesh['row'=16,'col'=4,'dp'=2] {'col'}, dimensions={0}, use_global_device_ids=true | all-gather | bytes 655360 | tf_op jit(solution)/shard_map/all_gather | solution.py:22
  243.0 6.0 %convolution_convert_fusion.3 = bf16[512,3584]{1,0:T(8,128)(2,1)} fusion(bf16[512,512]{1,0:T(8,128)(2,1)S(1)} %all_gather.14, bf16[3584,512]{1,0:T(8,128)(2,1)} %param.11), kind=kOutput, calls=%fused_computation.4 | convolution fusion | flops 1880883200 | bytes 7864320 | tf_op jit(solution)/shard_map/dot_general | solution.py:16
  249.1 81.0 %reduce-scatter.12.cloned.1.call-done = bf16[32,3584]{1,0:T(8,128)(2,1)} async-done(((bf16[512,3584]{1,0:T(8,128)(2,1)}), bf16[32,3584]{1,0:T(8,128)(2,1)}) %reduce-scatter.12.cloned.1.call-update) | async-done | bytes 229392 | tf_op jit(solution)/shard_map/reduce_scatter | solution.py:79
  332.1 6.0 %convolution_convert_fusion = bf16[3584,512]{1,0:T(8,128)(2,1)} fusion(bf16[512,3584]{1,0:T(8,128)(2,1)} %all-gather.6.cloned.1.call-done, bf16[512,512]{1,0:T(8,128)(2,1)S(1)} %all_gather.14), kind=kOutput, calls=%fused_computation.1 | convolution fusion | flops 1880883200 | bytes 7864320 | tf_op jit(solution)/shard_map/dot_general | solution.py:10
  338.1 61.8 %all-gather.4.cloned.1.call-done = bf16[2,512,3584]{2,1,0:T(8,128)(2,1)} async-done(((bf16[2,32,3584]{2,1,0:T(8,128)(2,1)}), bf16[2,512,3584]{2,1,0:T(8,128)(2,1)}) %all-gather.4.cloned.1.call-update) | async-done | bytes 7340048 | tf_op jit(solution)/shard_map/all_gather | solution.py:26
  399.9 5.4 %fusion.2 = f32[512,512]{1,0:T(8,128)S(1)} fusion(bf16[512,3584]{1,0:T(8,128)(2,1)} %param.9, bf16[2,512,3584]{2,1,0:T(8,128)(2,1)} %all-gather.4.cloned.1.call-done), kind=kOutput, calls=%fused_computation.11 | convolution fusion | flops 1879048192 | bytes 8388608 | tf_op jit(solution)/shard_map/dot_general | solution.py:16
  406.1 2.9 fusion.5
  409.3 6.0 %fusion.1 = bf16[512,3584]{0,1:T(8,128)(2,1)} fusion(bf16[512,512]{1,0:T(8,128)(2,1)S(1)} %all_gather.12, bf16[2,512,3584]{2,1,0:T(8,128)(2,1)} %all-gather.4.cloned.1.call-done), kind=kOutput, calls=%fused_computation.8 | convolution fusion | flops 1880883200 | bytes 7864320 | tf_op jit(solution)/shard_map/dot_general | solution.py:10
  415.4 6.3 %fusion = bf16[512,3584]{0,1:T(8,128)(2,1)} fusion(bf16[512,512]{1,0:T(8,128)(2,1)S(1)} %all_gather.12, bf16[2,512,3584]{2,1,0:T(8,128)(2,1)} %all-gather.4.cloned.1.call-done), kind=kOutput, calls=%fused_computation.7 | convolution fusion | flops 1880883200 | bytes 7864320 | tf_op jit(solution)/shard_map/dot_general | solution.py:10
  421.7 3.9 convert_element_type.94
  425.5 14.9 %reduce-scatter.20.cloned.1.call-done = bf16[128,512]{1,0:T(8,128)(2,1)} async-done(((bf16[512,512]{1,0:T(8,128)(2,1)}), bf16[128,512]{1,0:T(8,128)(2,1)}) %reduce-scatter.20.cloned.1.call-update) | async-done | bytes 131088 | tf_op jit(solution)/shard_map/reduce_scatter | solution.py:30
  442.2 17.1 %reduce-scatter.16.cloned.1.call-done = bf16[256,3584]{0,1:T(8,128)(2,1)} async-done(((bf16[512,3584]{0,1:T(8,128)(2,1)}), bf16[256,3584]{0,1:T(8,128)(2,1)}) %reduce-scatter.16.cloned.1.call-update) | async-done | bytes 1835024 | tf_op jit(solution)/shard_map/reduce_scatter | solution.py:102
  459.3 4.0 copy.13
  463.3 14.7 %reduce-scatter.14.cloned.1.call-done = bf16[256,3584]{0,1:T(8,128)(2,1)} async-done(((bf16[512,3584]{0,1:T(8,128)(2,1)}), bf16[256,3584]{0,1:T(8,128)(2,1)}) %reduce-scatter.14.cloned.1.call-update) | async-done | bytes 1835024 | tf_op jit(solution)/shard_map/reduce_scatter | solution.py:96
  478.0 4.0 copy.12
  (45 shorter events, 8.4 us)
Async XLA Ops:
  7.2 112.8 %reduce-scatter.8.cloned.1.call-start = ((), (), s32[]{:S(2)}) async-start(), calls=%async_computation.7 | async-start | bytes 7798784 | tf_op jit(solution)/shard_map/reduce_scatter | solution.py:44
  20.8 4.3 copy-start.6
  35.0 137.6 %all-gather.6.cloned.1.call-start = ((), (), s32[]{:S(2)}) async-start(), calls=%async_computation.15 | async-start | bytes 3899392 | tf_op jit(solution)/shard_map/all_gather | solution.py:26
  121.9 56.8 %copy-start.2 = (bf16[512]{0:T(512)(128)(2,1)S(1)}, bf16[512]{0:T(512)(128)(2,1)}, u32[]{:S(2)}) copy-start(bf16[512]{0:T(512)(128)(2,1)} %param.12) | copy-start | bytes 3076
  121.9 76.5 %copy-start = (bf16[128,512]{1,0:T(8,128)(2,1)S(1)}, bf16[128,512]{1,0:T(8,128)(2,1)}, u32[]{:S(2)}) copy-start(bf16[128,512]{1,0:T(8,128)(2,1)} %param.8) | copy-start | bytes 393220
  122.0 110.7 %copy-start.3 = (s32[128]{0:T(128)S(1)}, s32[128]{0:T(128)}, u32[]{:S(2)}) copy-start(s32[128]{0:T(128)} %param.14) | copy-start | bytes 1540
  122.0 110.7 %copy-start.4 = (s32[128]{0:T(128)S(1)}, s32[128]{0:T(128)}, u32[]{:S(2)}) copy-start(s32[128]{0:T(128)} %param.15) | copy-start | bytes 1540
  122.0 110.7 %copy-start.1 = (bf16[128,512]{1,0:T(8,128)(2,1)S(1)}, bf16[128,512]{1,0:T(8,128)(2,1)}, u32[]{:S(2)}) copy-start(bf16[128,512]{1,0:T(8,128)(2,1)} %param.13) | copy-start | bytes 393220
  122.0 76.4 %reduce-scatter.10.cloned.1.call-start = ((), (), s32[]{:S(2)}) async-start(), calls=%async_computation.8 | async-start | bytes 655360 | tf_op jit(solution)/shard_map/reduce_scatter | solution.py:30
  178.7 151.3 %reduce-scatter.12.cloned.1.call-start = ((), (), s32[]{:S(2)}) async-start(), calls=%async_computation.9 | async-start | bytes 3899392 | tf_op jit(solution)/shard_map/reduce_scatter | solution.py:79
  249.0 150.9 %all-gather.4.cloned.1.call-start = ((), (), s32[]{:S(2)}) async-start(), calls=%async_computation.10 | async-start | bytes 7798784 | tf_op jit(solution)/shard_map/all_gather | solution.py:26
  332.0 89.7 %reduce-scatter.18.cloned.1.call-start = ((), (), s32[]{:S(2)}) async-start(), calls=%async_computation.13 | async-start | bytes 5505024 | tf_op jit(solution)/shard_map/reduce_scatter | solution.py:108
  338.1 102.4 %reduce-scatter.20.cloned.1.call-start = ((), (), s32[]{:S(2)}) async-start(), calls=%async_computation.14 | async-start | bytes 655360 | tf_op jit(solution)/shard_map/reduce_scatter | solution.py:30
  399.9 5.4 %copy-start.5 = (bf16[2,512,3584]{2,1,0:T(8,128)(2,1)S(1)}, bf16[2,512,3584]{2,1,0:T(8,128)(2,1)}, u32[]{:S(2)}) copy-start(bf16[2,512,3584]{2,1,0:T(8,128)(2,1)} %all-gather.4.cloned.1.call-done) | copy-start | bytes 22020100
  399.9 6.3 %copy-start.7 = (bf16[512,3584]{1,0:T(8,128)(2,1)S(1)}, bf16[512,3584]{1,0:T(8,128)(2,1)}, u32[]{:S(2)}) copy-start(bf16[512,3584]{1,0:T(8,128)(2,1)} %param.10) | copy-start | bytes 11010052
  409.1 50.3 %reduce-scatter.16.cloned.1.call-start = ((), (), s32[]{:S(2)}) async-start(), calls=%async_computation.12 | async-start | bytes 5505024 | tf_op jit(solution)/shard_map/reduce_scatter | solution.py:102
  415.3 62.7 %reduce-scatter.14.cloned.1.call-start = ((), (), s32[]{:S(2)}) async-start(), calls=%async_computation.11 | async-start | bytes 5505024 | tf_op jit(solution)/shard_map/reduce_scatter | solution.py:96
Sparse Core Ops, SparseCore 0:
  35.1 84.8 reduce-scatter.7
  122.9 49.6 all-gather.5
  178.8 19.5 reduce-scatter.9
  249.1 80.8 reduce-scatter.11
  332.8 67.0 all-gather.3
  402.8 14.3 reduce-scatter.17
  419.6 20.8 reduce-scatter.19
  443.4 15.8 reduce-scatter.15
  462.4 15.5 reduce-scatter.13
where the time goes:
time: 489 us; the launch traced here: 488 us
  waiting for transfers between devices  345 us (71%)
  blocking collectives  56.9 us (12%)
  matrix products  47.8 us (10%)
  other arithmetic  15.5 us (3%)
  between operations  14 us (3%)
  local copies, waits for them, and re-layouts  8.87 us (2%)
    all_gather x2, waiting for transfers between devices, gather_hidden(): return lax.all_gather(stacked, 'row', axis=1, tiled=True)  112 us
    reduce_scatter x1, waiting for transfers between devices, per_device(): lax.psum_scatter(jnp.concatenate([jnp.dot(rows, gate_weight, preferred_el...  84.9 us
    reduce_scatter x1, waiting for transfers between devices, per_device(): lax.psum_scatter(right_transpose(rows, down_weight).astype(jnp.bfloat16),...  81 us
    reduce_scatter x2, waiting for transfers between devices, column_total(): lax.psum_scatter(term_fn(jnp.int32(0), count_rows * lax.axis_size('col'))...  34.6 us
    psum x1, blocking collectives, per_device(): score = lax.psum(partial_score, 'row')  33.2 us
    all_gather x2, blocking collectives, gather_tokens(): return lax.all_gather(block, 'col', axis=0, tiled=True)  23.8 us
    dot_general x3, matrix products, transpose_product(): lax.dot_general(left, right, (((0,), (0,)), ((), ())), preferred_element_...  18.2 us
    reduce_scatter x1, waiting for transfers between devices, per_device(): lax.psum_scatter(transpose_product(gathered, grads_all[1]).astype(jnp.bfl...  17.1 us
  transfers between devices with their start and end apart: 9, of which 8 were waited for; matrix products, arithmetic and copies ran while one was open for 7% of the time, Pallas kernels for 0%

commit v1 on v0

v1 whole, which is shorter than its diff:
```python
import jax
import jax.numpy as jnp
from jax import lax
from jax.sharding import PartitionSpec as P

reward_weight = 8.0
BF = jnp.bfloat16
F32 = jnp.float32


def transpose_product(left, right):
    return lax.dot_general(
        left, right, (((0,), (0,)), ((), ())), preferred_element_type=F32
    )


def right_transpose(left, right):
    return lax.dot_general(
        left, right, (((1,), (1,)), ((), ())), preferred_element_type=F32
    )


def per_device(
    inputs, gate_weight, up_weight, down_weight, reward_head, upstream, labels, label_mask
):
    tokens, depth = inputs.shape
    half = gate_weight.shape[1] // 2
    n_row = lax.axis_size("row")
    core = lax.axis_index("dp")
    row = lax.axis_index("row")
    token_axes = ("col", "dp")

    tags = jnp.stack([labels, label_mask], axis=1).astype(BF)
    tags = jnp.pad(tags, ((0, 0), (0, 126)))
    packed = jnp.concatenate([inputs, upstream, tags], axis=1)
    everyone = lax.all_gather(packed, token_axes, axis=0, tiled=True)
    x_all = everyone[:, :depth]
    upstream_all = everyone[:, depth : 2 * depth]
    total = x_all.shape[0]
    mine = total // n_row

    gate_half = lax.dynamic_slice_in_dim(gate_weight, core * half, half, 1)
    up_half = lax.dynamic_slice_in_dim(up_weight, core * half, half, 1)
    down_half = lax.dynamic_slice_in_dim(down_weight, core * half, half, 0)
    head_value = reward_head.astype(F32)

    head_hidden = jnp.dot(down_half.astype(F32), head_value, precision=lax.Precision.HIGHEST)
    head_inputs = jnp.dot(x_all.astype(F32), head_value, precision=lax.Precision.HIGHEST)
    per_token = half // mine
    extras = jnp.concatenate(
        [
            head_inputs[:, None],
            jnp.tile(head_hidden.reshape(mine, per_token), (n_row, 1)),
            jnp.zeros((total, 127 - per_token), F32),
        ],
        axis=1,
    )
    partial = jnp.concatenate(
        [
            jnp.dot(x_all, gate_half, preferred_element_type=F32).astype(BF),
            jnp.dot(x_all, up_half, preferred_element_type=F32).astype(BF),
            right_transpose(upstream_all, down_half).astype(BF),
            extras.astype(BF),
        ],
        axis=1,
    )
    summed = lax.psum_scatter(partial, "row", scatter_dimension=0, tiled=True).astype(F32)
    gate = summed[:, :half]
    upper = summed[:, half : 2 * half]
    grad_upstream = summed[:, 2 * half : 3 * half]
    extra = summed[:, 3 * half :]
    head_hidden = extra[:, 1 : 1 + per_token].reshape(half)

    sigmoid_gate = jax.nn.sigmoid(gate)
    hidden = (gate * sigmoid_gate * upper).astype(BF)
    score = extra[:, 0] + lax.psum(
        jnp.sum(hidden.astype(F32) * head_hidden[None, :], axis=1), token_axes
    )
    own_tags = lax.dynamic_slice_in_dim(everyone[:, 2 * depth :], row * mine, mine, 0).astype(F32)
    slope = reward_weight * own_tags[:, 1] * (jax.nn.sigmoid(score) - own_tags[:, 0])
    grad_hidden = grad_upstream + slope[:, None] * head_hidden[None, :]
    grad_gate = (grad_hidden * upper * sigmoid_gate * (1.0 + gate * (1.0 - sigmoid_gate))).astype(
        BF
    )
    grad_upper = (grad_hidden * gate * sigmoid_gate).astype(BF)
    slope_high = slope.astype(BF)
    slope_low = (slope - slope_high.astype(F32)).astype(BF)
    slopes = jnp.pad(jnp.stack([slope_high, slope_low], axis=1), ((0, 0), (0, 126)))
    gathered = lax.all_gather(
        jnp.concatenate([hidden, grad_gate, grad_upper, slopes], axis=1), "row", axis=0, tiled=True
    )
    hidden_all = gathered[:, :half]
    grad_gate_all = gathered[:, half : 2 * half]
    grad_upper_all = gathered[:, 2 * half : 3 * half]
    slope_all = gathered[:, 3 * half].astype(F32) + gathered[:, 3 * half + 1].astype(F32)

    input_part = right_transpose(grad_gate_all, gate_half) + right_transpose(
        grad_upper_all, up_half
    )
    input_sum = lax.psum_scatter(
        input_part.astype(BF), token_axes, scatter_dimension=0, tiled=True
    ).astype(F32)
    place = (lax.axis_index("col") * 2 + core) * tokens
    own_slope = lax.dynamic_slice_in_dim(slope_all, place, tokens, 0)
    input_grad = (
        upstream.astype(F32) + own_slope[:, None] * head_value[None, :] + input_sum
    )

    grad_mixed = (
        upstream_all.astype(F32) + slope_all[:, None] * head_value[None, :]
    ).astype(BF)
    down_grad = transpose_product(hidden_all, grad_mixed)

    def both_halves(part):
        keep = lax.dynamic_slice_in_dim(part, core * (depth // 2), depth // 2, 0)
        send = lax.dynamic_slice_in_dim(part, (1 - core) * (depth // 2), depth // 2, 0)
        other = lax.ppermute(send.astype(BF), "dp", [(0, 1), (1, 0)]).astype(F32)
        first = core == 0
        return jnp.concatenate(
            [jnp.where(first, keep, other), jnp.where(first, other, keep)], axis=1
        )

    gate_grad = both_halves(transpose_product(x_all, grad_gate_all))
    up_grad = both_halves(transpose_product(x_all, grad_upper_all))
    return (gate_grad, up_grad, down_grad, input_grad)


def solution(mesh):
    in_specs = (
        P(("col", "dp"), "row"),
        P("row", "col"),
        P("row", "col"),
        P("col", "row"),
        P("row"),
        P(("col", "dp"), "row"),
        P(("col", "dp")),
        P(("col", "dp")),
    )
    out_specs = (
        P(("row", "dp"), "col"),
        P(("row", "dp"), "col"),
        P(("col", "dp"), "row"),
        P(("col", "dp"), "row"),
    )
    return jax.shard_map(
        per_device, mesh=mesh, in_specs=in_specs, out_specs=out_specs, check_vma=False
    )
```

time: 489 us -> 314 us (0.64)
  waiting for transfers between devices: 345 us -> 205 us
  blocking collectives: 56.9 us -> 13.1 us
  local copies, waits for them, and re-layouts: 8.87 us -> 21.9 us
  matrix products: 47.8 us -> 42 us
    reduce_scatter x7 -> x2, waiting for transfers between devices: 232 us -> 95.9 us  [the longest x1 89.5 us: per_device(): lax.psum_scatter(partial, 'row', scatter_dimension=0, tiled=True)]
    all_gather x2 -> x0, blocking collectives: 23.8 us -> none  [gather_tokens(): return lax.all_gather(block, 'col', axis=0, tiled=True)]
    psum x1, blocking collectives: 33.2 us -> 13.1 us  [per_device(): lax.psum(jnp.sum(hidden.astype(F32) * head_hidden[None, :], axis=1), toke...]
    concatenate x0 -> x1, local copies, waits for them, and re-layouts: none -> 18.4 us  [per_device(): jnp.concatenate([jnp.dot(x_all, gate_half, preferred_element_type=F32).as...]
    unnamed x19 -> x16, local copies, waits for them, and re-layouts: 8.87 us -> 0.86 us
  transfers between devices with their start and end apart: 9 -> 6, of which waited for: 8 -> 4; matrix products, arithmetic and copies ran while one was open for 7% -> 8% of each run, Pallas kernels for 0% -> 0%
where the time goes in v1:
time: 314 us; the launch traced here: 310 us
  waiting for transfers between devices  205 us (65%)
  matrix products  42 us (13%)
  local copies, waits for them, and re-layouts  21.9 us (7%)
  between operations  14 us (4%)
  other arithmetic  13.6 us (4%)
  blocking collectives  13.1 us (4%)
    reduce_scatter x1, waiting for transfers between devices, per_device(): lax.psum_scatter(partial, 'row', scatter_dimension=0, tiled=True)  89.5 us
    all_gather x1, waiting for transfers between devices, per_device(): lax.all_gather(jnp.concatenate([hidden, grad_gate, grad_upper, slopes], a...  81.6 us
    all_gather x1, waiting for transfers between devices, per_device(): everyone = lax.all_gather(packed, token_axes, axis=0, tiled=True)  27 us
    concatenate x1, local copies, waits for them, and re-layouts, per_device(): jnp.concatenate([jnp.dot(x_all, gate_half, preferred_element_type=F32).as...  18.4 us
    dot_general x3, matrix products, right_transpose(): lax.dot_general(left, right, (((1,), (1,)), ((), ())), preferred_element_...  16 us
    dot_general x3, matrix products, transpose_product(): lax.dot_general(left, right, (((0,), (0,)), ((), ())), preferred_element_...  14.4 us
    psum x1, blocking collectives, per_device(): lax.psum(jnp.sum(hidden.astype(F32) * head_hidden[None, :], axis=1), toke...  13.1 us
    reduce_scatter x1, waiting for transfers between devices, per_device(): lax.psum_scatter(input_part.astype(BF), token_axes, scatter_dimension=0,...  6.42 us
  transfers between devices with their start and end apart: 6, of which 4 were waited for; matrix products, arithmetic and copies ran while one was open for 8% of the time, Pallas kernels for 0%

profile of v1, /device:TPU:1, one launch (start us, length us, event | category | flops | bytes accessed | tf_op | source)
XLA Modules:
  0.0 310.4 jit_solution(9628465307973189131)
XLA Ops:
  8.0 1.7 fusion.37
  10.5 2.1 fusion.22
  12.7 27.0 %all-gather.3.cloned.1.call-done = bf16[1024,1152]{1,0:T(8,128)(2,1)} async-done(((bf16[128,1152]{1,0:T(8,128)(2,1)}), bf16[1024,1152]{1,0:T(8,128)(2,1)}) %all-gather.3.cloned.1.call-update) | async-done | bytes 2359312 | tf_op jit(solution)/shard_map/all_gather | solution.py:36
  39.8 1.6 fusion.33
  41.6 5.9 %convolution_convert_fusion = bf16[1024,1792]{1,0:T(8,128)(2,1)} fusion(bf16[3584,512]{1,0:T(8,128)(2,1)} %param.11, s32[]{:T(128)S(6)} %select_n.40, bf16[1024,1152]{1,0:T(8,128)(2,1)} %all-gather.3.cloned.1.call-done), kind=kOutput, calls=%fused_computation | convolution fusion | flops 1880883200 | bytes 6553604 | tf_op jit(solution)/shard_map/dot_general | solution.py:18
  47.5 3.9 %convolution_convert_fusion.1 = bf16[1024,1792]{1,0:T(8,128)(2,1)} fusion(bf16[512,3584]{1,0:T(8,128)(2,1)S(1)} %copy-done.4, s32[]{:T(128)S(6)} %select_n.40, bf16[1024,1152]{1,0:T(8,128)(2,1)S(1)} %copy-done), kind=kOutput, calls=%fused_computation.1 | convolution fusion | flops 1880883200 | bytes 6553604 | tf_op jit(solution)/shard_map/dot_general | solution.py:61
  51.5 3.9 %convolution_convert_fusion.2 = bf16[1024,1792]{1,0:T(8,128)(2,1)} fusion(bf16[512,3584]{1,0:T(8,128)(2,1)S(1)} %copy-done.5, s32[]{:T(128)S(6)} %select_n.40, bf16[1024,1152]{1,0:T(8,128)(2,1)S(1)} %copy-done), kind=kOutput, calls=%fused_computation.2 | convolution fusion | flops 1880883200 | bytes 6553604 | tf_op jit(solution)/shard_map/dot_general | solution.py:60
  55.5 18.4 %concatenate.19 = bf16[1024,5504]{1,0:T(8,128)(2,1)} concatenate(bf16[1024,1792]{1,0:T(8,128)(2,1)} %convolution_convert_fusion.2, bf16[1024,1792]{1,0:T(8,128)(2,1)} %convolution_convert_fusion.1, bf16[1024,1792]{1,0:T(8,128)(2,1)} %convolution_convert_fusion, bf16[1024,1]{1,0:T(8,128)(2,1)S(1)} %broadcast_in_dim.14, bf16[1024,28]{1,0:T(8,128)(2,1)S(1)} %bitcast.12, ...), dimensions={1} | concatenate | bytes 22544384 | tf_op jit(solution)/shard_map/concatenate | solution.py:58
  75.0 89.5 %reduce-scatter.3.cloned.1.call-done = bf16[64,5504]{1,0:T(8,128)(2,1)} async-done(((bf16[1024,5504]{1,0:T(8,128)(2,1)}), bf16[64,5504]{1,0:T(8,128)(2,1)}) %reduce-scatter.3.cloned.1.call-update) | async-done | bytes 704528 | tf_op jit(solution)/shard_map/reduce_scatter | solution.py:67
  165.4 1.2 convert_element_type.87
  166.9 13.1 %psum.7 = f32[64]{0:T(128)S(1)} all-reduce(f32[64]{0:T(128)S(1)} %get-tuple-element.8), channel_id=1, replica_groups=mesh['row'=16,'col'=4,'dp'=2] {'col','dp'}, use_global_device_ids=true, to_apply=%region_2.3 | all-reduce | flops 64 | bytes 512 | tf_op jit(solution)/shard_map/psum | solution.py:76
  180.5 0.9 fusion.29
  181.5 81.6 %all-gather.5.cloned.1.call-done = bf16[1024,5504]{1,0:T(8,128)(2,1)} async-done(((bf16[64,5504]{1,0:T(8,128)(2,1)}), bf16[1024,5504]{1,0:T(8,128)(2,1)}) %all-gather.5.cloned.1.call-update) | async-done | bytes 11272208 | tf_op jit(solution)/shard_map/all_gather | solution.py:89
  263.1 4.8 %fusion.2 = f32[1024,512]{1,0:T(8,128)S(1)} fusion(bf16[1024,5504]{1,0:T(8,128)(2,1)} %all-gather.5.cloned.1.call-done, bf16[512,3584]{1,0:T(8,128)(2,1)} %param.10, s32[]{:T(128)S(6)} %select_n.40), kind=kOutput, calls=%fused_computation.7 | convolution fusion | flops 1879048192 | bytes 7602180 | tf_op jit(solution)/shard_map/dot_general | solution.py:18
  268.0 5.2 %add_convert_fusion = bf16[1024,512]{1,0:T(8,128)(2,1)} fusion(f32[1024,512]{1,0:T(8,128)S(1)} %fusion.2, bf16[512,3584]{1,0:T(8,128)(2,1)S(1)} %copy-done.6, s32[]{:T(128)S(6)} %select_n.40, bf16[1024,5504]{1,0:T(8,128)(2,1)} %all-gather.5.cloned.1.call-done), kind=kOutput, calls=%fused_computation.19 | convolution fusion | flops 1880096768 | bytes 8650756 | tf_op jit(solution)/shard_map/dot_general | solution.py:18
  273.3 4.2 %fusion.4 = f32[512,1792]{1,0:T(8,128)S(1)} fusion(bf16[1024,5504]{1,0:T(8,128)(2,1)} %all-gather.5.cloned.1.call-done, bf16[1024,1152]{1,0:T(8,128)(2,1)S(1)} %copy-done.1), kind=kOutput, calls=%fused_computation.9 | convolution fusion | flops 1879048192 | bytes 8388608 | tf_op jit(solution)/shard_map/dot_general | solution.py:12
  277.6 0.9 collective-permute-start.1
  278.5 4.1 %fusion.8 = f32[512,1792]{1,0:T(8,128)S(1)} fusion(bf16[1024,5504]{1,0:T(8,128)(2,1)} %all-gather.5.cloned.1.call-done, bf16[1024,1152]{1,0:T(8,128)(2,1)S(1)} %copy-done.1), kind=kOutput, calls=%fused_computation.13 | convolution fusion | flops 1879048192 | bytes 8388608 | tf_op jit(solution)/shard_map/dot_general | solution.py:12
  282.8 1.5 convert_add_fusion
  284.5 6.1 %fusion = f32[1792,512]{1,0:T(8,128)} fusion(bf16[1024,5504]{1,0:T(8,128)(2,1)} %all-gather.5.cloned.1.call-done, f32[512]{0:T(512)S(1)} %convert_element_type.103, f32[1024]{0:T(1024)S(1)} %get-tuple-element.11, bf16[1024,1152]{1,0:T(8,128)(2,1)S(1)} %copy-done.1), kind=kOutput, calls=%fused_computation.3 | convolution fusion | flops 1881145344 | bytes 8394752 | tf_op jit(solution)/shard_map/dot_general | solution.py:12
  290.9 2.3 pad_maximum_fusion.1
  293.4 2.3 pad_maximum_fusion
  295.8 6.4 %reduce-scatter.5.cloned.1.call-done = bf16[128,512]{1,0:T(8,128)(2,1)} async-done(((bf16[1024,512]{1,0:T(8,128)(2,1)}), bf16[128,512]{1,0:T(8,128)(2,1)}) %reduce-scatter.5.cloned.1.call-update) | async-done | bytes 131088 | tf_op jit(solution)/shard_map/reduce_scatter | solution.py:100
  302.2 1.7 convert_add_fusion.1
  (53 shorter events, 5.8 us)
Async XLA Ops:
  7.2 32.6 %all-gather.3.cloned.1.call-start = ((), (), s32[]{:S(2)}) async-start(), calls=%async_computation.2 | async-start | bytes 2654208 | tf_op jit(solution)/shard_map/all_gather | solution.py:36
  9.8 154.7 %reduce-scatter.3.cloned.1.call-start = ((), (), s32[]{:S(2)}) async-start(), calls=%async_computation.3 | async-start | bytes 11976704 | tf_op jit(solution)/shard_map/reduce_scatter | solution.py:67
  41.6 5.9 %copy-start = (bf16[1024,1152]{1,0:T(8,128)(2,1)S(1)}, bf16[1024,1152]{1,0:T(8,128)(2,1)}, u32[]{:S(2)}) copy-start(bf16[1024,1152]{1,0:T(8,128)(2,1)} %all-gather.3.cloned.1.call-done) | copy-start | bytes 7077892
  41.6 5.9 %copy-start.4 = (bf16[512,3584]{1,0:T(8,128)(2,1)S(1)}, bf16[512,3584]{1,0:T(8,128)(2,1)}, u32[]{:S(2)}) copy-start(bf16[512,3584]{1,0:T(8,128)(2,1)} %param.10) | copy-start | bytes 11010052
  47.5 3.9 %copy-start.5 = (bf16[512,3584]{1,0:T(8,128)(2,1)S(1)}, bf16[512,3584]{1,0:T(8,128)(2,1)}, u32[]{:S(2)}) copy-start(bf16[512,3584]{1,0:T(8,128)(2,1)} %param.9) | copy-start | bytes 11010052
  73.9 0.9 slice-start
  73.9 189.2 %all-gather.5.cloned.1.call-start = ((), (), s32[]{:S(2)}) async-start(), calls=%async_computation.4 | async-start | bytes 11976704 | tf_op jit(solution)/shard_map/all_gather | solution.py:89
  166.7 14.8 %copy-start.3 = (bf16[512]{0:T(512)(128)(2,1)S(1)}, bf16[512]{0:T(512)(128)(2,1)}, u32[]{:S(2)}) copy-start(bf16[512]{0:T(512)(128)(2,1)} %param.12) | copy-start | bytes 3076
  181.4 120.7 %reduce-scatter.5.cloned.1.call-start = ((), (), s32[]{:S(2)}) async-start(), calls=%async_computation.5 | async-start | bytes 1179648 | tf_op jit(solution)/shard_map/reduce_scatter | solution.py:100
  263.1 4.9 %copy-start.6 = (bf16[512,3584]{1,0:T(8,128)(2,1)S(1)}, bf16[512,3584]{1,0:T(8,128)(2,1)}, u32[]{:S(2)}) copy-start(bf16[512,3584]{1,0:T(8,128)(2,1)} %param.9) | copy-start | bytes 11010052
  268.0 5.3 %copy-start.1 = (bf16[1024,1152]{1,0:T(8,128)(2,1)S(1)}, bf16[1024,1152]{1,0:T(8,128)(2,1)}, u32[]{:S(2)}) copy-start(bf16[1024,1152]{1,0:T(8,128)(2,1)} %all-gather.3.cloned.1.call-done) | copy-start | bytes 7077892
  277.6 13.0 %collective-permute-start.1 = (bf16[256,1792]{1,0:T(8,128)(2,1)S(1)}, bf16[256,1792]{1,0:T(8,128)(2,1)S(1)}, u32[]{:S(2)}, u32[]{:S(2)}) collective-permute-start(bf16[256,1792]{1,0:T(8,128)(2,1)S(1)} %dynamic-slice_convert_fusion), channel_id=1, source_target_pairs={{0,1},{1,0},{2,3},{3,2},{4,5},{5,4},{6,7},{7,6},{8,9},{9,8},{10,11... | collective-permute-start | bytes 2752520 | tf_op jit(solution)/shard_map/ppermute | solution.py:117
  282.8 10.4 %collective-permute-start = (bf16[256,1792]{1,0:T(8,128)(2,1)S(1)}, bf16[256,1792]{1,0:T(8,128)(2,1)S(1)}, u32[]{:S(2)}, u32[]{:S(2)}) collective-permute-start(bf16[256,1792]{1,0:T(8,128)(2,1)S(1)} %dynamic-slice_convert_fusion.1), channel_id=1, source_target_pairs={{0,1},{1,0},{2,3},{3,2},{4,5},{5,4},{6,7},{7,6},{8,9},{9,8},{10,11... | collective-permute-start | bytes 2752520 | tf_op jit(solution)/shard_map/ppermute | solution.py:117
  293.4 8.8 %copy-start.2 = (bf16[128,512]{1,0:T(8,128)(2,1)S(1)}, bf16[128,512]{1,0:T(8,128)(2,1)}, u32[]{:S(2)}) copy-start(bf16[128,512]{1,0:T(8,128)(2,1)} %param.13) | copy-start | bytes 393220
Sparse Core Ops, SparseCore 0:
  10.3 29.4 all-gather.2
  74.0 90.4 reduce-scatter.2
  181.6 81.5 all-gather.4
  273.4 28.7 reduce-scatter.4

commit v2 on v1

v2 whole, which is shorter than its diff:
```python
import jax
import jax.numpy as jnp
from jax import lax
from jax.experimental import pallas as pl
from jax.experimental.pallas import tpu as pltpu
from jax.sharding import PartitionSpec as P

reward_weight = 8.0
BF = jnp.bfloat16
F32 = jnp.float32
AXES = ("row", "col", "dp")
SIDE = 4


def transpose_product(left, right):
    return lax.dot_general(
        left, right, (((0,), (0,)), ((), ())), preferred_element_type=F32
    )


def right_transpose(left, right):
    return lax.dot_general(
        left, right, (((1,), (1,)), ((), ())), preferred_element_type=F32
    )


def product(left, right):
    return jnp.dot(left, right, preferred_element_type=F32)


def flat(y, x, z, c):
    return ((y * SIDE + x) * 4 + z) * 2 + c


def pairs(move):
    found = []
    for y in range(SIDE):
        for x in range(SIDE):
            for z in range(4):
                for c in range(2):
                    found.append((flat(y, x, z, c), flat(*move(y, x, z, c))))
    return found


def step_first(s):
    return pairs(
        lambda y, x, z, c: (y, (x + s) % SIDE, z, c) if c == 0 else ((y + s) % SIDE, x, z, c)
    )


def step_second(s):
    return pairs(
        lambda y, x, z, c: ((y + s) % SIDE, x, z, c) if c == 0 else (y, (x + s) % SIDE, z, c)
    )


FIRST = {s: step_first(s) for s in (1, 2, 3)}
SECOND = {s: step_second(s) for s in (1, 2, 3)}
TWIN = pairs(lambda y, x, z, c: (x, y, z, 1 - c))


def move(value, links):
    return lax.ppermute(value, AXES, links)


AHEAD = {s: pairs(lambda y, x, z, c, s=s: (y, x, (z + s) % 4, c)) for s in (1, 2, 3)}
OTHER = pairs(lambda y, x, z, c: (y, x, z, 1 - c))


def together(*values):
    return lax.optimization_barrier(values)


def parts_of(value, n):
    found = []
    for _ in range(n):
        found.append(value.astype(BF))
        value = value - found[-1].astype(F32)
    return found


def params(mib=50):
    return pltpu.CompilerParams(vmem_limit_bytes=mib << 20)


def project(core, x_all, u_all, weights, heads, far):
    total, depth = x_all.shape
    tile = weights[0].shape[1] // 4
    n = total // 4
    h = n // 2
    spread = heads[1].shape[0]
    starts = (0, h) if far else (n + h, 3 * n, n, 3 * n + h, 0, h)
    types = (BF, BF) if far else (BF, BF, F32, F32, F32, F32)

    def kernel(core_ref, x_ref, u_ref, gate_ref, up_ref, down_ref, head_ref, spread_ref, *outs):
        step = pl.program_id(0)

        def run(rows_ref, of):
            for start, out in zip(starts, outs):
                value = of(rows_ref[start : start + h])
                out[:, : value.shape[1]] = value.astype(out.dtype)

        def heads_of(rows):
            return product(rows, head_ref[...]) + jnp.concatenate(
                [spread_ref[...]] * (h // spread), 0
            )

        pl.when(step < 2)(lambda: run(x_ref, lambda rows: product(rows, gate_ref[...])))
        pl.when((step >= 2) & (step < 4))(
            lambda: run(x_ref, lambda rows: product(rows, up_ref[...]))
        )
        pl.when((step >= 4) & (step < 6))(
            lambda: run(u_ref, lambda rows: right_transpose(rows, down_ref[...]))
        )
        pl.when(step == 6)(lambda: run(x_ref, heads_of))

    whole = lambda v: pl.BlockSpec(v.shape, lambda i, s: (0, 0))
    tokens = pl.BlockSpec((n, depth), lambda i, s: (2, 0)) if far else whole(x_all)
    return pl.pallas_call(
        kernel,
        out_shape=[jax.ShapeDtypeStruct((h, 6 * tile + 128), t) for t in types],
        grid_spec=pltpu.PrefetchScalarGridSpec(
            num_scalar_prefetch=1,
            grid=(7,),
            in_specs=[
                tokens,
                tokens,
                pl.BlockSpec((depth, tile), lambda i, s: (0, 2 * s[0] + jnp.minimum(i, 1))),
                pl.BlockSpec((depth, tile), lambda i, s: (0, 2 * s[0] + jnp.clip(i - 2, 0, 1))),
                pl.BlockSpec((tile, depth), lambda i, s: (2 * s[0] + jnp.clip(i - 4, 0, 1), 0)),
                whole(heads[0]),
                whole(heads[1]),
            ],
            out_specs=[pl.BlockSpec((h, tile), lambda i, s: (0, i)) for _ in types],
        ),
        compiler_params=params(),
        name="project_far" if far else "project_rest",
    )(core[None], x_all, u_all, *weights, *heads)


def joined(refs):
    return jnp.concatenate([ref[...] for ref in refs], 0)


def mixed(u_rows, slopes, head):
    slope = (
        slopes[:, 0:1].astype(F32) + slopes[:, 1:2].astype(F32) + slopes[:, 2:3].astype(F32)
    )
    return (u_rows.astype(F32) + slope * head).astype(BF)


def first_kernel(core, *refs):
    slopes, (turned_inputs, u_rows, head, gate, up, down_out, input_out, weight_out) = (
        refs[4:8],
        refs[8:],
    )
    step = pl.program_id(0)
    piece = joined(refs[:4])

    @pl.when(step == 0)
    def _():
        input_out[...] = jnp.zeros_like(input_out)

    @pl.when(step < 2)
    def _():
        down_out[...] = transpose_product(piece, mixed(u_rows[...], joined(slopes), head[...]))

    def run(weight):
        input_out[...] += right_transpose(piece, weight[...])
        weight_out[...] = product(turned_inputs[...], piece)

    pl.when((step >= 2) & (step < 4))(lambda: run(gate))
    pl.when(step >= 4)(lambda: run(up))


def first_products(core, pieces, gate_weight, up_weight, turned_inputs, u_rows, head):
    depth, count = turned_inputs.shape
    tile = gate_weight.shape[1] // 4
    h = count // 4
    whole = lambda v: pl.BlockSpec(v.shape, lambda i, s: (0, 0))
    return pl.pallas_call(
        first_kernel,
        out_shape=[
            jax.ShapeDtypeStruct((2 * tile, depth), F32),
            jax.ShapeDtypeStruct((count, depth), F32),
            jax.ShapeDtypeStruct((depth, 4 * tile), F32),
        ],
        grid_spec=pltpu.PrefetchScalarGridSpec(
            num_scalar_prefetch=1,
            grid=(6,),
            in_specs=[pl.BlockSpec((h, tile), lambda i, s: (0, i))] * 4
            + [pl.BlockSpec((h, 128), lambda i, s: (0, 6 * tile // 128))] * 4
            + [
                whole(turned_inputs),
                whole(u_rows),
                whole(head),
                pl.BlockSpec((depth, tile), lambda i, s: (0, 2 * s[0] + jnp.clip(i - 2, 0, 1))),
                pl.BlockSpec((depth, tile), lambda i, s: (0, 2 * s[0] + jnp.clip(i - 4, 0, 1))),
            ],
            out_specs=[
                pl.BlockSpec((tile, depth), lambda i, s: (jnp.minimum(i, 1), 0)),
                pl.BlockSpec((count, depth), lambda i, s: (0, 0)),
                pl.BlockSpec((depth, tile), lambda i, s: (0, jnp.maximum(i - 2, 0))),
            ],
        ),
        compiler_params=params(),
        name="first_products",
    )(core[None], *pieces, *pieces, turned_inputs, u_rows, head, gate_weight, up_weight)


def down_kernel(*refs):
    u_rows, head, near, out = refs[8:]
    out[...] = near[...] + transpose_product(
        joined(refs[:4]), mixed(u_rows[...], joined(refs[4:8]), head[...])
    )


def down_product(pieces, u_rows, head, near):
    width, depth = near.shape
    tile = width // 2
    h = pieces[0].shape[0]
    return pl.pallas_call(
        down_kernel,
        out_shape=jax.ShapeDtypeStruct((width, depth), F32),
        grid=(2,),
        in_specs=[pl.BlockSpec((h, tile), lambda i: (0, i))] * 4
        + [pl.BlockSpec((h, 128), lambda i: (0, 6 * tile // 128))] * 4
        + [
            pl.BlockSpec(u_rows.shape, lambda i: (0, 0)),
            pl.BlockSpec((1, depth), lambda i: (0, 0)),
            pl.BlockSpec((tile, depth), lambda i: (i, 0)),
        ],
        out_specs=pl.BlockSpec((tile, depth), lambda i: (i, 0)),
        compiler_params=params(),
        name="down_product",
    )(*pieces, *pieces, u_rows, head, near)


def input_kernel(core, source, *refs):
    gate, up, near, own_out, other_out, total = refs[4:]
    step = pl.program_id(0)
    piece = joined(refs[:4])
    n = near.shape[0]

    @pl.when(step == 0)
    def _():
        total[:n] = near[...]
        total[n:] = jnp.zeros((n, total.shape[1]), F32)

    def run(weight):
        total[n:] += right_transpose(piece, weight[...])

    pl.when(step < 2)(lambda: run(gate))
    pl.when(step >= 2)(lambda: run(up))

    @pl.when(step == pl.num_programs(0) - 1)
    def _():
        m = n // 8
        for i in range(8):
            own_out[i * m : (i + 1) * m] = total[pl.ds(pl.multiple_of(source[i] * m, m), m)]
            other_out[i * m : (i + 1) * m] = total[
                pl.ds(pl.multiple_of(source[8 + i] * m, m), m)
            ].astype(BF)


def input_product(core, source, pieces, gate_weight, up_weight, near):
    depth = gate_weight.shape[0]
    tile = gate_weight.shape[1] // 4
    h = pieces[0].shape[0]
    return pl.pallas_call(
        input_kernel,
        out_shape=[
            jax.ShapeDtypeStruct((4 * h, depth), F32),
            jax.ShapeDtypeStruct((4 * h, depth), BF),
        ],
        grid_spec=pltpu.PrefetchScalarGridSpec(
            num_scalar_prefetch=2,
            grid=(4,),
            in_specs=[pl.BlockSpec((h, tile), lambda i, s, t: (0, i + 2))] * 4
            + [
                pl.BlockSpec((depth, tile), lambda i, s, t: (0, 2 * s[0] + jnp.minimum(i, 1))),
                pl.BlockSpec(
                    (depth, tile), lambda i, s, t: (0, 2 * s[0] + jnp.maximum(i - 2, 0))
                ),
                pl.BlockSpec((4 * h, depth), lambda i, s, t: (0, 0)),
            ],
            out_specs=[pl.BlockSpec((4 * h, depth), lambda i, s, t: (0, 0))] * 2,
            scratch_shapes=[pltpu.VMEM((8 * h, depth), F32)],
        ),
        compiler_params=params(),
        name="input_product",
    )(core[None], source, *pieces, gate_weight, up_weight, near)


def weight_kernel(core, *refs):
    turned_inputs, near, keep_out, send_out = refs[4:]
    piece = joined(refs[:4])
    n = keep_out.shape[0]

    def product_of(first):
        rows = pl.ds(pl.multiple_of(first, n), n)
        return near[rows, :] + product(turned_inputs[rows, :], piece)

    keep_out[...] = product_of(core[0] * n)
    send_out[...] = product_of((1 - core[0]) * n).astype(BF)


def weight_product(core, pieces, turned_inputs, near):
    depth, width = near.shape
    tile = width // 4
    h = pieces[0].shape[0]
    return pl.pallas_call(
        weight_kernel,
        out_shape=[
            jax.ShapeDtypeStruct((depth // 2, width), F32),
            jax.ShapeDtypeStruct((depth // 2, width), BF),
        ],
        grid_spec=pltpu.PrefetchScalarGridSpec(
            num_scalar_prefetch=1,
            grid=(4,),
            in_specs=[pl.BlockSpec((h, tile), lambda i, s: (0, i + 2))] * 4
            + [
                pl.BlockSpec(turned_inputs.shape, lambda i, s: (0, 0)),
                pl.BlockSpec((depth, tile), lambda i, s: (0, i)),
            ],
            out_specs=[pl.BlockSpec((depth // 2, tile), lambda i, s: (0, i))] * 2,
        ),
        compiler_params=params(),
        name="weight_product",
    )(core[None], *pieces, turned_inputs, near)


def add_halves(direct, added, arrived, top_added):
    h, width = direct.shape
    if direct.dtype == F32:
        added = added + arrived.astype(F32)
        both = (added, direct) if top_added else (direct, added)
        return jnp.concatenate(both, 0).astype(BF)
    tile = (width - 128) // 6

    def kernel(direct_ref, added_ref, arrived_ref, out_ref):
        at = 0 if top_added else h
        out_ref[at : at + h] = (added_ref[...] + arrived_ref[...].astype(F32)).astype(BF)
        out_ref[h - at : 2 * h - at] = direct_ref[...].astype(BF)

    return pl.pallas_call(
        kernel,
        out_shape=jax.ShapeDtypeStruct((2 * h, width), BF),
        grid=(7,),
        in_specs=[pl.BlockSpec((h, tile), lambda i: (0, i))] * 3,
        out_specs=pl.BlockSpec((2 * h, tile), lambda i: (0, i)),
        compiler_params=params(16),
        name="add_halves",
    )(direct, added, arrived)


def ring_reduce(far, direct, added, own, ring):
    up, down = move(far[0], ring[1]), move(far[1], ring[3])
    up, down, *held = together(up, down, *direct, *added, *own)
    direct, added, own = held[:2], held[2:4], held[4:]
    below = move(add_halves(direct[0], added[0], up, True), ring[1])
    above = move(add_halves(direct[1], added[1], down, False), ring[3])
    h = own[0].shape[0]
    top = own[0] + below[:h].astype(F32) + above[:h].astype(F32)
    bottom = own[1] + below[h:].astype(F32) + above[h:].astype(F32)
    return top, bottom


def halves(value):
    h = value.shape[0] // 2
    return value[:h], value[h:]


def ring_start(top, bottom, ring):
    ahead_top, behind_bottom = move(top, ring[3]), move(bottom, ring[1])
    ahead_bottom, behind_top = move(bottom, ring[3]), move(top, ring[1])
    return ahead_top, ahead_bottom, behind_top, behind_bottom


def ring_pass(arrived, ring):
    return move(arrived[0], ring[3]), move(arrived[3], ring[1])


def per_device(
    inputs, gate_weight, up_weight, down_weight, reward_head, upstream, labels, label_mask
):
    tokens, depth = inputs.shape
    half = gate_weight.shape[1] // 2
    core = lax.axis_index("dp")
    row = lax.axis_index("row")
    z = lax.axis_index("col")
    y, x = row // SIDE, row % SIDE
    a = jnp.where(core == 0, x, y)
    b = jnp.where(core == 0, y, x)
    turn = (a + 4 - z) % 4
    mine = tokens // 2
    total = tokens * 8
    head_value = reward_head.astype(F32)
    weights = (gate_weight, up_weight)
    all_weights = (gate_weight, up_weight, down_weight)

    def around_z(value):
        return [value] + [move(value, AHEAD[4 - s]) for s in (1, 2, 3)]

    def both_cores(own, axis):
        other = move(own, OTHER)
        shape = own.shape[:axis] + (4, 1, tokens) + own.shape[axis + 1 :]
        own, other = own.reshape(shape), other.reshape(shape)
        return jnp.where(
            core == 0,
            jnp.concatenate([own, other], axis + 1),
            jnp.concatenate([other, own], axis + 1),
        )

    def ordered(whole):
        whole = lax.dynamic_slice_in_dim(jnp.concatenate([whole, whole], 0), turn, 4, 0)
        whole = lax.dynamic_slice_in_dim(jnp.concatenate([whole, whole], 1), b, 4, 1)
        return whole.reshape(total, depth)

    down_half = lax.dynamic_slice_in_dim(down_weight, core * half, half, 0)
    head_hidden = jnp.dot(down_half.astype(F32), head_value, precision=lax.Precision.HIGHEST)

    x_own, u_own = around_z(inputs), around_z(upstream)
    *x_own, head_hidden = together(*x_own, head_hidden)
    x_whole = both_cores(jnp.concatenate(x_own, 0), 0).reshape(4, 4, mine, depth)
    x_all = ordered(x_whole)
    u_all = ordered(both_cores(jnp.concatenate(u_own, 0), 0).reshape(4, 4, mine, depth))
    per_token = half // mine
    heads = (
        jnp.pad(reward_head[:, None], ((0, 0), (0, 127))),
        jnp.pad(head_hidden.reshape(mine, per_token), ((0, 0), (1, 127 - per_token))),
    )

    far = project(core, x_all, u_all, all_weights, heads, True)
    rest = project(core, x_all, u_all, all_weights, heads, False)
    top, bottom = ring_reduce(far, rest[:2], rest[2:4], rest[4:], FIRST)
    tags = both_cores(jnp.concatenate(around_z(jnp.stack([labels, label_mask])), 1), 1)
    late, later = tokens * 3, tokens * 7
    early_u = jnp.concatenate([u_all[later:], u_all[:late]], 0)
    early_x = jnp.concatenate([x_all[later:], x_all[:late]], 0).T
    late_u, late_x = u_all[late:later], x_all[late:later].T

    first, second = halves(top)
    third, fourth = halves(bottom)
    second, fourth = halves(second), halves(fourth)
    top, bottom = ring_reduce(
        halves(third.astype(BF)),
        (second[1], fourth[0]),
        (second[0], fourth[1]),
        halves(first),
        SECOND,
    )
    sums = jnp.concatenate([top, bottom], 0)

    gate, upper, grad_upstream = (sums[:, i * half : (i + 1) * half] for i in range(3))
    extra = sums[:, 3 * half :]
    own_inputs, head_hidden = extra[:, 0], extra[:, 1 : 1 + per_token].reshape(half)
    own_tags = lax.dynamic_slice_in_dim(
        tags.reshape(2, total), (turn * 4 + b) * mine, mine, 1
    ).astype(F32)
    sigmoid_gate = jax.nn.sigmoid(gate)
    hidden = (gate * sigmoid_gate * upper).astype(BF)

    part = jnp.sum(hidden.astype(F32) * head_hidden[None, :], axis=1)
    part = part + move(part, AHEAD[1]) + move(part, AHEAD[2]) + move(part, AHEAD[3])
    score = own_inputs + part + move(part, TWIN)
    slope = reward_weight * own_tags[1] * (jax.nn.sigmoid(score) - own_tags[0])
    grad_hidden = grad_upstream + slope[:, None] * head_hidden[None, :]
    grad_gate = (grad_hidden * upper * sigmoid_gate * (1.0 + gate * (1.0 - sigmoid_gate))).astype(
        BF
    )
    grad_upper = (grad_hidden * gate * sigmoid_gate).astype(BF)
    slopes = jnp.pad(jnp.stack(parts_of(slope, 3), axis=1), ((0, 0), (0, 125)))
    block = jnp.concatenate([hidden, grad_gate, grad_upper, slopes], axis=1)

    near = ring_start(*halves(block), SECOND)
    far = ring_pass(near, SECOND)
    top = jnp.concatenate([block, *near[:2]], 0)
    bottom = jnp.concatenate([*far, *near[2:]], 0)
    near = ring_start(top, bottom, FIRST)
    far = ring_pass(near, FIRST)
    head_row = head_value[None, :]
    early = (near[3], top, bottom, near[0])
    near_down, near_input, near_weight = first_products(
        core, early, *weights, early_x, early_u, head_row
    )
    *last, near_down, near_input, near_weight = together(
        near[1], *far, near[2], near_down, near_input, near_weight
    )

    spot = jnp.arange(16, dtype=jnp.int32)
    whose = jnp.where(spot < 8, core, 1 - core)
    ahead_of = (z + (spot // 2) % 4 + 4 - a) % 4
    source = ahead_of * 4 + (whose * 2 + spot % 2 + 4 - b) % 4
    source_early = (source + 2) % 16
    own_part, other_part = input_product(core, source_early, last, *weights, near_input)
    near_weight, own_part = together(near_weight, own_part)
    other_arrived = move(other_part, OTHER)
    keep, send = weight_product(core, last, late_x, near_weight)
    other = move(send, OTHER)
    near_down, other_arrived = together(near_down, other_arrived)
    blocks = jnp.split(own_part + other_arrived.astype(F32), 4, 0)
    input_sum = blocks[0]
    blocks = [t.astype(BF) for t in blocks[1:]]
    *blocks, near_down = together(*blocks, near_down)
    arrived = [move(blocks[s - 1], AHEAD[s]) for s in (1, 2, 3)]
    down_grad = down_product(last, late_u, head_row, near_down)

    slope_parts = jnp.concatenate(
        [
            p[:, 6 * (half // 2) :]
            for p in (top, bottom, near[0], *last, near[3])
        ],
        0,
    )
    slope_all = slope_parts[:, :3].astype(F32).sum(1)
    own_slope = jnp.concatenate(
        [lax.dynamic_slice_in_dim(slope_all, source[i] * mine, mine, 0) for i in range(2)]
    )

    def both_halves(start):
        k, o = keep[:, start : start + half], other[:, start : start + half].astype(F32)
        return jnp.concatenate([jnp.where(core == 0, k, o), jnp.where(core == 0, o, k)], axis=1)

    gate_grad, up_grad = both_halves(0), both_halves(half)
    *arrived, gate_grad, up_grad, down_grad = together(*arrived, gate_grad, up_grad, down_grad)
    for t in arrived:
        input_sum = input_sum + t.astype(F32)
    input_grad = upstream.astype(F32) + own_slope[:, None] * head_value[None, :] + input_sum
    return (gate_grad, up_grad, down_grad, input_grad)


def solution(mesh):
    in_specs = (
        P(("col", "dp"), "row"),
        P("row", "col"),
        P("row", "col"),
        P("col", "row"),
        P("row"),
        P(("col", "dp"), "row"),
        P(("col", "dp")),
        P(("col", "dp")),
    )
    out_specs = (
        P(("row", "dp"), "col"),
        P(("row", "dp"), "col"),
        P(("col", "dp"), "row"),
        P(("col", "dp"), "row"),
    )
    return jax.shard_map(
        per_device, mesh=mesh, in_specs=in_specs, out_specs=out_specs, check_vma=False
    )
```

time: 314 us -> 248 us (0.79)
  waiting for transfers between devices: 205 us -> 75.6 us
  starting transfers between devices: 1.19 us -> 69.6 us
  Pallas kernels: 0 us -> 56.8 us
  matrix products: 42 us -> 2.1 us
  blocking collectives: 13.1 us -> 0 us
  between operations: 14 us -> 2.52 us
  local copies, waits for them, and re-layouts: 21.9 us -> 25.3 us
    all_gather x2 -> x0, waiting for transfers between devices: 109 us -> none  [the longest x1 81.6 us: per_device(): lax.all_gather(jnp.concatenate([hidden, grad_gate, grad_upper, slopes], a...]
    reduce_scatter x2 -> x0, waiting for transfers between devices: 95.9 us -> none  [the longest x1 89.5 us: per_device(): lax.psum_scatter(partial, 'row', scatter_dimension=0, tiled=True)]
    ppermute x2 -> x41, waiting for transfers between devices: 0.01 us -> 75.6 us  [move(): return lax.ppermute(value, AXES, links)]
    ppermute x2 -> x41, starting transfers between devices: 1.03 us -> 69.6 us  [move(): return lax.ppermute(value, AXES, links)]
    pallas_call x0 -> x8, Pallas kernels: none -> 56.8 us  [the longest x2 20.4 us: project(): pl.pallas_call(kernel, out_shape=[jax.ShapeDtypeStruct((h, 6 * tile + 128...]
    dot_general x9 -> x0, matrix products: 39.9 us -> none  [the longest x3 16 us: right_transpose(): lax.dot_general(left, right, (((1,), (1,)), ((), ())), preferred_element_...]
    concatenate x1 -> x4, local copies, waits for them, and re-layouts: 18.4 us -> 1.54 us  [the longest x1 0.77 us: per_device(): jnp.concatenate([p[:, 6 * (half // 2):] for p in (top, bottom, near[0], *...]
    unnamed x16 -> x60, local copies, waits for them, and re-layouts: 0.86 us -> 15.9 us
  transfers between devices with their start and end apart: 6 -> 41, of which waited for: 4 -> 21; matrix products, arithmetic and copies ran while one was open for 8% -> 13% of each run, Pallas kernels for 0% -> 13%
where the time goes in v2:
time: 248 us; the launch traced here: 247 us
  waiting for transfers between devices  75.6 us (30%)
  starting transfers between devices  69.6 us (28%)
  Pallas kernels  56.8 us (23%)
  local copies, waits for them, and re-layouts  25.3 us (10%)
  other arithmetic  14.6 us (6%)
  between operations  2.52 us (1%)
    ppermute x41, waiting for transfers between devices, move(): return lax.ppermute(value, AXES, links)  75.6 us
    ppermute x41, starting transfers between devices, move(): return lax.ppermute(value, AXES, links)  69.6 us
    pallas_call x2, Pallas kernels, project(): pl.pallas_call(kernel, out_shape=[jax.ShapeDtypeStruct((h, 6 * tile + 128...  20.4 us
    unnamed x60, local copies, waits for them, and re-layouts  15.9 us
    pallas_call x1, Pallas kernels, first_products(): pl.pallas_call(first_kernel, out_shape=[jax.ShapeDtypeStruct((2 * tile, d...  13.2 us
    pallas_call x1, Pallas kernels, weight_product(): pl.pallas_call(weight_kernel, out_shape=[jax.ShapeDtypeStruct((depth // 2...  7.3 us
    pallas_call x1, Pallas kernels, input_product(): pl.pallas_call(input_kernel, out_shape=[jax.ShapeDtypeStruct((4 * h, dept...  6.89 us
    pallas_call x1, Pallas kernels, down_product(): pl.pallas_call(down_kernel, out_shape=jax.ShapeDtypeStruct((width, depth)...  4.98 us
  transfers between devices with their start and end apart: 41, of which 21 were waited for; matrix products, arithmetic and copies ran while one was open for 13% of the time, Pallas kernels for 13%

profile of v2, /device:TPU:1, one launch (start us, length us, event | category | flops | bytes accessed | tf_op | source)
XLA Modules:
  0.0 246.6 jit_solution(16180146342705318279)
XLA Ops:
  0.7 4.7 %collective-permute-start = (bf16[128,512]{1,0:T(8,128)(2,1)}, bf16[128,512]{1,0:T(8,128)(2,1)S(1)}, u32[]{:S(2)}, u32[]{:S(2)}) collective-permute-start(bf16[128,512]{1,0:T(8,128)(2,1)} %param.8), channel_id=1, source_target_pairs={{0,6},{1,7},{2,0},{3,1},{4,2},{5,3},{6,4},{7,5},{8,14},{9,15},{10,... | collective-permute-start | bytes 393224 | tf_op jit(solution)/shard_map/ppermute | solution.py:63
  12.7 2.6 %collective-permute-done.2 = bf16[128,512]{1,0:T(8,128)(2,1)S(1)} collective-permute-done((bf16[128,512]{1,0:T(8,128)(2,1)}, bf16[128,512]{1,0:T(8,128)(2,1)S(1)}, u32[]{:S(2)}, u32[]{:S(2)}) %collective-permute-start.2) | collective-permute-done | bytes 131104 | tf_op jit(solution)/shard_map/ppermute | solution.py:63
  16.9 2.5 %collective-permute-done.6 = bf16[128,512]{1,0:T(8,128)(2,1)S(1)} collective-permute-done((bf16[128,512]{1,0:T(8,128)(2,1)S(1)}, bf16[128,512]{1,0:T(8,128)(2,1)S(1)}, u32[]{:S(2)}, u32[]{:S(2)}) %collective-permute-start.6) | collective-permute-done | bytes 131104 | tf_op jit(solution)/shard_map/ppermute | solution.py:63
  19.4 2.7 %collective-permute-start.7 = (bf16[512,512]{1,0:T(8,128)(2,1)S(1)}, bf16[512,512]{1,0:T(8,128)(2,1)S(1)}, u32[]{:S(2)}, u32[]{:S(2)}) collective-permute-start(bf16[512,512]{1,0:T(8,128)(2,1)S(1)} %constant_dynamic-update-slice_fusion.4), channel_id=1, source_target_pairs={{0,1},{1,0},{2,3},{3,2},{4,5},{5,4},{6,7},{7,6},{8,9},{9,8},{10,11... | collective-permute-start | bytes 1572872 | tf_op jit(solution)/shard_map/ppermute | solution.py:63
  25.5 8.0 %project_far.1 = (bf16[128,5504]{1,0:T(8,128)(2,1)S(1)}, bf16[128,5504]{1,0:T(8,128)(2,1)}) custom-call(s32[1]{0:T(128)} %bitcast.core_ref.core, bf16[1024,512]{1,0:T(8,128)(2,1)S(1)} %bitcast.35, bf16[1024,512]{1,0:T(8,128)(2,1)S(1)} %bitcast.30, bf16[512,3584]{1,0:T(8,128)(2,1)} %refs_4_.1, bf16[512,3584]{1,0:T(8,128)(2,1)} %refs_5_.1, ...), custom_call_target="tpu_custom_call" | custom-call | tf_op jit(solution)/shard_map/project_far/pallas_call | solution.py:119
  36.3 12.4 %project_rest.1 = (bf16[128,5504]{1,0:T(8,128)(2,1)S(1)}, bf16[128,5504]{1,0:T(8,128)(2,1)}, f32[128,5504]{1,0:T(8,128)}, f32[128,5504]{1,0:T(8,128)}, f32[128,5504]{1,0:T(8,128)}, /*index=5*/f32[128,5504]{1,0:T(8,128)}) custom-call(s32[1]{0:T(128)} %bitcast.core_ref.core, bf16[1024,512]{1,0:T(8,128)(2,1)S(1)} %bitcast.36, bf16[1024,512]{1,0:T(8,128)(2,1)S(1)} %bitcast.31, ...), custom_call_target="tpu_custom_call" | custom-call | tf_op jit(solution)/shard_map/project_rest/pallas_call | solution.py:119
  48.7 3.9 %collective-permute-done.8.arrived_ref = bf16[128,5504]{1,0:T(8,128)(2,1)S(1)} collective-permute-done((bf16[128,5504]{1,0:T(8,128)(2,1)S(1)}, bf16[128,5504]{1,0:T(8,128)(2,1)S(1)}, u32[]{:S(2)}, u32[]{:S(2)}) %collective-permute-start.8) | collective-permute-done | bytes 1409056 | tf_op jit(solution)/shard_map/ppermute | solution.py:63
  61.7 29.3 %collective-permute-done.10 = bf16[256,5504]{1,0:T(8,128)(2,1)S(1)} collective-permute-done((bf16[256,5504]{1,0:T(8,128)(2,1)S(1)}, bf16[256,5504]{1,0:T(8,128)(2,1)S(1)}, u32[]{:S(2)}, u32[]{:S(2)}) %collective-permute-start.10) | collective-permute-done | bytes 2818080 | tf_op jit(solution)/shard_map/ppermute | solution.py:63
  97.1 4.7 %collective-permute-done.12 = bf16[32,5504]{1,0:T(8,128)(2,1)S(1)} collective-permute-done((bf16[32,5504]{1,0:T(8,128)(2,1)S(1)}, bf16[32,5504]{1,0:T(8,128)(2,1)S(1)}, u32[]{:S(2)}, u32[]{:S(2)}) %collective-permute-start.12) | collective-permute-done | bytes 352288 | tf_op jit(solution)/shard_map/ppermute | solution.py:63
  107.5 3.2 %collective-permute-done.17 = s32[2,128]{1,0:T(2,128)S(1)} collective-permute-done((s32[2,128]{1,0:T(2,128)S(1)}, s32[2,128]{1,0:T(2,128)S(1)}, u32[]{:S(2)}, u32[]{:S(2)}) %collective-permute-start.17) | collective-permute-done | bytes 1056 | tf_op jit(solution)/shard_map/ppermute | solution.py:63
  110.7 5.7 %collective-permute-start.19 = (s32[2,512]{1,0:T(2,128)S(1)}, s32[2,512]{1,0:T(2,128)S(1)}, u32[]{:S(2)}, u32[]{:S(2)}) collective-permute-start(s32[2,512]{1,0:T(2,128)S(1)} %pad_add_fusion), channel_id=1, source_target_pairs={{0,1},{1,0},{2,3},{3,2},{4,5},{5,4},{6,7},{7,6},{8,9},{9,8},{10,11... | collective-permute-start | bytes 12296 | tf_op jit(solution)/shard_map/ppermute | solution.py:63
  123.6 3.9 %collective-permute-start.23 = (f32[64]{0:T(128)S(1)}, f32[64]{0:T(128)S(1)}, u32[]{:S(2)}, u32[]{:S(2)}) collective-permute-start(f32[64]{0:T(128)S(1)} %add_add_fusion), channel_id=1, source_target_pairs={{0,1},{1,0},{2,3},{3,2},{4,5},{5,4},{6,7},{7,6},{8,33},{9,32},{10,... | collective-permute-start | bytes 776 | tf_op jit(solution)/shard_map/ppermute | solution.py:63
  128.9 5.3 %collective-permute-start.24 = (bf16[32,5504]{1,0:T(8,128)(2,1)S(1)}, bf16[32,5504]{1,0:T(8,128)(2,1)S(1)}, u32[]{:S(2)}, u32[]{:S(2)}) collective-permute-start(bf16[32,5504]{1,0:T(8,128)(2,1)S(1)} %get-tuple-element.143), channel_id=1, source_target_pairs={{0,96},{1,25},{2,98},{3,27},{4,100},{5,29},{6,102},{7,31},{8,104},... | collective-permute-start | bytes 1056776 | tf_op jit(solution)/shard_map/ppermute | solution.py:63
  135.7 2.8 %collective-permute-done.24 = bf16[32,5504]{1,0:T(8,128)(2,1)S(1)} collective-permute-done((bf16[32,5504]{1,0:T(8,128)(2,1)S(1)}, bf16[32,5504]{1,0:T(8,128)(2,1)S(1)}, u32[]{:S(2)}, u32[]{:S(2)}) %collective-permute-start.24) | collective-permute-done | bytes 352288 | tf_op jit(solution)/shard_map/ppermute | solution.py:63
  138.5 3.1 %collective-permute-start.25 = (bf16[32,5504]{1,0:T(8,128)(2,1)S(1)}, bf16[32,5504]{1,0:T(8,128)(2,1)S(1)}, u32[]{:S(2)}, u32[]{:S(2)}) collective-permute-start(bf16[32,5504]{1,0:T(8,128)(2,1)S(1)} %collective-permute-done.24), channel_id=1, source_target_pairs={{0,96},{1,25},{2,98},{3,27},{4,100},{5,29},{6,102},{7,31},{8,104},... | collective-permute-start | bytes 1056776 | tf_op jit(solution)/shard_map/ppermute | solution.py:63
  147.8 5.3 %collective-permute-done.27 = bf16[32,5504]{1,0:T(8,128)(2,1)S(1)} collective-permute-done((bf16[32,5504]{1,0:T(8,128)(2,1)S(1)}, bf16[32,5504]{1,0:T(8,128)(2,1)S(1)}, u32[]{:S(2)}, u32[]{:S(2)}) %collective-permute-start.27) | collective-permute-done | bytes 352288 | tf_op jit(solution)/shard_map/ppermute | solution.py:63
  158.2 7.3 %collective-permute-done.31.refs_3_.refs_7_ = bf16[128,5504]{1,0:T(8,128)(2,1)} collective-permute-done((bf16[128,5504]{1,0:T(8,128)(2,1)}, bf16[128,5504]{1,0:T(8,128)(2,1)}, u32[]{:S(2)}, u32[]{:S(2)}) %collective-permute-start.31) | collective-permute-done | bytes 1409056 | tf_op jit(solution)/shard_map/ppermute | solution.py:63
  165.5 3.4 %collective-permute-start.32 = (bf16[128,5504]{1,0:T(8,128)(2,1)}, bf16[128,5504]{1,0:T(8,128)(2,1)S(1)}, u32[]{:S(2)}, u32[]{:S(2)}) collective-permute-start(bf16[128,5504]{1,0:T(8,128)(2,1)} %collective-permute-done.31.refs_3_.refs_7_), channel_id=1, source_target_pairs={{0,24},{1,97},{2,26},{3,99},{4,28},{5,101},{6,30},{7,103},{8,0},{9... | collective-permute-start | bytes 4227080 | tf_op jit(solution)/shard_map/ppermute | solution.py:63
  168.9 5.9 %collective-permute-done.33.refs_0_.refs_4_ = bf16[128,5504]{1,0:T(8,128)(2,1)} collective-permute-done((bf16[128,5504]{1,0:T(8,128)(2,1)}, bf16[128,5504]{1,0:T(8,128)(2,1)}, u32[]{:S(2)}, u32[]{:S(2)}) %collective-permute-start.33) | collective-permute-done | bytes 1409056 | tf_op jit(solution)/shard_map/ppermute | solution.py:63
  192.1 13.2 %first_products.1 = (f32[1792,512]{1,0:T(8,128)}, f32[512,512]{1,0:T(8,128)S(1)}, f32[512,3584]{1,0:T(8,128)}) custom-call(s32[1]{0:T(128)} %bitcast.core_ref.core, bf16[128,5504]{1,0:T(8,128)(2,1)} %collective-permute-done.33.refs_0_.refs_4_, bf16[128,5504]{1,0:T(8,128)(2,1)} %pad_maximum_fusion.2.refs_1_.refs_5_, ...), custom_call_target="tpu_custom_call" | custom-call | tf_op jit(solution)/shard_map/first_products/pallas_call | solution.py:181
  206.5 6.9 %input_product.1 = (f32[512,512]{1,0:T(8,128)S(1)}, bf16[512,512]{1,0:T(8,128)(2,1)S(1)}) custom-call(s32[1]{0:T(128)} %bitcast.core_ref.core, s32[16]{0:T(128)S(1)} %get-tuple-element.120.source, bf16[128,5504]{1,0:T(8,128)(2,1)S(1)} %collective-permute-done.29.refs_0_.refs_4_, bf16[128,5504]{1,0:T(8,128)(2,1)} %copy-done, ...), custom_call_target="tpu_custom_call" | custom-call | tf_op jit(solution)/shard_map/input_product/pallas_call | solution.py:270
  214.7 7.3 %weight_product.1 = (f32[256,3584]{1,0:T(8,128)}, bf16[256,3584]{1,0:T(8,128)(2,1)}) custom-call(s32[1]{0:T(128)} %bitcast.core_ref.core, bf16[128,5504]{1,0:T(8,128)(2,1)S(1)} %collective-permute-done.29.refs_0_.refs_4_, bf16[128,5504]{1,0:T(8,128)(2,1)S(1)} %copy-done.1, bf16[128,5504]{1,0:T(8,128)(2,1)} %collective-permute-done.34.refs_2_.refs_6_, ...), custom_call_target="tpu_custom_call" | custom-call | tf_op jit(solution)/shard_map/weight_product/pallas_call | solution.py:312
  222.0 5.9 %collective-permute-start.40 = (bf16[256,3584]{1,0:T(8,128)(2,1)}, bf16[256,3584]{1,0:T(8,128)(2,1)S(1)}, u32[]{:S(2)}, u32[]{:S(2)}) collective-permute-start(bf16[256,3584]{1,0:T(8,128)(2,1)} %get-tuple-element.110), channel_id=1, source_target_pairs={{0,1},{1,0},{2,3},{3,2},{4,5},{5,4},{6,7},{7,6},{8,9},{9,8},{10,11... | collective-permute-start | bytes 5505032 | tf_op jit(solution)/shard_map/ppermute | solution.py:63
  235.7 5.0 %down_product.1 = f32[1792,512]{1,0:T(8,128)} custom-call(bf16[128,5504]{1,0:T(8,128)(2,1)S(1)} %collective-permute-done.29.refs_0_.refs_4_, bf16[128,5504]{1,0:T(8,128)(2,1)S(1)} %copy-done.1, bf16[128,5504]{1,0:T(8,128)(2,1)} %collective-permute-done.34.refs_2_.refs_6_, bf16[128,5504]{1,0:T(8,128)(2,1)} %collective-permute-done.35.refs_3_.refs_7_, ...), custom_call_target="tpu_custom_call" | custom-call | tf_op jit(solution)/shard_map/down_product/pallas_call | solution.py:222
  (193 shorter events, 88.8 us)
Async XLA Ops:
  0.7 11.9 %collective-permute-start = (bf16[128,512]{1,0:T(8,128)(2,1)}, bf16[128,512]{1,0:T(8,128)(2,1)S(1)}, u32[]{:S(2)}, u32[]{:S(2)}) collective-permute-start(bf16[128,512]{1,0:T(8,128)(2,1)} %param.8), channel_id=1, source_target_pairs={{0,6},{1,7},{2,0},{3,1},{4,2},{5,3},{6,4},{7,5},{8,14},{9,15},{10,... | collective-permute-start | bytes 393224 | tf_op jit(solution)/shard_map/ppermute | solution.py:63
  5.3 10.0 %collective-permute-start.2 = (bf16[128,512]{1,0:T(8,128)(2,1)}, bf16[128,512]{1,0:T(8,128)(2,1)S(1)}, u32[]{:S(2)}, u32[]{:S(2)}) collective-permute-start(bf16[128,512]{1,0:T(8,128)(2,1)} %param.8), channel_id=1, source_target_pairs={{0,2},{1,3},{2,4},{3,5},{4,6},{5,7},{6,0},{7,1},{8,10},{9,11},{10,... | collective-permute-start | bytes 393224 | tf_op jit(solution)/shard_map/ppermute | solution.py:63
  6.0 10.8 %collective-permute-start.4 = (bf16[128,512]{1,0:T(8,128)(2,1)}, bf16[128,512]{1,0:T(8,128)(2,1)S(1)}, u32[]{:S(2)}, u32[]{:S(2)}) collective-permute-start(bf16[128,512]{1,0:T(8,128)(2,1)} %param.13), channel_id=1, source_target_pairs={{0,6},{1,7},{2,0},{3,1},{4,2},{5,3},{6,4},{7,5},{8,14},{9,15},{10,... | collective-permute-start | bytes 393224 | tf_op jit(solution)/shard_map/ppermute | solution.py:63
  8.0 8.9 %collective-permute-start.5 = (bf16[128,512]{1,0:T(8,128)(2,1)}, bf16[128,512]{1,0:T(8,128)(2,1)S(1)}, u32[]{:S(2)}, u32[]{:S(2)}) collective-permute-start(bf16[128,512]{1,0:T(8,128)(2,1)} %param.13), channel_id=1, source_target_pairs={{0,4},{1,5},{2,6},{3,7},{4,0},{5,1},{6,2},{7,3},{8,12},{9,13},{10,... | collective-permute-start | bytes 393224 | tf_op jit(solution)/shard_map/ppermute | solution.py:63
  33.6 19.1 %collective-permute-start.8 = (bf16[128,5504]{1,0:T(8,128)(2,1)S(1)}, bf16[128,5504]{1,0:T(8,128)(2,1)S(1)}, u32[]{:S(2)}, u32[]{:S(2)}) collective-permute-start(bf16[128,5504]{1,0:T(8,128)(2,1)S(1)} %get-tuple-element.66), channel_id=1, source_target_pairs={{0,8},{1,33},{2,10},{3,35},{4,12},{5,37},{6,14},{7,39},{8,16},{9,4... | collective-permute-start | bytes 4227080 | tf_op jit(solution)/shard_map/ppermute | solution.py:63
  34.9 18.0 %collective-permute-start.9 = (bf16[128,5504]{1,0:T(8,128)(2,1)}, bf16[128,5504]{1,0:T(8,128)(2,1)S(1)}, u32[]{:S(2)}, u32[]{:S(2)}) collective-permute-start(bf16[128,5504]{1,0:T(8,128)(2,1)} %get-tuple-element.67), channel_id=1, source_target_pairs={{0,24},{1,97},{2,26},{3,99},{4,28},{5,101},{6,30},{7,103},{8,0},{9... | collective-permute-start | bytes 4227080 | tf_op jit(solution)/shard_map/ppermute | solution.py:63
  56.7 34.4 %collective-permute-start.10 = (bf16[256,5504]{1,0:T(8,128)(2,1)S(1)}, bf16[256,5504]{1,0:T(8,128)(2,1)S(1)}, u32[]{:S(2)}, u32[]{:S(2)}) collective-permute-start(bf16[256,5504]{1,0:T(8,128)(2,1)S(1)} %add_halves.2), channel_id=1, source_target_pairs={{0,8},{1,33},{2,10},{3,35},{4,12},{5,37},{6,14},{7,39},{8,16},{9,4... | collective-permute-start | bytes 8454152 | tf_op jit(solution)/shard_map/ppermute | solution.py:63
  60.2 33.0 %collective-permute-start.11 = (bf16[256,5504]{1,0:T(8,128)(2,1)S(1)}, bf16[256,5504]{1,0:T(8,128)(2,1)S(1)}, u32[]{:S(2)}, u32[]{:S(2)}) collective-permute-start(bf16[256,5504]{1,0:T(8,128)(2,1)S(1)} %add_halves.3), channel_id=1, source_target_pairs={{0,24},{1,97},{2,26},{3,99},{4,28},{5,101},{6,30},{7,103},{8,0},{9... | collective-permute-start | bytes 8454152 | tf_op jit(solution)/shard_map/ppermute | solution.py:63
  102.0 15.3 %collective-permute-start.14 = (bf16[64,5504]{1,0:T(8,128)(2,1)S(1)}, bf16[64,5504]{1,0:T(8,128)(2,1)S(1)}, u32[]{:S(2)}, u32[]{:S(2)}) collective-permute-start(bf16[64,5504]{1,0:T(8,128)(2,1)S(1)} %pad_maximum_fusion.3), channel_id=1, source_target_pairs={{0,32},{1,9},{2,34},{3,11},{4,36},{5,13},{6,38},{7,15},{8,40},{9,1... | collective-permute-start | bytes 2113544 | tf_op jit(solution)/shard_map/ppermute | solution.py:63
  103.4 14.0 %collective-permute-start.15 = (bf16[64,5504]{1,0:T(8,128)(2,1)S(1)}, bf16[64,5504]{1,0:T(8,128)(2,1)}, u32[]{:S(2)}, u32[]{:S(2)}) collective-permute-start(bf16[64,5504]{1,0:T(8,128)(2,1)S(1)} %pad_maximum_fusion.4), channel_id=1, source_target_pairs={{0,96},{1,25},{2,98},{3,27},{4,100},{5,29},{6,102},{7,31},{8,104},... | collective-permute-start | bytes 2113544 | tf_op jit(solution)/shard_map/ppermute | solution.py:63
  128.9 9.6 %collective-permute-start.24 = (bf16[32,5504]{1,0:T(8,128)(2,1)S(1)}, bf16[32,5504]{1,0:T(8,128)(2,1)S(1)}, u32[]{:S(2)}, u32[]{:S(2)}) collective-permute-start(bf16[32,5504]{1,0:T(8,128)(2,1)S(1)} %get-tuple-element.143), channel_id=1, source_target_pairs={{0,96},{1,25},{2,98},{3,27},{4,100},{5,29},{6,102},{7,31},{8,104},... | collective-permute-start | bytes 1056776 | tf_op jit(solution)/shard_map/ppermute | solution.py:63
  134.7 11.1 %collective-permute-start.26 = (bf16[32,5504]{1,0:T(8,128)(2,1)S(1)}, bf16[32,5504]{1,0:T(8,128)(2,1)S(1)}, u32[]{:S(2)}, u32[]{:S(2)}) collective-permute-start(bf16[32,5504]{1,0:T(8,128)(2,1)S(1)} %get-tuple-element.142), channel_id=1, source_target_pairs={{0,32},{1,9},{2,34},{3,11},{4,36},{5,13},{6,38},{7,15},{8,40},{9,1... | collective-permute-start | bytes 1056776 | tf_op jit(solution)/shard_map/ppermute | solution.py:63
  135.7 18.2 %collective-permute-start.28 = (bf16[32,5504]{1,0:T(8,128)(2,1)S(1)}, bf16[32,5504]{1,0:T(8,128)(2,1)S(1)}, u32[]{:S(2)}, u32[]{:S(2)}) collective-permute-start(bf16[32,5504]{1,0:T(8,128)(2,1)S(1)} %get-tuple-element.143), channel_id=1, source_target_pairs={{0,32},{1,9},{2,34},{3,11},{4,36},{5,13},{6,38},{7,15},{8,40},{9,1... | collective-permute-start | bytes 1056776 | tf_op jit(solution)/shard_map/ppermute | solution.py:63
  138.5 8.5 %collective-permute-start.25 = (bf16[32,5504]{1,0:T(8,128)(2,1)S(1)}, bf16[32,5504]{1,0:T(8,128)(2,1)S(1)}, u32[]{:S(2)}, u32[]{:S(2)}) collective-permute-start(bf16[32,5504]{1,0:T(8,128)(2,1)S(1)} %collective-permute-done.24), channel_id=1, source_target_pairs={{0,96},{1,25},{2,98},{3,27},{4,100},{5,29},{6,102},{7,31},{8,104},... | collective-permute-start | bytes 1056776 | tf_op jit(solution)/shard_map/ppermute | solution.py:63
  143.5 22.0 %collective-permute-start.31 = (bf16[128,5504]{1,0:T(8,128)(2,1)}, bf16[128,5504]{1,0:T(8,128)(2,1)}, u32[]{:S(2)}, u32[]{:S(2)}) collective-permute-start(bf16[128,5504]{1,0:T(8,128)(2,1)} %pad_maximum_fusion.2.refs_1_.refs_5_), channel_id=1, source_target_pairs={{0,24},{1,97},{2,26},{3,99},{4,28},{5,101},{6,30},{7,103},{8,0},{9... | collective-permute-start | bytes 4227080 | tf_op jit(solution)/shard_map/ppermute | solution.py:63
  155.4 19.3 %collective-permute-start.33 = (bf16[128,5504]{1,0:T(8,128)(2,1)}, bf16[128,5504]{1,0:T(8,128)(2,1)}, u32[]{:S(2)}, u32[]{:S(2)}) collective-permute-start(bf16[128,5504]{1,0:T(8,128)(2,1)} %constant_dynamic-update-slice_fusion.8.refs_2_.refs_6_), channel_id=1, source_target_pairs={{0,8},{1,33},{2,10},{3,35},{4,12},{5,37},{6,14},{7,39},{8,16},{9,4... | collective-permute-start | bytes 4227080 | tf_op jit(solution)/shard_map/ppermute | solution.py:63
  155.5 49.9 %collective-permute-start.35 = (bf16[128,5504]{1,0:T(8,128)(2,1)}, bf16[128,5504]{1,0:T(8,128)(2,1)}, u32[]{:S(2)}, u32[]{:S(2)}) collective-permute-start(bf16[128,5504]{1,0:T(8,128)(2,1)} %pad_maximum_fusion.2.refs_1_.refs_5_), channel_id=1, source_target_pairs={{0,8},{1,33},{2,10},{3,35},{4,12},{5,37},{6,14},{7,39},{8,16},{9,4... | collective-permute-start | bytes 4227080 | tf_op jit(solution)/shard_map/ppermute | solution.py:63
  156.3 49.1 %collective-permute-start.29 = (bf16[128,5504]{1,0:T(8,128)(2,1)}, bf16[128,5504]{1,0:T(8,128)(2,1)S(1)}, u32[]{:S(2)}, u32[]{:S(2)}) collective-permute-start(bf16[128,5504]{1,0:T(8,128)(2,1)} %constant_dynamic-update-slice_fusion.8.refs_2_.refs_6_), channel_id=1, source_target_pairs={{0,24},{1,97},{2,26},{3,99},{4,28},{5,101},{6,30},{7,103},{8,0},{9... | collective-permute-start | bytes 4227080 | tf_op jit(solution)/shard_map/ppermute | solution.py:63
  165.5 39.9 %collective-permute-start.32 = (bf16[128,5504]{1,0:T(8,128)(2,1)}, bf16[128,5504]{1,0:T(8,128)(2,1)S(1)}, u32[]{:S(2)}, u32[]{:S(2)}) collective-permute-start(bf16[128,5504]{1,0:T(8,128)(2,1)} %collective-permute-done.31.refs_3_.refs_7_), channel_id=1, source_target_pairs={{0,24},{1,97},{2,26},{3,99},{4,28},{5,101},{6,30},{7,103},{8,0},{9... | collective-permute-start | bytes 4227080 | tf_op jit(solution)/shard_map/ppermute | solution.py:63
  174.8 30.6 %collective-permute-start.34 = (bf16[128,5504]{1,0:T(8,128)(2,1)}, bf16[128,5504]{1,0:T(8,128)(2,1)}, u32[]{:S(2)}, u32[]{:S(2)}) collective-permute-start(bf16[128,5504]{1,0:T(8,128)(2,1)} %collective-permute-done.33.refs_0_.refs_4_), channel_id=1, source_target_pairs={{0,8},{1,33},{2,10},{3,35},{4,12},{5,37},{6,14},{7,39},{8,16},{9,4... | collective-permute-start | bytes 4227080 | tf_op jit(solution)/shard_map/ppermute | solution.py:63
  222.0 18.6 %collective-permute-start.40 = (bf16[256,3584]{1,0:T(8,128)(2,1)}, bf16[256,3584]{1,0:T(8,128)(2,1)S(1)}, u32[]{:S(2)}, u32[]{:S(2)}) collective-permute-start(bf16[256,3584]{1,0:T(8,128)(2,1)} %get-tuple-element.110), channel_id=1, source_target_pairs={{0,1},{1,0},{2,3},{3,2},{4,5},{5,4},{6,7},{7,6},{8,9},{9,8},{10,11... | collective-permute-start | bytes 5505032 | tf_op jit(solution)/shard_map/ppermute | solution.py:63
  232.2 13.5 %collective-permute-start.37 = (bf16[128,512]{1,0:T(8,128)(2,1)S(1)}, bf16[128,512]{1,0:T(8,128)(2,1)S(1)}, u32[]{:S(2)}, u32[]{:S(2)}) collective-permute-start(bf16[128,512]{1,0:T(8,128)(2,1)S(1)} %get-tuple-element.105), channel_id=1, source_target_pairs={{0,2},{1,3},{2,4},{3,5},{4,6},{5,7},{6,0},{7,1},{8,10},{9,11},{10,... | collective-permute-start | bytes 393224 | tf_op jit(solution)/shard_map/ppermute | solution.py:63
  232.6 13.1 %collective-permute-start.38 = (bf16[128,512]{1,0:T(8,128)(2,1)S(1)}, bf16[128,512]{1,0:T(8,128)(2,1)S(1)}, u32[]{:S(2)}, u32[]{:S(2)}) collective-permute-start(bf16[128,512]{1,0:T(8,128)(2,1)S(1)} %get-tuple-element.106), channel_id=1, source_target_pairs={{0,4},{1,5},{2,6},{3,7},{4,0},{5,1},{6,2},{7,3},{8,12},{9,13},{10,... | collective-permute-start | bytes 393224 | tf_op jit(solution)/shard_map/ppermute | solution.py:63
  234.6 11.1 %collective-permute-start.39 = (bf16[128,512]{1,0:T(8,128)(2,1)S(1)}, bf16[128,512]{1,0:T(8,128)(2,1)S(1)}, u32[]{:S(2)}, u32[]{:S(2)}) collective-permute-start(bf16[128,512]{1,0:T(8,128)(2,1)S(1)} %get-tuple-element.107), channel_id=1, source_target_pairs={{0,6},{1,7},{2,0},{3,1},{4,2},{5,3},{6,4},{7,5},{8,14},{9,15},{10,... | collective-permute-start | bytes 393224 | tf_op jit(solution)/shard_map/ppermute | solution.py:63
  (37 other events, 266.3 us)

commit v3 on v2

--- a/solution.py
+++ b/solution.py
@@ -56,7 +56,6 @@
 
 FIRST = {s: step_first(s) for s in (1, 2, 3)}
 SECOND = {s: step_second(s) for s in (1, 2, 3)}
-TWIN = pairs(lambda y, x, z, c: (x, y, z, 1 - c))
 
 
 def move(value, links):
@@ -79,7 +78,7 @@
     return found
 
 
-def params(mib=50):
+def params(mib=24):
     return pltpu.CompilerParams(vmem_limit_bytes=mib << 20)
 
 
@@ -142,6 +141,12 @@
     return jnp.concatenate([ref[...] for ref in refs], 0)
 
 
+def pairs_of(refs):
+    return [
+        jnp.concatenate([refs[i][...], refs[i + 1][...]], 0) for i in range(0, len(refs), 2)
+    ]
+
+
 def mixed(u_rows, slopes, head):
     slope = (
         slopes[:, 0:1].astype(F32) + slopes[:, 1:2].astype(F32) + slopes[:, 2:3].astype(F32)
@@ -149,13 +154,12 @@
     return (u_rows.astype(F32) + slope * head).astype(BF)
 
 
-def first_kernel(core, *refs):
-    slopes, (turned_inputs, u_rows, head, gate, up, down_out, input_out, weight_out) = (
-        refs[4:8],
-        refs[8:],
-    )
+def near_kernel(*refs):
+    pieces, slopes, refs = pairs_of(refs[:6]), refs[6:12], refs[12:]
+    turned_inputs, u_all, head, weight, down_out, input_out, weight_out = refs
     step = pl.program_id(0)
-    piece = joined(refs[:4])
+    n = pieces[0].shape[0]
+    starts = (0, n, 3 * n)
 
     @pl.when(step == 0)
     def _():
@@ -163,99 +167,136 @@
 
     @pl.when(step < 2)
     def _():
-        down_out[...] = transpose_product(piece, mixed(u_rows[...], joined(slopes), head[...]))
-
-    def run(weight):
-        input_out[...] += right_transpose(piece, weight[...])
-        weight_out[...] = product(turned_inputs[...], piece)
-
-    pl.when((step >= 2) & (step < 4))(lambda: run(gate))
-    pl.when(step >= 4)(lambda: run(up))
-
-
-def first_products(core, pieces, gate_weight, up_weight, turned_inputs, u_rows, head):
-    depth, count = turned_inputs.shape
-    tile = gate_weight.shape[1] // 4
-    h = count // 4
-    whole = lambda v: pl.BlockSpec(v.shape, lambda i, s: (0, 0))
-    return pl.pallas_call(
-        first_kernel,
+        found = None
+        for piece, slope, at in zip(pieces, pairs_of(slopes), starts):
+            term = transpose_product(piece, mixed(u_all[at : at + n], slope, head[...]))
+            found = term if found is None else found + term
+        down_out[...] = found
+
+    @pl.when(step >= 2)
+    def _():
+        found = None
+        for i, piece in enumerate(pieces):
+            input_out[i * n : (i + 1) * n] += product(piece, weight[...])
+            term = product(turned_inputs[:, starts[i] : starts[i] + n], piece)
+            found = term if found is None else found + term
+        weight_out[...] = found
+
+
+def near_products(pieces, turned_weight, turned_inputs, u_all, head):
+    depth, total = turned_inputs.shape
+    tile = turned_weight.shape[0] // 4
+    h = pieces[0].shape[0]
+    n = 2 * h
+    return pl.pallas_call(
+        near_kernel,
         out_shape=[
             jax.ShapeDtypeStruct((2 * tile, depth), F32),
-            jax.ShapeDtypeStruct((count, depth), F32),
+            jax.ShapeDtypeStruct((3 * n, depth), F32),
             jax.ShapeDtypeStruct((depth, 4 * tile), F32),
         ],
-        grid_spec=pltpu.PrefetchScalarGridSpec(
-            num_scalar_prefetch=1,
+        grid_spec=pl.GridSpec(
             grid=(6,),
-            in_specs=[pl.BlockSpec((h, tile), lambda i, s: (0, i))] * 4
-            + [pl.BlockSpec((h, 128), lambda i, s: (0, 6 * tile // 128))] * 4
+            in_specs=[pl.BlockSpec((h, tile), lambda i: (0, i))] * 6
+            + [pl.BlockSpec((h, 128), lambda i: (0, 6 * tile // 128))] * 6
             + [
-                whole(turned_inputs),
-                whole(u_rows),
-                whole(head),
-                pl.BlockSpec((depth, tile), lambda i, s: (0, 2 * s[0] + jnp.clip(i - 2, 0, 1))),
-                pl.BlockSpec((depth, tile), lambda i, s: (0, 2 * s[0] + jnp.clip(i - 4, 0, 1))),
+                pl.BlockSpec((depth, total), lambda i: (0, 0)),
+                pl.BlockSpec((total, depth), lambda i: (0, 0)),
+                pl.BlockSpec((1, depth), lambda i: (0, 0)),
+                pl.BlockSpec((tile, depth), lambda i: (jnp.maximum(i - 2, 0), 0)),
             ],
             out_specs=[
-                pl.BlockSpec((tile, depth), lambda i, s: (jnp.minimum(i, 1), 0)),
-                pl.BlockSpec((count, depth), lambda i, s: (0, 0)),
-                pl.BlockSpec((depth, tile), lambda i, s: (0, jnp.maximum(i - 2, 0))),
+                pl.BlockSpec((tile, depth), lambda i: (jnp.minimum(i, 1), 0)),
+                pl.BlockSpec((3 * n, depth), lambda i: (0, 0)),
+                pl.BlockSpec((depth, tile), lambda i: (0, jnp.maximum(i - 2, 0))),
             ],
         ),
-        compiler_params=params(),
-        name="first_products",
-    )(core[None], *pieces, *pieces, turned_inputs, u_rows, head, gate_weight, up_weight)
-
-
-def down_kernel(*refs):
-    u_rows, head, near, out = refs[8:]
-    out[...] = near[...] + transpose_product(
-        joined(refs[:4]), mixed(u_rows[...], joined(refs[4:8]), head[...])
-    )
-
-
-def down_product(pieces, u_rows, head, near):
+        compiler_params=params(24),
+        name="near_products",
+    )(*pieces, *pieces, turned_inputs, u_all, head, turned_weight)
+
+
+def down_kernel(top, bottom, slope_top, slope_bottom, u_far, head, near, out):
+    slopes = jnp.concatenate([slope_top[...], slope_bottom[...]], 0)
+    rows = jnp.concatenate([top[...], bottom[...]], 0)
+    out[...] = near[...] + transpose_product(rows, mixed(u_far[...], slopes, head[...]))
+
+
+def down_product(top, bottom, u_all, head, near):
     width, depth = near.shape
     tile = width // 2
-    h = pieces[0].shape[0]
+    h = top.shape[0]
+    piece = pl.BlockSpec((h, tile), lambda i: (0, i))
+    slope = pl.BlockSpec((h, 128), lambda i: (0, 6 * tile // 128))
     return pl.pallas_call(
         down_kernel,
         out_shape=jax.ShapeDtypeStruct((width, depth), F32),
         grid=(2,),
-        in_specs=[pl.BlockSpec((h, tile), lambda i: (0, i))] * 4
-        + [pl.BlockSpec((h, 128), lambda i: (0, 6 * tile // 128))] * 4
-        + [
-            pl.BlockSpec(u_rows.shape, lambda i: (0, 0)),
+        in_specs=[
+            piece,
+            piece,
+            slope,
+            slope,
+            pl.BlockSpec((2 * h, depth), lambda i: (2, 0)),
             pl.BlockSpec((1, depth), lambda i: (0, 0)),
             pl.BlockSpec((tile, depth), lambda i: (i, 0)),
         ],
         out_specs=pl.BlockSpec((tile, depth), lambda i: (i, 0)),
-        compiler_params=params(),
+        compiler_params=params(24),
         name="down_product",
-    )(*pieces, *pieces, u_rows, head, near)
-
-
-def input_kernel(core, source, *refs):
-    gate, up, near, own_out, other_out, total = refs[4:]
+    )(top, bottom, top, bottom, u_all, head, near)
+
+
+def turn_kernel(core, gate, up, out):
+    del core
     step = pl.program_id(0)
-    piece = joined(refs[:4])
-    n = near.shape[0]
+
+    @pl.when(step < 2)
+    def _():
+        out[...] = gate[...].T
+
+    @pl.when(step >= 2)
+    def _():
+        out[...] = up[...].T
+
+
+def turned_columns(core, gate_weight, up_weight):
+    depth, width = gate_weight.shape
+    tile = width // 4
+    return pl.pallas_call(
+        turn_kernel,
+        out_shape=jax.ShapeDtypeStruct((width, depth), BF),
+        grid_spec=pltpu.PrefetchScalarGridSpec(
+            num_scalar_prefetch=1,
+            grid=(4,),
+            in_specs=[
+                pl.BlockSpec((depth, tile), lambda i, s: (0, 2 * s[0] + jnp.minimum(i, 1))),
+                pl.BlockSpec((depth, tile), lambda i, s: (0, 2 * s[0] + jnp.maximum(i - 2, 0))),
+            ],
+            out_specs=pl.BlockSpec((tile, depth), lambda i, s: (i, 0)),
+        ),
+        compiler_params=params(16),
+        name="turned_columns",
+    )(core[None], gate_weight, up_weight)
+
+
+def input_kernel(source, top, bottom, weight, near, own_out, other_out, total):
+    step = pl.program_id(0)
+    n = near.shape[0] // 3
+    h = n // 2
 
     @pl.when(step == 0)
     def _():
-        total[:n] = near[...]
-        total[n:] = jnp.zeros((n, total.shape[1]), F32)
-
-    def run(weight):
-        total[n:] += right_transpose(piece, weight[...])
-
-    pl.when(step < 2)(lambda: run(gate))
-    pl.when(step >= 2)(lambda: run(up))
+        total[: 2 * n] = near[: 2 * n]
+        total[2 * n : 3 * n] = jnp.zeros((n, total.shape[1]), F32)
+        total[3 * n :] = near[2 * n :]
+
+    total[2 * n : 2 * n + h] += product(top[...], weight[...])
+    total[2 * n + h : 3 * n] += product(bottom[...], weight[...])
 
     @pl.when(step == pl.num_programs(0) - 1)
     def _():
-        m = n // 8
+        m = n // 4
         for i in range(8):
             own_out[i * m : (i + 1) * m] = total[pl.ds(pl.multiple_of(source[i] * m, m), m)]
             other_out[i * m : (i + 1) * m] = total[
@@ -263,10 +304,10 @@
             ].astype(BF)
 
 
-def input_product(core, source, pieces, gate_weight, up_weight, near):
-    depth = gate_weight.shape[0]
-    tile = gate_weight.shape[1] // 4
-    h = pieces[0].shape[0]
+def input_product(source, top, bottom, turned_weight, near):
+    depth = turned_weight.shape[1]
+    tile = turned_weight.shape[0] // 4
+    h = top.shape[0]
     return pl.pallas_call(
         input_kernel,
         out_shape=[
@@ -274,60 +315,94 @@
             jax.ShapeDtypeStruct((4 * h, depth), BF),
         ],
         grid_spec=pltpu.PrefetchScalarGridSpec(
-            num_scalar_prefetch=2,
+            num_scalar_prefetch=1,
             grid=(4,),
-            in_specs=[pl.BlockSpec((h, tile), lambda i, s, t: (0, i + 2))] * 4
+            in_specs=[pl.BlockSpec((h, tile), lambda i, s: (0, i + 2))] * 2
             + [
-                pl.BlockSpec((depth, tile), lambda i, s, t: (0, 2 * s[0] + jnp.minimum(i, 1))),
-                pl.BlockSpec(
-                    (depth, tile), lambda i, s, t: (0, 2 * s[0] + jnp.maximum(i - 2, 0))
-                ),
-                pl.BlockSpec((4 * h, depth), lambda i, s, t: (0, 0)),
+                pl.BlockSpec((tile, depth), lambda i, s: (i, 0)),
+                pl.BlockSpec((6 * h, depth), lambda i, s: (0, 0)),
             ],
-            out_specs=[pl.BlockSpec((4 * h, depth), lambda i, s, t: (0, 0))] * 2,
+            out_specs=[pl.BlockSpec((4 * h, depth), lambda i, s: (0, 0))] * 2,
             scratch_shapes=[pltpu.VMEM((8 * h, depth), F32)],
         ),
-        compiler_params=params(),
+        compiler_params=params(24),
         name="input_product",
-    )(core[None], source, *pieces, gate_weight, up_weight, near)
-
-
-def weight_kernel(core, *refs):
-    turned_inputs, near, keep_out, send_out = refs[4:]
-    piece = joined(refs[:4])
-    n = keep_out.shape[0]
+    )(source, top, bottom, turned_weight, near)
+
+
+def weight_kernel(core, top, bottom, turned_inputs, near, gate_out, up_out, send_out):
+    step = pl.program_id(0)
+    n = gate_out.shape[0]
+    h = top.shape[0]
+    piece = joined((top, bottom))
 
     def product_of(first):
         rows = pl.ds(pl.multiple_of(first, n), n)
-        return near[rows, :] + product(turned_inputs[rows, :], piece)
-
-    keep_out[...] = product_of(core[0] * n)
+        return near[rows, :] + product(turned_inputs[rows, 4 * h : 6 * h], piece)
+
+    def keep(out):
+        out[...] = product_of(core[0] * n)
+
+    pl.when(step < 2)(lambda: keep(gate_out))
+    pl.when(step >= 2)(lambda: keep(up_out))
     send_out[...] = product_of((1 - core[0]) * n).astype(BF)
 
 
-def weight_product(core, pieces, turned_inputs, near):
+def weight_product(core, top, bottom, turned_inputs, near):
     depth, width = near.shape
     tile = width // 4
-    h = pieces[0].shape[0]
+    h = top.shape[0]
+    rows = depth // 2
     return pl.pallas_call(
         weight_kernel,
         out_shape=[
-            jax.ShapeDtypeStruct((depth // 2, width), F32),
-            jax.ShapeDtypeStruct((depth // 2, width), BF),
+            jax.ShapeDtypeStruct((rows, width), F32),
+            jax.ShapeDtypeStruct((rows, width), F32),
+            jax.ShapeDtypeStruct((rows, width), BF),
         ],
         grid_spec=pltpu.PrefetchScalarGridSpec(
             num_scalar_prefetch=1,
             grid=(4,),
-            in_specs=[pl.BlockSpec((h, tile), lambda i, s: (0, i + 2))] * 4
+            in_specs=[pl.BlockSpec((h, tile), lambda i, s: (0, i + 2))] * 2
             + [
                 pl.BlockSpec(turned_inputs.shape, lambda i, s: (0, 0)),
                 pl.BlockSpec((depth, tile), lambda i, s: (0, i)),
             ],
-            out_specs=[pl.BlockSpec((depth // 2, tile), lambda i, s: (0, i))] * 2,
+            out_specs=[
+                pl.BlockSpec((rows, tile), lambda i, s: (0, 2 * s[0] + jnp.minimum(i, 1))),
+                pl.BlockSpec((rows, tile), lambda i, s: (0, 2 * s[0] + jnp.maximum(i - 2, 0))),
+                pl.BlockSpec((rows, tile), lambda i, s: (0, i)),
+            ],
         ),
-        compiler_params=params(),
+        compiler_params=params(24),
         name="weight_product",
-    )(core[None], *pieces, turned_inputs, near)
+    )(core[None], top, bottom, turned_inputs, near)
+
+
+def fill_kernel(core, gate_part, up_part, gate_in, up_in, gate_out, up_out):
+    del core, gate_in, up_in
+    gate_out[...] = gate_part[...].astype(F32)
+    up_out[...] = up_part[...].astype(F32)
+
+
+def fill_columns(core, other, gate_grad, up_grad):
+    rows, width = gate_grad.shape
+    tile = width // 4
+    part = lambda first: pl.BlockSpec((rows, tile), lambda i, s: (0, first + i))
+    target = pl.BlockSpec((rows, tile), lambda i, s: (0, 2 - 2 * s[0] + i))
+    return pl.pallas_call(
+        fill_kernel,
+        out_shape=[jax.ShapeDtypeStruct((rows, width), F32)] * 2,
+        grid_spec=pltpu.PrefetchScalarGridSpec(
+            num_scalar_prefetch=1,
+            grid=(2,),
+            in_specs=[part(0), part(2)] + [pl.BlockSpec(memory_space=pl.ANY)] * 2,
+            out_specs=[target] * 2,
+        ),
+        input_output_aliases={3: 0, 4: 1},
+        compiler_params=params(16),
+        name="fill_columns",
+    )(core[None], other, other, gate_grad, up_grad)
 
 
 def add_halves(direct, added, arrived, top_added):
@@ -390,13 +465,10 @@
     row = lax.axis_index("row")
     z = lax.axis_index("col")
     y, x = row // SIDE, row % SIDE
-    a = jnp.where(core == 0, x, y)
-    b = jnp.where(core == 0, y, x)
-    turn = (a + 4 - z) % 4
+    turn = (x + 4 - z) % 4
     mine = tokens // 2
     total = tokens * 8
     head_value = reward_head.astype(F32)
-    weights = (gate_weight, up_weight)
     all_weights = (gate_weight, up_weight, down_weight)
 
     def around_z(value):
@@ -414,8 +486,8 @@
 
     def ordered(whole):
         whole = lax.dynamic_slice_in_dim(jnp.concatenate([whole, whole], 0), turn, 4, 0)
-        whole = lax.dynamic_slice_in_dim(jnp.concatenate([whole, whole], 1), b, 4, 1)
-        return whole.reshape(total, depth)
+        whole = lax.dynamic_slice_in_dim(jnp.concatenate([whole, whole], 1), y, 4, 1)
+        return jnp.where(core == 0, whole, whole.transpose(1, 0, 2, 3)).reshape(total, depth)
 
     down_half = lax.dynamic_slice_in_dim(down_weight, core * half, half, 0)
     head_hidden = jnp.dot(down_half.astype(F32), head_value, precision=lax.Precision.HIGHEST)
@@ -435,10 +507,8 @@
     rest = project(core, x_all, u_all, all_weights, heads, False)
     top, bottom = ring_reduce(far, rest[:2], rest[2:4], rest[4:], FIRST)
     tags = both_cores(jnp.concatenate(around_z(jnp.stack([labels, label_mask])), 1), 1)
-    late, later = tokens * 3, tokens * 7
-    early_u = jnp.concatenate([u_all[later:], u_all[:late]], 0)
-    early_x = jnp.concatenate([x_all[later:], x_all[:late]], 0).T
-    late_u, late_x = u_all[late:later], x_all[late:later].T
+    turned_inputs = x_all.T
+    turned_weight = turned_columns(core, gate_weight, up_weight)
 
     first, second = halves(top)
     third, fourth = halves(bottom)
@@ -456,14 +526,14 @@
     extra = sums[:, 3 * half :]
     own_inputs, head_hidden = extra[:, 0], extra[:, 1 : 1 + per_token].reshape(half)
     own_tags = lax.dynamic_slice_in_dim(
-        tags.reshape(2, total), (turn * 4 + b) * mine, mine, 1
+        tags.reshape(2, total), (turn * 4 + y) * mine, mine, 1
     ).astype(F32)
     sigmoid_gate = jax.nn.sigmoid(gate)
     hidden = (gate * sigmoid_gate * upper).astype(BF)
 
     part = jnp.sum(hidden.astype(F32) * head_hidden[None, :], axis=1)
     part = part + move(part, AHEAD[1]) + move(part, AHEAD[2]) + move(part, AHEAD[3])
-    score = own_inputs + part + move(part, TWIN)
+    score = own_inputs + part + move(part, OTHER)
     slope = reward_weight * own_tags[1] * (jax.nn.sigmoid(score) - own_tags[0])
     grad_hidden = grad_upstream + slope[:, None] * head_hidden[None, :]
     grad_gate = (grad_hidden * upper * sigmoid_gate * (1.0 + gate * (1.0 - sigmoid_gate))).astype(
@@ -478,25 +548,26 @@
     top = jnp.concatenate([block, *near[:2]], 0)
     bottom = jnp.concatenate([*far, *near[2:]], 0)
     near = ring_start(top, bottom, FIRST)
-    far = ring_pass(near, FIRST)
+    far_top, far_bottom = ring_pass(near, FIRST)
+
     head_row = head_value[None, :]
-    early = (near[3], top, bottom, near[0])
-    near_down, near_input, near_weight = first_products(
-        core, early, *weights, early_x, early_u, head_row
-    )
-    *last, near_down, near_input, near_weight = together(
-        near[1], *far, near[2], near_down, near_input, near_weight
+    near_down, near_input, near_weight = near_products(
+        [top, bottom, *near], turned_weight, turned_inputs, u_all, head_row
+    )
+    far_top, far_bottom, near_down, near_weight, near_input = together(
+        far_top, far_bottom, near_down, near_weight, near_input
     )
 
     spot = jnp.arange(16, dtype=jnp.int32)
     whose = jnp.where(spot < 8, core, 1 - core)
-    ahead_of = (z + (spot // 2) % 4 + 4 - a) % 4
-    source = ahead_of * 4 + (whose * 2 + spot % 2 + 4 - b) % 4
-    source_early = (source + 2) % 16
-    own_part, other_part = input_product(core, source_early, last, *weights, near_input)
+    along_x = (z + (spot // 2) % 4 + 4 - x) % 4
+    along_y = (whose * 2 + spot % 2 + 4 - y) % 4
+    source = jnp.where(core == 0, along_x * 4 + along_y, along_y * 4 + along_x)
+    last = (far_top, far_bottom)
+    own_part, other_part = input_product(source, *last, turned_weight, near_input)
     near_weight, own_part = together(near_weight, own_part)
     other_arrived = move(other_part, OTHER)
-    keep, send = weight_product(core, last, late_x, near_weight)
+    gate_grad, up_grad, send = weight_product(core, *last, turned_inputs, near_weight)
     other = move(send, OTHER)
     near_down, other_arrived = together(near_down, other_arrived)
     blocks = jnp.split(own_part + other_arrived.astype(F32), 4, 0)
@@ -504,12 +575,12 @@
     blocks = [t.astype(BF) for t in blocks[1:]]
     *blocks, near_down = together(*blocks, near_down)
     arrived = [move(blocks[s - 1], AHEAD[s]) for s in (1, 2, 3)]
-    down_grad = down_product(last, late_u, head_row, near_down)
+    down_grad = down_product(*last, u_all, head_row, near_down)
 
     slope_parts = jnp.concatenate(
         [
             p[:, 6 * (half // 2) :]
-            for p in (top, bottom, near[0], *last, near[3])
+            for p in (top, bottom, *near[:2], far_top, far_bottom, *near[2:])
         ],
         0,
     )
@@ -518,11 +589,7 @@
         [lax.dynamic_slice_in_dim(slope_all, source[i] * mine, mine, 0) for i in range(2)]
     )
 
-    def both_halves(start):
-        k, o = keep[:, start : start + half], other[:, start : start + half].astype(F32)
-        return jnp.concatenate([jnp.where(core == 0, k, o), jnp.where(core == 0, o, k)], axis=1)
-
-    gate_grad, up_grad = both_halves(0), both_halves(half)
+    gate_grad, up_grad = fill_columns(core, other, gate_grad, up_grad)
     *arrived, gate_grad, up_grad, down_grad = together(*arrived, gate_grad, up_grad, down_grad)
     for t in arrived:
         input_sum = input_sum + t.astype(F32)

time: 248 us -> 237 us (0.956)
  Pallas kernels: 56.8 us -> 49 us
  starting transfers between devices: 69.6 us -> 63.9 us
  waiting for transfers between devices: 75.6 us -> 80.5 us
    slice x6 -> x0, local copies, waits for them, and re-layouts: 6.17 us -> none  [the longest x2 2.84 us: per_device(): early_x = jnp.concatenate([x_all[later:], x_all[:late]], 0).T]
    ppermute x41, starting transfers between devices: 69.6 us -> 63.9 us  [move(): return lax.ppermute(value, AXES, links)]
    concatenate x3 -> x0, other arithmetic: 5.6 us -> none  [the longest x2 4.57 us: both_halves(): jnp.concatenate([jnp.where(core == 0, k, o), jnp.where(core == 0, o, k)],...]
    ppermute x41, waiting for transfers between devices: 75.6 us -> 80.5 us  [move(): return lax.ppermute(value, AXES, links)]
    pallas_call x2, Pallas kernels: 20.4 us -> 15.6 us  [project(): pl.pallas_call(kernel, out_shape=[jax.ShapeDtypeStruct((h, 6 * tile + 128...]
    unnamed x60 -> x65, local copies, waits for them, and re-layouts: 15.9 us -> 19.6 us
    pallas_call x1, Pallas kernels: 6.89 us -> 4.28 us  [input_product(): pl.pallas_call(input_kernel, out_shape=[jax.ShapeDtypeStruct((4 * h, dept...]
    pallas_call x2 -> x4, Pallas kernels: 20.5 us -> 21.7 us  [the longest x1 12.7 us: near_products(): pl.pallas_call(near_kernel, out_shape=[jax.ShapeDtypeStruct((2 * tile, de...]
  transfers between devices with their start and end apart: 41 -> 41, of which waited for: 21 -> 22; matrix products, arithmetic and copies ran while one was open for 13% -> 7% of each run, Pallas kernels for 13% -> 14%
where the time goes in v3:
time: 237 us; the launch traced here: 236 us
  waiting for transfers between devices  80.5 us (34%)
  starting transfers between devices  63.9 us (27%)
  Pallas kernels  49 us (21%)
  local copies, waits for them, and re-layouts  25.2 us (11%)
  other arithmetic  12.8 us (5%)
  between operations  2.48 us (1%)
    ppermute x41, waiting for transfers between devices, move(): return lax.ppermute(value, AXES, links)  80.5 us
    ppermute x41, starting transfers between devices, move(): return lax.ppermute(value, AXES, links)  63.9 us
    unnamed x65, local copies, waits for them, and re-layouts  19.6 us
    pallas_call x2, Pallas kernels, project(): pl.pallas_call(kernel, out_shape=[jax.ShapeDtypeStruct((h, 6 * tile + 128...  15.6 us
    pallas_call x1, Pallas kernels, near_products(): pl.pallas_call(near_kernel, out_shape=[jax.ShapeDtypeStruct((2 * tile, de...  12.7 us
    pallas_call x1, Pallas kernels, weight_product(): pl.pallas_call(weight_kernel, out_shape=[jax.ShapeDtypeStruct((rows, widt...  5.22 us
  transfers between devices with their start and end apart: 41, of which 22 were waited for; matrix products, arithmetic and copies ran while one was open for 7% of the time, Pallas kernels for 14%

profile of v3, /device:TPU:1, one launch (start us, length us, event | category | flops | bytes accessed | tf_op | source)
XLA Modules:
  0.0 236.0 jit_solution(3757004192526220746)
XLA Ops:
  0.7 4.7 %collective-permute-start = (bf16[128,512]{1,0:T(8,128)(2,1)}, bf16[128,512]{1,0:T(8,128)(2,1)S(1)}, u32[]{:S(2)}, u32[]{:S(2)}) collective-permute-start(bf16[128,512]{1,0:T(8,128)(2,1)} %param.8), channel_id=1, source_target_pairs={{0,6},{1,7},{2,0},{3,1},{4,2},{5,3},{6,4},{7,5},{8,14},{9,15},{10,... | collective-permute-start | bytes 393224 | tf_op jit(solution)/shard_map/ppermute | solution.py:62
  19.4 2.7 %collective-permute-start.7 = (bf16[512,512]{1,0:T(8,128)(2,1)S(1)}, bf16[512,512]{1,0:T(8,128)(2,1)S(1)}, u32[]{:S(2)}, u32[]{:S(2)}) collective-permute-start(bf16[512,512]{1,0:T(8,128)(2,1)S(1)} %constant_dynamic-update-slice_fusion.4), channel_id=1, source_target_pairs={{0,1},{1,0},{2,3},{3,2},{4,5},{5,4},{6,7},{7,6},{8,9},{9,8},{10,11... | collective-permute-start | bytes 1572872 | tf_op jit(solution)/shard_map/ppermute | solution.py:62
  28.3 4.8 %project_far.1 = (bf16[128,5504]{1,0:T(8,128)(2,1)S(1)}, bf16[128,5504]{1,0:T(8,128)(2,1)S(1)}) custom-call(s32[1]{0:T(128)} %bitcast.core_ref.core, bf16[1024,512]{1,0:T(8,128)(2,1)S(1)} %bitcast.38, bf16[1024,512]{1,0:T(8,128)(2,1)S(1)} %bitcast.34, bf16[512,3584]{1,0:T(8,128)(2,1)S(1)} %copy-done, bf16[512,3584]{1,0:T(8,128)(2,1)S(1)} %copy-done.2, ...), custom_call_target="tpu_custom_call" | custom-call | tf_op jit(solution)/shard_map/project_far/pallas_call | solution.py:118
  37.0 10.9 %project_rest.1 = (bf16[128,5504]{1,0:T(8,128)(2,1)S(1)}, bf16[128,5504]{1,0:T(8,128)(2,1)S(1)}, f32[128,5504]{1,0:T(8,128)S(1)}, f32[128,5504]{1,0:T(8,128)S(1)...) custom-call(s32[1]{0:T(128)} %bitcast.core_ref.core, bf16[1024,512]{1,0:T(8,128)(2,1)S(1)} %bitcast.39, ...), custom_call_target="tpu_custom_call" | custom-call | tf_op jit(solution)/shard_map/project_rest/pallas_call | solution.py:118
  47.9 4.3 %collective-permute-done.8.arrived_ref = bf16[128,5504]{1,0:T(8,128)(2,1)S(1)} collective-permute-done((bf16[128,5504]{1,0:T(8,128)(2,1)S(1)}, bf16[128,5504]{1,0:T(8,128)(2,1)S(1)}, u32[]{:S(2)}, u32[]{:S(2)}) %collective-permute-start.8) | collective-permute-done | bytes 1409056 | tf_op jit(solution)/shard_map/ppermute | solution.py:62
  59.3 29.4 %collective-permute-done.10 = bf16[256,5504]{1,0:T(8,128)(2,1)S(1)} collective-permute-done((bf16[256,5504]{1,0:T(8,128)(2,1)S(1)}, bf16[256,5504]{1,0:T(8,128)(2,1)S(1)}, u32[]{:S(2)}, u32[]{:S(2)}) %collective-permute-start.10) | collective-permute-done | bytes 2818080 | tf_op jit(solution)/shard_map/ppermute | solution.py:62
  97.3 3.7 %collective-permute-done.12 = bf16[32,5504]{1,0:T(8,128)(2,1)S(1)} collective-permute-done((bf16[32,5504]{1,0:T(8,128)(2,1)S(1)}, bf16[32,5504]{1,0:T(8,128)(2,1)S(1)}, u32[]{:S(2)}, u32[]{:S(2)}) %collective-permute-start.12) | collective-permute-done | bytes 352288 | tf_op jit(solution)/shard_map/ppermute | solution.py:62
  106.6 3.2 %collective-permute-done.17 = s32[2,128]{1,0:T(2,128)S(1)} collective-permute-done((s32[2,128]{1,0:T(2,128)S(1)}, s32[2,128]{1,0:T(2,128)S(1)}, u32[]{:S(2)}, u32[]{:S(2)}) %collective-permute-start.17) | collective-permute-done | bytes 1056 | tf_op jit(solution)/shard_map/ppermute | solution.py:62
  109.9 5.7 %collective-permute-start.19 = (s32[2,512]{1,0:T(2,128)S(1)}, s32[2,512]{1,0:T(2,128)S(1)}, u32[]{:S(2)}, u32[]{:S(2)}) collective-permute-start(s32[2,512]{1,0:T(2,128)S(1)} %pad_add_fusion), channel_id=1, source_target_pairs={{0,1},{1,0},{2,3},{3,2},{4,5},{5,4},{6,7},{7,6},{8,9},{9,8},{10,11... | collective-permute-start | bytes 12296 | tf_op jit(solution)/shard_map/ppermute | solution.py:62
  124.1 3.9 %collective-permute-start.23 = (f32[64]{0:T(128)S(1)}, f32[64]{0:T(128)S(1)}, u32[]{:S(2)}, u32[]{:S(2)}) collective-permute-start(f32[64]{0:T(128)S(1)} %add_add_fusion), channel_id=1, source_target_pairs={{0,1},{1,0},{2,3},{3,2},{4,5},{5,4},{6,7},{7,6},{8,9},{9,8},{10,11... | collective-permute-start | bytes 776 | tf_op jit(solution)/shard_map/ppermute | solution.py:62
  131.5 2.7 %collective-permute-start.24 = (bf16[32,5504]{1,0:T(8,128)(2,1)S(1)}, bf16[32,5504]{1,0:T(8,128)(2,1)S(1)}, u32[]{:S(2)}, u32[]{:S(2)}) collective-permute-start(bf16[32,5504]{1,0:T(8,128)(2,1)S(1)} %get-tuple-element.138), channel_id=1, source_target_pairs={{0,96},{1,25},{2,98},{3,27},{4,100},{5,29},{6,102},{7,31},{8,104},... | collective-permute-start | bytes 1056776 | tf_op jit(solution)/shard_map/ppermute | solution.py:62
  135.7 2.8 %collective-permute-done.24 = bf16[32,5504]{1,0:T(8,128)(2,1)S(1)} collective-permute-done((bf16[32,5504]{1,0:T(8,128)(2,1)S(1)}, bf16[32,5504]{1,0:T(8,128)(2,1)S(1)}, u32[]{:S(2)}, u32[]{:S(2)}) %collective-permute-start.24) | collective-permute-done | bytes 352288 | tf_op jit(solution)/shard_map/ppermute | solution.py:62
  138.5 3.1 %collective-permute-start.28 = (bf16[32,5504]{1,0:T(8,128)(2,1)S(1)}, bf16[32,5504]{1,0:T(8,128)(2,1)S(1)}, u32[]{:S(2)}, u32[]{:S(2)}) collective-permute-start(bf16[32,5504]{1,0:T(8,128)(2,1)S(1)} %collective-permute-done.24), channel_id=1, source_target_pairs={{0,96},{1,25},{2,98},{3,27},{4,100},{5,29},{6,102},{7,31},{8,104},... | collective-permute-start | bytes 1056776 | tf_op jit(solution)/shard_map/ppermute | solution.py:62
  147.3 7.2 %collective-permute-done.30 = bf16[32,5504]{1,0:T(8,128)(2,1)S(1)} collective-permute-done((bf16[32,5504]{1,0:T(8,128)(2,1)S(1)}, bf16[32,5504]{1,0:T(8,128)(2,1)S(1)}, u32[]{:S(2)}, u32[]{:S(2)}) %collective-permute-start.30) | collective-permute-done | bytes 352288 | tf_op jit(solution)/shard_map/ppermute | solution.py:62
  156.8 2.7 %collective-permute-start.34 = (bf16[128,5504]{1,0:T(8,128)(2,1)}, bf16[128,5504]{1,0:T(8,128)(2,1)}, u32[]{:S(2)}, u32[]{:S(2)}) collective-permute-start(bf16[128,5504]{1,0:T(8,128)(2,1)} %constant_dynamic-update-slice_fusion.8.refs_1_.refs_7_), channel_id=1, source_target_pairs={{0,24},{1,97},{2,26},{3,99},{4,28},{5,101},{6,30},{7,103},{8,0},{9... | collective-permute-start | bytes 4227080 | tf_op jit(solution)/shard_map/ppermute | solution.py:62
  159.5 3.4 %collective-permute-done.26.refs_2_.refs_8_ = bf16[128,5504]{1,0:T(8,128)(2,1)} collective-permute-done((bf16[128,5504]{1,0:T(8,128)(2,1)}, bf16[128,5504]{1,0:T(8,128)(2,1)}, u32[]{:S(2)}, u32[]{:S(2)}) %collective-permute-start.26) | collective-permute-done | bytes 1409056 | tf_op jit(solution)/shard_map/ppermute | solution.py:62
  162.9 3.4 %collective-permute-start.27 = (bf16[128,5504]{1,0:T(8,128)(2,1)}, bf16[128,5504]{1,0:T(8,128)(2,1)S(1)}, u32[]{:S(2)}, u32[]{:S(2)}) collective-permute-start(bf16[128,5504]{1,0:T(8,128)(2,1)} %collective-permute-done.26.refs_2_.refs_8_), channel_id=1, source_target_pairs={{0,24},{1,97},{2,26},{3,99},{4,28},{5,101},{6,30},{7,103},{8,0},{9... | collective-permute-start | bytes 4227080 | tf_op jit(solution)/shard_map/ppermute | solution.py:62
  166.4 9.8 %collective-permute-done.32.refs_5_.refs_11_ = bf16[128,5504]{1,0:T(8,128)(2,1)} collective-permute-done((bf16[128,5504]{1,0:T(8,128)(2,1)}, bf16[128,5504]{1,0:T(8,128)(2,1)}, u32[]{:S(2)}, u32[]{:S(2)}) %collective-permute-start.32) | collective-permute-done | bytes 1409056 | tf_op jit(solution)/shard_map/ppermute | solution.py:62
  185.1 6.1 %collective-permute-done.35.refs_4_.refs_10_ = bf16[128,5504]{1,0:T(8,128)(2,1)} collective-permute-done((bf16[128,5504]{1,0:T(8,128)(2,1)}, bf16[128,5504]{1,0:T(8,128)(2,1)}, u32[]{:S(2)}, u32[]{:S(2)}) %collective-permute-start.35) | collective-permute-done | bytes 1409056 | tf_op jit(solution)/shard_map/ppermute | solution.py:62
  194.5 12.7 %near_products.1 = (f32[1792,512]{1,0:T(8,128)S(1)}, f32[768,512]{1,0:T(8,128)S(1)}, f32[512,3584]{1,0:T(8,128)S(1)}) custom-call(bf16[128,5504]{1,0:T(8,128)(2,1)} %pad_maximum_fusion.refs_0_.refs_6_, bf16[128,5504]{1,0:T(8,128)(2,1)} %constant_dynamic-update-slice_fusion.8.refs_1_.refs_7_, bf16[128,5504]{1,0:T(8,128)(2,1)} %collective-permute-done.26.refs_2_.refs_8_, ...), custom_call_target="tpu_custom_call" | custom-call | tf_op jit(solution)/shard_map/near_products/pallas_call | solution.py:191
  209.1 4.3 %input_product.1 = (f32[512,512]{1,0:T(8,128)S(1)}, bf16[512,512]{1,0:T(8,128)(2,1)S(1)}) custom-call(s32[16]{0:T(128)S(1)} %broadcast_select_fusion.source, bf16[128,5504]{1,0:T(8,128)(2,1)S(1)} %collective-permute-done.27.top.slope_top, bf16[128,5504]{1,0:T(8,128)(2,1)} %collective-permute-done.33.bottom.slope_bottom, bf16[3584,512]{1,0:T(8,128)(2,1)S(1)} %copy-done.6, ...), custom_call_target="tpu_custom_call" | custom-call | tf_op jit(solution)/shard_map/input_product/pallas_call | solution.py:311
  213.4 5.2 %weight_product.1 = (f32[256,3584]{1,0:T(8,128)}, f32[256,3584]{1,0:T(8,128)}, bf16[256,3584]{1,0:T(8,128)(2,1)S(1)}) custom-call(s32[1]{0:T(128)} %bitcast.core_ref.core, bf16[128,5504]{1,0:T(8,128)(2,1)S(1)} %collective-permute-done.27.top.slope_top, bf16[128,5504]{1,0:T(8,128)(2,1)} %collective-permute-done.33.bottom.slope_bottom, ...), custom_call_target="tpu_custom_call" | custom-call | tf_op jit(solution)/shard_map/weight_product/pallas_call | solution.py:356
  218.6 2.9 %collective-permute-start.40 = (bf16[256,3584]{1,0:T(8,128)(2,1)S(1)}, bf16[256,3584]{1,0:T(8,128)(2,1)S(1)}, u32[]{:S(2)}, u32[]{:S(2)}) collective-permute-start(bf16[256,3584]{1,0:T(8,128)(2,1)S(1)} %get-tuple-element.108), channel_id=1, source_target_pairs={{0,1},{1,0},{2,3},{3,2},{4,5},{5,4},{6,7},{7,6},{8,9},{9,8},{10,11... | collective-permute-start | bytes 5505032 | tf_op jit(solution)/shard_map/ppermute | solution.py:62
  229.7 3.4 %down_product.1 = f32[1792,512]{1,0:T(8,128)} custom-call(bf16[128,5504]{1,0:T(8,128)(2,1)S(1)} %collective-permute-done.27.top.slope_top, bf16[128,5504]{1,0:T(8,128)(2,1)} %collective-permute-done.33.bottom.slope_bottom, bf16[128,5504]{1,0:T(8,128)(2,1)S(1)} %collective-permute-done.27.top.slope_top, ...), custom_call_target="tpu_custom_call" | custom-call | tf_op jit(solution)/shard_map/down_product/pallas_call | solution.py:231
  (192 shorter events, 90.7 us)
Async XLA Ops:
  0.7 11.9 %collective-permute-start = (bf16[128,512]{1,0:T(8,128)(2,1)}, bf16[128,512]{1,0:T(8,128)(2,1)S(1)}, u32[]{:S(2)}, u32[]{:S(2)}) collective-permute-start(bf16[128,512]{1,0:T(8,128)(2,1)} %param.8), channel_id=1, source_target_pairs={{0,6},{1,7},{2,0},{3,1},{4,2},{5,3},{6,4},{7,5},{8,14},{9,15},{10,... | collective-permute-start | bytes 393224 | tf_op jit(solution)/shard_map/ppermute | solution.py:62
  5.3 10.0 %collective-permute-start.2 = (bf16[128,512]{1,0:T(8,128)(2,1)}, bf16[128,512]{1,0:T(8,128)(2,1)S(1)}, u32[]{:S(2)}, u32[]{:S(2)}) collective-permute-start(bf16[128,512]{1,0:T(8,128)(2,1)} %param.8), channel_id=1, source_target_pairs={{0,2},{1,3},{2,4},{3,5},{4,6},{5,7},{6,0},{7,1},{8,10},{9,11},{10,... | collective-permute-start | bytes 393224 | tf_op jit(solution)/shard_map/ppermute | solution.py:62
  6.0 10.8 %collective-permute-start.4 = (bf16[128,512]{1,0:T(8,128)(2,1)}, bf16[128,512]{1,0:T(8,128)(2,1)S(1)}, u32[]{:S(2)}, u32[]{:S(2)}) collective-permute-start(bf16[128,512]{1,0:T(8,128)(2,1)} %param.13), channel_id=1, source_target_pairs={{0,6},{1,7},{2,0},{3,1},{4,2},{5,3},{6,4},{7,5},{8,14},{9,15},{10,... | collective-permute-start | bytes 393224 | tf_op jit(solution)/shard_map/ppermute | solution.py:62
  8.0 8.9 %collective-permute-start.5 = (bf16[128,512]{1,0:T(8,128)(2,1)}, bf16[128,512]{1,0:T(8,128)(2,1)S(1)}, u32[]{:S(2)}, u32[]{:S(2)}) collective-permute-start(bf16[128,512]{1,0:T(8,128)(2,1)} %param.13), channel_id=1, source_target_pairs={{0,4},{1,5},{2,6},{3,7},{4,0},{5,1},{6,2},{7,3},{8,12},{9,13},{10,... | collective-permute-start | bytes 393224 | tf_op jit(solution)/shard_map/ppermute | solution.py:62
  33.1 19.1 %collective-permute-start.8 = (bf16[128,5504]{1,0:T(8,128)(2,1)S(1)}, bf16[128,5504]{1,0:T(8,128)(2,1)S(1)}, u32[]{:S(2)}, u32[]{:S(2)}) collective-permute-start(bf16[128,5504]{1,0:T(8,128)(2,1)S(1)} %get-tuple-element.67), channel_id=1, source_target_pairs={{0,8},{1,33},{2,10},{3,35},{4,12},{5,37},{6,14},{7,39},{8,16},{9,4... | collective-permute-start | bytes 4227080 | tf_op jit(solution)/shard_map/ppermute | solution.py:62
  34.4 17.8 %collective-permute-start.9 = (bf16[128,5504]{1,0:T(8,128)(2,1)S(1)}, bf16[128,5504]{1,0:T(8,128)(2,1)S(1)}, u32[]{:S(2)}, u32[]{:S(2)}) collective-permute-start(bf16[128,5504]{1,0:T(8,128)(2,1)S(1)} %get-tuple-element.68), channel_id=1, source_target_pairs={{0,24},{1,97},{2,26},{3,99},{4,28},{5,101},{6,30},{7,103},{8,0},{9... | collective-permute-start | bytes 4227080 | tf_op jit(solution)/shard_map/ppermute | solution.py:62
  54.2 34.4 %collective-permute-start.10 = (bf16[256,5504]{1,0:T(8,128)(2,1)S(1)}, bf16[256,5504]{1,0:T(8,128)(2,1)S(1)}, u32[]{:S(2)}, u32[]{:S(2)}) collective-permute-start(bf16[256,5504]{1,0:T(8,128)(2,1)S(1)} %add_halves.2), channel_id=1, source_target_pairs={{0,8},{1,33},{2,10},{3,35},{4,12},{5,37},{6,14},{7,39},{8,16},{9,4... | collective-permute-start | bytes 8454152 | tf_op jit(solution)/shard_map/ppermute | solution.py:62
  57.5 33.0 %collective-permute-start.11 = (bf16[256,5504]{1,0:T(8,128)(2,1)S(1)}, bf16[256,5504]{1,0:T(8,128)(2,1)S(1)}, u32[]{:S(2)}, u32[]{:S(2)}) collective-permute-start(bf16[256,5504]{1,0:T(8,128)(2,1)S(1)} %add_halves.3), channel_id=1, source_target_pairs={{0,24},{1,97},{2,26},{3,99},{4,28},{5,101},{6,30},{7,103},{8,0},{9... | collective-permute-start | bytes 8454152 | tf_op jit(solution)/shard_map/ppermute | solution.py:62
  101.1 15.4 %collective-permute-start.14 = (bf16[64,5504]{1,0:T(8,128)(2,1)S(1)}, bf16[64,5504]{1,0:T(8,128)(2,1)}, u32[]{:S(2)}, u32[]{:S(2)}) collective-permute-start(bf16[64,5504]{1,0:T(8,128)(2,1)S(1)} %pad_maximum_fusion.1), channel_id=1, source_target_pairs={{0,32},{1,9},{2,34},{3,11},{4,36},{5,13},{6,38},{7,15},{8,40},{9,1... | collective-permute-start | bytes 2113544 | tf_op jit(solution)/shard_map/ppermute | solution.py:62
  102.5 14.0 %collective-permute-start.15 = (bf16[64,5504]{1,0:T(8,128)(2,1)S(1)}, bf16[64,5504]{1,0:T(8,128)(2,1)}, u32[]{:S(2)}, u32[]{:S(2)}) collective-permute-start(bf16[64,5504]{1,0:T(8,128)(2,1)S(1)} %pad_maximum_fusion.2), channel_id=1, source_target_pairs={{0,96},{1,25},{2,98},{3,27},{4,100},{5,29},{6,102},{7,31},{8,104},... | collective-permute-start | bytes 2113544 | tf_op jit(solution)/shard_map/ppermute | solution.py:62
  134.2 8.1 %collective-permute-start.25 = (bf16[32,5504]{1,0:T(8,128)(2,1)S(1)}, bf16[32,5504]{1,0:T(8,128)(2,1)S(1)}, u32[]{:S(2)}, u32[]{:S(2)}) collective-permute-start(bf16[32,5504]{1,0:T(8,128)(2,1)S(1)} %get-tuple-element.139), channel_id=1, source_target_pairs={{0,96},{1,25},{2,98},{3,27},{4,100},{5,29},{6,102},{7,31},{8,104},... | collective-permute-start | bytes 1056776 | tf_op jit(solution)/shard_map/ppermute | solution.py:62
  134.5 11.6 %collective-permute-start.29 = (bf16[32,5504]{1,0:T(8,128)(2,1)S(1)}, bf16[32,5504]{1,0:T(8,128)(2,1)S(1)}, u32[]{:S(2)}, u32[]{:S(2)}) collective-permute-start(bf16[32,5504]{1,0:T(8,128)(2,1)S(1)} %get-tuple-element.139), channel_id=1, source_target_pairs={{0,32},{1,9},{2,34},{3,11},{4,36},{5,13},{6,38},{7,15},{8,40},{9,1... | collective-permute-start | bytes 1056776 | tf_op jit(solution)/shard_map/ppermute | solution.py:62
  135.7 19.6 %collective-permute-start.31 = (bf16[32,5504]{1,0:T(8,128)(2,1)S(1)}, bf16[32,5504]{1,0:T(8,128)(2,1)S(1)}, u32[]{:S(2)}, u32[]{:S(2)}) collective-permute-start(bf16[32,5504]{1,0:T(8,128)(2,1)S(1)} %get-tuple-element.138), channel_id=1, source_target_pairs={{0,32},{1,9},{2,34},{3,11},{4,36},{5,13},{6,38},{7,15},{8,40},{9,1... | collective-permute-start | bytes 1056776 | tf_op jit(solution)/shard_map/ppermute | solution.py:62
  138.5 8.0 %collective-permute-start.28 = (bf16[32,5504]{1,0:T(8,128)(2,1)S(1)}, bf16[32,5504]{1,0:T(8,128)(2,1)S(1)}, u32[]{:S(2)}, u32[]{:S(2)}) collective-permute-start(bf16[32,5504]{1,0:T(8,128)(2,1)S(1)} %collective-permute-done.24), channel_id=1, source_target_pairs={{0,96},{1,25},{2,98},{3,27},{4,100},{5,29},{6,102},{7,31},{8,104},... | collective-permute-start | bytes 1056776 | tf_op jit(solution)/shard_map/ppermute | solution.py:62
  143.5 19.5 %collective-permute-start.26 = (bf16[128,5504]{1,0:T(8,128)(2,1)}, bf16[128,5504]{1,0:T(8,128)(2,1)}, u32[]{:S(2)}, u32[]{:S(2)}) collective-permute-start(bf16[128,5504]{1,0:T(8,128)(2,1)} %pad_maximum_fusion.refs_0_.refs_6_), channel_id=1, source_target_pairs={{0,24},{1,97},{2,26},{3,99},{4,28},{5,101},{6,30},{7,103},{8,0},{9... | collective-permute-start | bytes 4227080 | tf_op jit(solution)/shard_map/ppermute | solution.py:62
  146.1 8.4 %collective-permute-start.30 = (bf16[32,5504]{1,0:T(8,128)(2,1)S(1)}, bf16[32,5504]{1,0:T(8,128)(2,1)S(1)}, u32[]{:S(2)}, u32[]{:S(2)}) collective-permute-start(bf16[32,5504]{1,0:T(8,128)(2,1)S(1)} %collective-permute-done.29), channel_id=1, source_target_pairs={{0,32},{1,9},{2,34},{3,11},{4,36},{5,13},{6,38},{7,15},{8,40},{9,1... | collective-permute-start | bytes 1056776 | tf_op jit(solution)/shard_map/ppermute | solution.py:62
  156.8 19.3 %collective-permute-start.32 = (bf16[128,5504]{1,0:T(8,128)(2,1)}, bf16[128,5504]{1,0:T(8,128)(2,1)}, u32[]{:S(2)}, u32[]{:S(2)}) collective-permute-start(bf16[128,5504]{1,0:T(8,128)(2,1)} %constant_dynamic-update-slice_fusion.8.refs_1_.refs_7_), channel_id=1, source_target_pairs={{0,8},{1,33},{2,10},{3,35},{4,12},{5,37},{6,14},{7,39},{8,16},{9,4... | collective-permute-start | bytes 4227080 | tf_op jit(solution)/shard_map/ppermute | solution.py:62
  156.8 34.4 %collective-permute-start.35 = (bf16[128,5504]{1,0:T(8,128)(2,1)}, bf16[128,5504]{1,0:T(8,128)(2,1)}, u32[]{:S(2)}, u32[]{:S(2)}) collective-permute-start(bf16[128,5504]{1,0:T(8,128)(2,1)} %pad_maximum_fusion.refs_0_.refs_6_), channel_id=1, source_target_pairs={{0,8},{1,33},{2,10},{3,35},{4,12},{5,37},{6,14},{7,39},{8,16},{9,4... | collective-permute-start | bytes 4227080 | tf_op jit(solution)/shard_map/ppermute | solution.py:62
  156.8 34.4 %collective-permute-start.34 = (bf16[128,5504]{1,0:T(8,128)(2,1)}, bf16[128,5504]{1,0:T(8,128)(2,1)}, u32[]{:S(2)}, u32[]{:S(2)}) collective-permute-start(bf16[128,5504]{1,0:T(8,128)(2,1)} %constant_dynamic-update-slice_fusion.8.refs_1_.refs_7_), channel_id=1, source_target_pairs={{0,24},{1,97},{2,26},{3,99},{4,28},{5,101},{6,30},{7,103},{8,0},{9... | collective-permute-start | bytes 4227080 | tf_op jit(solution)/shard_map/ppermute | solution.py:62
  162.9 46.1 %collective-permute-start.27 = (bf16[128,5504]{1,0:T(8,128)(2,1)}, bf16[128,5504]{1,0:T(8,128)(2,1)S(1)}, u32[]{:S(2)}, u32[]{:S(2)}) collective-permute-start(bf16[128,5504]{1,0:T(8,128)(2,1)} %collective-permute-done.26.refs_2_.refs_8_), channel_id=1, source_target_pairs={{0,24},{1,97},{2,26},{3,99},{4,28},{5,101},{6,30},{7,103},{8,0},{9... | collective-permute-start | bytes 4227080 | tf_op jit(solution)/shard_map/ppermute | solution.py:62
  176.1 32.9 %collective-permute-start.33 = (bf16[128,5504]{1,0:T(8,128)(2,1)}, bf16[128,5504]{1,0:T(8,128)(2,1)}, u32[]{:S(2)}, u32[]{:S(2)}) collective-permute-start(bf16[128,5504]{1,0:T(8,128)(2,1)} %collective-permute-done.32.refs_5_.refs_11_), channel_id=1, source_target_pairs={{0,8},{1,33},{2,10},{3,35},{4,12},{5,37},{6,14},{7,39},{8,16},{9,4... | collective-permute-start | bytes 4227080 | tf_op jit(solution)/shard_map/ppermute | solution.py:62
  218.6 14.5 %collective-permute-start.40 = (bf16[256,3584]{1,0:T(8,128)(2,1)S(1)}, bf16[256,3584]{1,0:T(8,128)(2,1)S(1)}, u32[]{:S(2)}, u32[]{:S(2)}) collective-permute-start(bf16[256,3584]{1,0:T(8,128)(2,1)S(1)} %get-tuple-element.108), channel_id=1, source_target_pairs={{0,1},{1,0},{2,3},{3,2},{4,5},{5,4},{6,7},{7,6},{8,9},{9,8},{10,11... | collective-permute-start | bytes 5505032 | tf_op jit(solution)/shard_map/ppermute | solution.py:62
  225.8 9.3 %collective-permute-start.37 = (bf16[128,512]{1,0:T(8,128)(2,1)S(1)}, bf16[128,512]{1,0:T(8,128)(2,1)S(1)}, u32[]{:S(2)}, u32[]{:S(2)}) collective-permute-start(bf16[128,512]{1,0:T(8,128)(2,1)S(1)} %get-tuple-element.104), channel_id=1, source_target_pairs={{0,2},{1,3},{2,4},{3,5},{4,6},{5,7},{6,0},{7,1},{8,10},{9,11},{10,... | collective-permute-start | bytes 393224 | tf_op jit(solution)/shard_map/ppermute | solution.py:62
  226.2 8.9 %collective-permute-start.38 = (bf16[128,512]{1,0:T(8,128)(2,1)S(1)}, bf16[128,512]{1,0:T(8,128)(2,1)S(1)}, u32[]{:S(2)}, u32[]{:S(2)}) collective-permute-start(bf16[128,512]{1,0:T(8,128)(2,1)S(1)} %get-tuple-element.105), channel_id=1, source_target_pairs={{0,4},{1,5},{2,6},{3,7},{4,0},{5,1},{6,2},{7,3},{8,12},{9,13},{10,... | collective-permute-start | bytes 393224 | tf_op jit(solution)/shard_map/ppermute | solution.py:62
  (41 other events, 312.9 us)

commit v4 on v3

--- a/solution.py
+++ b/solution.py
@@ -211,7 +211,7 @@
                 pl.BlockSpec((depth, tile), lambda i: (0, jnp.maximum(i - 2, 0))),
             ],
         ),
-        compiler_params=params(24),
+        compiler_params=params(54),
         name="near_products",
     )(*pieces, *pieces, turned_inputs, u_all, head, turned_weight)
 

time: 237 us -> 234 us (0.987)
  other arithmetic: 12.8 us -> 8.22 us
  local copies, waits for them, and re-layouts: 25.2 us -> 22.1 us
  waiting for transfers between devices: 80.5 us -> 83.5 us
    pallas_call x1, Pallas kernels: 12.7 us -> 16.7 us  [near_products(): pl.pallas_call(near_kernel, out_shape=[jax.ShapeDtypeStruct((2 * tile, de...]
    unnamed x65 -> x59, local copies, waits for them, and re-layouts: 19.6 us -> 16.6 us
    ppermute x41, waiting for transfers between devices: 80.5 us -> 83.5 us  [move(): return lax.ppermute(value, AXES, links)]
  transfers between devices with their start and end apart: 41 -> 41, of which waited for: 22 -> 22; matrix products, arithmetic and copies ran while one was open for 7% -> 7% of each run, Pallas kernels for 14% -> 16%
where the time goes in v4:
time: 234 us; the launch traced here: 233 us
  waiting for transfers between devices  83.5 us (36%)
  starting transfers between devices  64 us (27%)
  Pallas kernels  50.6 us (22%)
  local copies, waits for them, and re-layouts  22.1 us (9%)
  other arithmetic  8.22 us (4%)
  between operations  2.44 us (1%)
    ppermute x41, waiting for transfers between devices, move(): return lax.ppermute(value, AXES, links)  83.5 us
    ppermute x41, starting transfers between devices, move(): return lax.ppermute(value, AXES, links)  64 us
    pallas_call x1, Pallas kernels, near_products(): pl.pallas_call(near_kernel, out_shape=[jax.ShapeDtypeStruct((2 * tile, de...  16.7 us
    unnamed x59, local copies, waits for them, and re-layouts  16.6 us
    pallas_call x2, Pallas kernels, project(): pl.pallas_call(kernel, out_shape=[jax.ShapeDtypeStruct((h, 6 * tile + 128...  15.9 us
  transfers between devices with their start and end apart: 41, of which 22 were waited for; matrix products, arithmetic and copies ran while one was open for 7% of the time, Pallas kernels for 16%

profile of v4, /device:TPU:1, one launch (start us, length us, event | category | flops | bytes accessed | tf_op | source)
XLA Modules:
  0.0 233.0 jit_solution(4388405008613318423)
XLA Ops:
  0.7 4.7 %collective-permute-start = (bf16[128,512]{1,0:T(8,128)(2,1)}, bf16[128,512]{1,0:T(8,128)(2,1)S(1)}, u32[]{:S(2)}, u32[]{:S(2)}) collective-permute-start(bf16[128,512]{1,0:T(8,128)(2,1)} %param.8), channel_id=1, source_target_pairs={{0,6},{1,7},{2,0},{3,1},{4,2},{5,3},{6,4},{7,5},{8,14},{9,15},{10,... | collective-permute-start | bytes 393224 | tf_op jit(solution)/shard_map/ppermute | solution.py:62
  19.4 2.7 %collective-permute-start.7 = (bf16[512,512]{1,0:T(8,128)(2,1)S(1)}, bf16[512,512]{1,0:T(8,128)(2,1)S(1)}, u32[]{:S(2)}, u32[]{:S(2)}) collective-permute-start(bf16[512,512]{1,0:T(8,128)(2,1)S(1)} %constant_dynamic-update-slice_fusion.4), channel_id=1, source_target_pairs={{0,1},{1,0},{2,3},{3,2},{4,5},{5,4},{6,7},{7,6},{8,9},{9,8},{10,11... | collective-permute-start | bytes 1572872 | tf_op jit(solution)/shard_map/ppermute | solution.py:62
  29.1 4.8 %project_far.1 = (bf16[128,5504]{1,0:T(8,128)(2,1)S(1)}, bf16[128,5504]{1,0:T(8,128)(2,1)S(1)}) custom-call(s32[1]{0:T(128)} %bitcast.core_ref.core, bf16[1024,512]{1,0:T(8,128)(2,1)S(1)} %bitcast.38, bf16[1024,512]{1,0:T(8,128)(2,1)S(1)} %bitcast.34, bf16[512,3584]{1,0:T(8,128)(2,1)S(1)} %copy-done, bf16[512,3584]{1,0:T(8,128)(2,1)S(1)} %copy-done.2, ...), custom_call_target="tpu_custom_call" | custom-call | tf_op jit(solution)/shard_map/project_far/pallas_call | solution.py:118
  37.0 11.1 %project_rest.1 = (bf16[128,5504]{1,0:T(8,128)(2,1)S(1)}, bf16[128,5504]{1,0:T(8,128)(2,1)S(1)}, f32[128,5504]{1,0:T(8,128)S(1)}, f32[128,5504]{1,0:T(8,128)S(1)...) custom-call(s32[1]{0:T(128)} %bitcast.core_ref.core, bf16[1024,512]{1,0:T(8,128)(2,1)S(1)} %bitcast.39, ...), custom_call_target="tpu_custom_call" | custom-call | tf_op jit(solution)/shard_map/project_rest/pallas_call | solution.py:118
  48.1 5.0 %collective-permute-done.8.arrived_ref = bf16[128,5504]{1,0:T(8,128)(2,1)S(1)} collective-permute-done((bf16[128,5504]{1,0:T(8,128)(2,1)S(1)}, bf16[128,5504]{1,0:T(8,128)(2,1)S(1)}, u32[]{:S(2)}, u32[]{:S(2)}) %collective-permute-start.8) | collective-permute-done | bytes 1409056 | tf_op jit(solution)/shard_map/ppermute | solution.py:62
  60.1 29.4 %collective-permute-done.10 = bf16[256,5504]{1,0:T(8,128)(2,1)S(1)} collective-permute-done((bf16[256,5504]{1,0:T(8,128)(2,1)S(1)}, bf16[256,5504]{1,0:T(8,128)(2,1)S(1)}, u32[]{:S(2)}, u32[]{:S(2)}) %collective-permute-start.10) | collective-permute-done | bytes 2818080 | tf_op jit(solution)/shard_map/ppermute | solution.py:62
  95.3 4.7 %collective-permute-done.12 = bf16[32,5504]{1,0:T(8,128)(2,1)S(1)} collective-permute-done((bf16[32,5504]{1,0:T(8,128)(2,1)S(1)}, bf16[32,5504]{1,0:T(8,128)(2,1)S(1)}, u32[]{:S(2)}, u32[]{:S(2)}) %collective-permute-start.12) | collective-permute-done | bytes 352288 | tf_op jit(solution)/shard_map/ppermute | solution.py:62
  105.7 3.2 %collective-permute-done.17 = s32[2,128]{1,0:T(2,128)S(1)} collective-permute-done((s32[2,128]{1,0:T(2,128)S(1)}, s32[2,128]{1,0:T(2,128)S(1)}, u32[]{:S(2)}, u32[]{:S(2)}) %collective-permute-start.17) | collective-permute-done | bytes 1056 | tf_op jit(solution)/shard_map/ppermute | solution.py:62
  108.9 5.8 %collective-permute-start.19 = (s32[2,512]{1,0:T(2,128)S(1)}, s32[2,512]{1,0:T(2,128)S(1)}, u32[]{:S(2)}, u32[]{:S(2)}) collective-permute-start(s32[2,512]{1,0:T(2,128)S(1)} %pad_add_fusion), channel_id=1, source_target_pairs={{0,1},{1,0},{2,3},{3,2},{4,5},{5,4},{6,7},{7,6},{8,9},{9,8},{10,11... | collective-permute-start | bytes 12296 | tf_op jit(solution)/shard_map/ppermute | solution.py:62
  121.8 3.9 %collective-permute-start.23 = (f32[64]{0:T(128)S(1)}, f32[64]{0:T(128)S(1)}, u32[]{:S(2)}, u32[]{:S(2)}) collective-permute-start(f32[64]{0:T(128)S(1)} %add_add_fusion), channel_id=1, source_target_pairs={{0,1},{1,0},{2,3},{3,2},{4,5},{5,4},{6,7},{7,6},{8,9},{9,8},{10,11... | collective-permute-start | bytes 776 | tf_op jit(solution)/shard_map/ppermute | solution.py:62
  127.1 2.7 %collective-permute-start.24 = (bf16[32,5504]{1,0:T(8,128)(2,1)S(1)}, bf16[32,5504]{1,0:T(8,128)(2,1)S(1)}, u32[]{:S(2)}, u32[]{:S(2)}) collective-permute-start(bf16[32,5504]{1,0:T(8,128)(2,1)S(1)} %get-tuple-element.138), channel_id=1, source_target_pairs={{0,96},{1,25},{2,98},{3,27},{4,100},{5,29},{6,102},{7,31},{8,104},... | collective-permute-start | bytes 1056776 | tf_op jit(solution)/shard_map/ppermute | solution.py:62
  131.3 2.8 %collective-permute-done.24 = bf16[32,5504]{1,0:T(8,128)(2,1)S(1)} collective-permute-done((bf16[32,5504]{1,0:T(8,128)(2,1)S(1)}, bf16[32,5504]{1,0:T(8,128)(2,1)S(1)}, u32[]{:S(2)}, u32[]{:S(2)}) %collective-permute-start.24) | collective-permute-done | bytes 352288 | tf_op jit(solution)/shard_map/ppermute | solution.py:62
  134.1 3.1 %collective-permute-start.28 = (bf16[32,5504]{1,0:T(8,128)(2,1)S(1)}, bf16[32,5504]{1,0:T(8,128)(2,1)S(1)}, u32[]{:S(2)}, u32[]{:S(2)}) collective-permute-start(bf16[32,5504]{1,0:T(8,128)(2,1)S(1)} %collective-permute-done.24), channel_id=1, source_target_pairs={{0,96},{1,25},{2,98},{3,27},{4,100},{5,29},{6,102},{7,31},{8,104},... | collective-permute-start | bytes 1056776 | tf_op jit(solution)/shard_map/ppermute | solution.py:62
  142.9 7.2 %collective-permute-done.30 = bf16[32,5504]{1,0:T(8,128)(2,1)S(1)} collective-permute-done((bf16[32,5504]{1,0:T(8,128)(2,1)S(1)}, bf16[32,5504]{1,0:T(8,128)(2,1)S(1)}, u32[]{:S(2)}, u32[]{:S(2)}) %collective-permute-start.30) | collective-permute-done | bytes 352288 | tf_op jit(solution)/shard_map/ppermute | solution.py:62
  152.4 2.7 %collective-permute-start.34 = (bf16[128,5504]{1,0:T(8,128)(2,1)}, bf16[128,5504]{1,0:T(8,128)(2,1)}, u32[]{:S(2)}, u32[]{:S(2)}) collective-permute-start(bf16[128,5504]{1,0:T(8,128)(2,1)} %constant_dynamic-update-slice_fusion.8.refs_1_.refs_7_), channel_id=1, source_target_pairs={{0,24},{1,97},{2,26},{3,99},{4,28},{5,101},{6,30},{7,103},{8,0},{9... | collective-permute-start | bytes 4227080 | tf_op jit(solution)/shard_map/ppermute | solution.py:62
  155.1 3.4 %collective-permute-done.26.refs_2_.refs_8_ = bf16[128,5504]{1,0:T(8,128)(2,1)} collective-permute-done((bf16[128,5504]{1,0:T(8,128)(2,1)}, bf16[128,5504]{1,0:T(8,128)(2,1)}, u32[]{:S(2)}, u32[]{:S(2)}) %collective-permute-start.26) | collective-permute-done | bytes 1409056 | tf_op jit(solution)/shard_map/ppermute | solution.py:62
  158.6 3.4 %collective-permute-start.27 = (bf16[128,5504]{1,0:T(8,128)(2,1)}, bf16[128,5504]{1,0:T(8,128)(2,1)S(1)}, u32[]{:S(2)}, u32[]{:S(2)}) collective-permute-start(bf16[128,5504]{1,0:T(8,128)(2,1)} %collective-permute-done.26.refs_2_.refs_8_), channel_id=1, source_target_pairs={{0,24},{1,97},{2,26},{3,99},{4,28},{5,101},{6,30},{7,103},{8,0},{9... | collective-permute-start | bytes 4227080 | tf_op jit(solution)/shard_map/ppermute | solution.py:62
  162.0 9.8 %collective-permute-done.32.refs_5_.refs_11_ = bf16[128,5504]{1,0:T(8,128)(2,1)} collective-permute-done((bf16[128,5504]{1,0:T(8,128)(2,1)}, bf16[128,5504]{1,0:T(8,128)(2,1)}, u32[]{:S(2)}, u32[]{:S(2)}) %collective-permute-start.32) | collective-permute-done | bytes 1409056 | tf_op jit(solution)/shard_map/ppermute | solution.py:62
  182.2 4.7 %collective-permute-done.35.refs_4_.refs_10_ = bf16[128,5504]{1,0:T(8,128)(2,1)} collective-permute-done((bf16[128,5504]{1,0:T(8,128)(2,1)}, bf16[128,5504]{1,0:T(8,128)(2,1)}, u32[]{:S(2)}, u32[]{:S(2)}) %collective-permute-start.35) | collective-permute-done | bytes 1409056 | tf_op jit(solution)/shard_map/ppermute | solution.py:62
  186.9 16.7 %near_products.1 = (f32[1792,512]{1,0:T(8,128)}, f32[768,512]{1,0:T(8,128)}, f32[512,3584]{1,0:T(8,128)}) custom-call(bf16[128,5504]{1,0:T(8,128)(2,1)} %pad_maximum_fusion.refs_0_.refs_6_, bf16[128,5504]{1,0:T(8,128)(2,1)} %constant_dynamic-update-slice_fusion.8.refs_1_.refs_7_, bf16[128,5504]{1,0:T(8,128)(2,1)} %collective-permute-done.26.refs_2_.refs_8_, ...), custom_call_target="tpu_custom_call" | custom-call | tf_op jit(solution)/shard_map/near_products/pallas_call | solution.py:191
  205.0 3.1 %input_product.1 = (f32[512,512]{1,0:T(8,128)S(1)}, bf16[512,512]{1,0:T(8,128)(2,1)S(1)}) custom-call(s32[16]{0:T(128)S(1)} %broadcast_select_fusion.source, bf16[128,5504]{1,0:T(8,128)(2,1)S(1)} %collective-permute-done.27.top.slope_top, bf16[128,5504]{1,0:T(8,128)(2,1)S(1)} %collective-permute-done.33.bottom.slope_bottom, bf16[3584,512]{1,0:T(8,128)(2,1)S(1)} %copy-done.5, ...), custom_call_target="tpu_custom_call" | custom-call | tf_op jit(solution)/shard_map/input_product/pallas_call | solution.py:311
  208.2 3.1 %copy-done.11 = f32[512,3584]{1,0:T(8,128)S(1)} copy-done((f32[512,3584]{1,0:T(8,128)S(1)}, f32[512,3584]{1,0:T(8,128)}, u32[]{:S(2)}) %copy-start.11) | copy-done | bytes 7340056
  211.2 4.6 %weight_product.1 = (f32[256,3584]{1,0:T(8,128)}, f32[256,3584]{1,0:T(8,128)}, bf16[256,3584]{1,0:T(8,128)(2,1)S(1)}) custom-call(s32[1]{0:T(128)} %bitcast.core_ref.core, bf16[128,5504]{1,0:T(8,128)(2,1)S(1)} %collective-permute-done.27.top.slope_top, bf16[128,5504]{1,0:T(8,128)(2,1)S(1)} %collective-permute-done.33.bottom.slope_bottom, ...), custom_call_target="tpu_custom_call" | custom-call | tf_op jit(solution)/shard_map/weight_product/pallas_call | solution.py:356
  215.8 2.9 %collective-permute-start.40 = (bf16[256,3584]{1,0:T(8,128)(2,1)S(1)}, bf16[256,3584]{1,0:T(8,128)(2,1)S(1)}, u32[]{:S(2)}, u32[]{:S(2)}) collective-permute-start(bf16[256,3584]{1,0:T(8,128)(2,1)S(1)} %get-tuple-element.108), channel_id=1, source_target_pairs={{0,1},{1,0},{2,3},{3,2},{4,5},{5,4},{6,7},{7,6},{8,9},{9,8},{10,11... | collective-permute-start | bytes 5505032 | tf_op jit(solution)/shard_map/ppermute | solution.py:62
  (186 shorter events, 85.2 us)
Async XLA Ops:
  0.7 11.9 %collective-permute-start = (bf16[128,512]{1,0:T(8,128)(2,1)}, bf16[128,512]{1,0:T(8,128)(2,1)S(1)}, u32[]{:S(2)}, u32[]{:S(2)}) collective-permute-start(bf16[128,512]{1,0:T(8,128)(2,1)} %param.8), channel_id=1, source_target_pairs={{0,6},{1,7},{2,0},{3,1},{4,2},{5,3},{6,4},{7,5},{8,14},{9,15},{10,... | collective-permute-start | bytes 393224 | tf_op jit(solution)/shard_map/ppermute | solution.py:62
  5.3 10.0 %collective-permute-start.2 = (bf16[128,512]{1,0:T(8,128)(2,1)}, bf16[128,512]{1,0:T(8,128)(2,1)S(1)}, u32[]{:S(2)}, u32[]{:S(2)}) collective-permute-start(bf16[128,512]{1,0:T(8,128)(2,1)} %param.8), channel_id=1, source_target_pairs={{0,2},{1,3},{2,4},{3,5},{4,6},{5,7},{6,0},{7,1},{8,10},{9,11},{10,... | collective-permute-start | bytes 393224 | tf_op jit(solution)/shard_map/ppermute | solution.py:62
  6.0 10.8 %collective-permute-start.4 = (bf16[128,512]{1,0:T(8,128)(2,1)}, bf16[128,512]{1,0:T(8,128)(2,1)S(1)}, u32[]{:S(2)}, u32[]{:S(2)}) collective-permute-start(bf16[128,512]{1,0:T(8,128)(2,1)} %param.13), channel_id=1, source_target_pairs={{0,6},{1,7},{2,0},{3,1},{4,2},{5,3},{6,4},{7,5},{8,14},{9,15},{10,... | collective-permute-start | bytes 393224 | tf_op jit(solution)/shard_map/ppermute | solution.py:62
  8.0 8.9 %collective-permute-start.5 = (bf16[128,512]{1,0:T(8,128)(2,1)}, bf16[128,512]{1,0:T(8,128)(2,1)S(1)}, u32[]{:S(2)}, u32[]{:S(2)}) collective-permute-start(bf16[128,512]{1,0:T(8,128)(2,1)} %param.13), channel_id=1, source_target_pairs={{0,4},{1,5},{2,6},{3,7},{4,0},{5,1},{6,2},{7,3},{8,12},{9,13},{10,... | collective-permute-start | bytes 393224 | tf_op jit(solution)/shard_map/ppermute | solution.py:62
  33.9 19.1 %collective-permute-start.8 = (bf16[128,5504]{1,0:T(8,128)(2,1)S(1)}, bf16[128,5504]{1,0:T(8,128)(2,1)S(1)}, u32[]{:S(2)}, u32[]{:S(2)}) collective-permute-start(bf16[128,5504]{1,0:T(8,128)(2,1)S(1)} %get-tuple-element.67), channel_id=1, source_target_pairs={{0,8},{1,33},{2,10},{3,35},{4,12},{5,37},{6,14},{7,39},{8,16},{9,4... | collective-permute-start | bytes 4227080 | tf_op jit(solution)/shard_map/ppermute | solution.py:62
  35.3 17.8 %collective-permute-start.9 = (bf16[128,5504]{1,0:T(8,128)(2,1)S(1)}, bf16[128,5504]{1,0:T(8,128)(2,1)S(1)}, u32[]{:S(2)}, u32[]{:S(2)}) collective-permute-start(bf16[128,5504]{1,0:T(8,128)(2,1)S(1)} %get-tuple-element.68), channel_id=1, source_target_pairs={{0,24},{1,97},{2,26},{3,99},{4,28},{5,101},{6,30},{7,103},{8,0},{9... | collective-permute-start | bytes 4227080 | tf_op jit(solution)/shard_map/ppermute | solution.py:62
  55.1 34.4 %collective-permute-start.10 = (bf16[256,5504]{1,0:T(8,128)(2,1)S(1)}, bf16[256,5504]{1,0:T(8,128)(2,1)S(1)}, u32[]{:S(2)}, u32[]{:S(2)}) collective-permute-start(bf16[256,5504]{1,0:T(8,128)(2,1)S(1)} %add_halves.2), channel_id=1, source_target_pairs={{0,8},{1,33},{2,10},{3,35},{4,12},{5,37},{6,14},{7,39},{8,16},{9,4... | collective-permute-start | bytes 8454152 | tf_op jit(solution)/shard_map/ppermute | solution.py:62
  58.4 33.0 %collective-permute-start.11 = (bf16[256,5504]{1,0:T(8,128)(2,1)S(1)}, bf16[256,5504]{1,0:T(8,128)(2,1)S(1)}, u32[]{:S(2)}, u32[]{:S(2)}) collective-permute-start(bf16[256,5504]{1,0:T(8,128)(2,1)S(1)} %add_halves.3), channel_id=1, source_target_pairs={{0,24},{1,97},{2,26},{3,99},{4,28},{5,101},{6,30},{7,103},{8,0},{9... | collective-permute-start | bytes 8454152 | tf_op jit(solution)/shard_map/ppermute | solution.py:62
  100.2 15.3 %collective-permute-start.14 = (bf16[64,5504]{1,0:T(8,128)(2,1)S(1)}, bf16[64,5504]{1,0:T(8,128)(2,1)S(1)}, u32[]{:S(2)}, u32[]{:S(2)}) collective-permute-start(bf16[64,5504]{1,0:T(8,128)(2,1)S(1)} %pad_maximum_fusion.1), channel_id=1, source_target_pairs={{0,32},{1,9},{2,34},{3,11},{4,36},{5,13},{6,38},{7,15},{8,40},{9,1... | collective-permute-start | bytes 2113544 | tf_op jit(solution)/shard_map/ppermute | solution.py:62
  101.6 14.0 %collective-permute-start.15 = (bf16[64,5504]{1,0:T(8,128)(2,1)S(1)}, bf16[64,5504]{1,0:T(8,128)(2,1)}, u32[]{:S(2)}, u32[]{:S(2)}) collective-permute-start(bf16[64,5504]{1,0:T(8,128)(2,1)S(1)} %pad_maximum_fusion.2), channel_id=1, source_target_pairs={{0,96},{1,25},{2,98},{3,27},{4,100},{5,29},{6,102},{7,31},{8,104},... | collective-permute-start | bytes 2113544 | tf_op jit(solution)/shard_map/ppermute | solution.py:62
  129.8 8.1 %collective-permute-start.25 = (bf16[32,5504]{1,0:T(8,128)(2,1)S(1)}, bf16[32,5504]{1,0:T(8,128)(2,1)S(1)}, u32[]{:S(2)}, u32[]{:S(2)}) collective-permute-start(bf16[32,5504]{1,0:T(8,128)(2,1)S(1)} %get-tuple-element.139), channel_id=1, source_target_pairs={{0,96},{1,25},{2,98},{3,27},{4,100},{5,29},{6,102},{7,31},{8,104},... | collective-permute-start | bytes 1056776 | tf_op jit(solution)/shard_map/ppermute | solution.py:62
  130.1 11.6 %collective-permute-start.29 = (bf16[32,5504]{1,0:T(8,128)(2,1)S(1)}, bf16[32,5504]{1,0:T(8,128)(2,1)S(1)}, u32[]{:S(2)}, u32[]{:S(2)}) collective-permute-start(bf16[32,5504]{1,0:T(8,128)(2,1)S(1)} %get-tuple-element.139), channel_id=1, source_target_pairs={{0,32},{1,9},{2,34},{3,11},{4,36},{5,13},{6,38},{7,15},{8,40},{9,1... | collective-permute-start | bytes 1056776 | tf_op jit(solution)/shard_map/ppermute | solution.py:62
  131.3 19.6 %collective-permute-start.31 = (bf16[32,5504]{1,0:T(8,128)(2,1)S(1)}, bf16[32,5504]{1,0:T(8,128)(2,1)S(1)}, u32[]{:S(2)}, u32[]{:S(2)}) collective-permute-start(bf16[32,5504]{1,0:T(8,128)(2,1)S(1)} %get-tuple-element.138), channel_id=1, source_target_pairs={{0,32},{1,9},{2,34},{3,11},{4,36},{5,13},{6,38},{7,15},{8,40},{9,1... | collective-permute-start | bytes 1056776 | tf_op jit(solution)/shard_map/ppermute | solution.py:62
  134.1 8.0 %collective-permute-start.28 = (bf16[32,5504]{1,0:T(8,128)(2,1)S(1)}, bf16[32,5504]{1,0:T(8,128)(2,1)S(1)}, u32[]{:S(2)}, u32[]{:S(2)}) collective-permute-start(bf16[32,5504]{1,0:T(8,128)(2,1)S(1)} %collective-permute-done.24), channel_id=1, source_target_pairs={{0,96},{1,25},{2,98},{3,27},{4,100},{5,29},{6,102},{7,31},{8,104},... | collective-permute-start | bytes 1056776 | tf_op jit(solution)/shard_map/ppermute | solution.py:62
  139.1 19.5 %collective-permute-start.26 = (bf16[128,5504]{1,0:T(8,128)(2,1)}, bf16[128,5504]{1,0:T(8,128)(2,1)}, u32[]{:S(2)}, u32[]{:S(2)}) collective-permute-start(bf16[128,5504]{1,0:T(8,128)(2,1)} %pad_maximum_fusion.refs_0_.refs_6_), channel_id=1, source_target_pairs={{0,24},{1,97},{2,26},{3,99},{4,28},{5,101},{6,30},{7,103},{8,0},{9... | collective-permute-start | bytes 4227080 | tf_op jit(solution)/shard_map/ppermute | solution.py:62
  141.7 8.4 %collective-permute-start.30 = (bf16[32,5504]{1,0:T(8,128)(2,1)S(1)}, bf16[32,5504]{1,0:T(8,128)(2,1)S(1)}, u32[]{:S(2)}, u32[]{:S(2)}) collective-permute-start(bf16[32,5504]{1,0:T(8,128)(2,1)S(1)} %collective-permute-done.29), channel_id=1, source_target_pairs={{0,32},{1,9},{2,34},{3,11},{4,36},{5,13},{6,38},{7,15},{8,40},{9,1... | collective-permute-start | bytes 1056776 | tf_op jit(solution)/shard_map/ppermute | solution.py:62
  152.4 19.3 %collective-permute-start.32 = (bf16[128,5504]{1,0:T(8,128)(2,1)}, bf16[128,5504]{1,0:T(8,128)(2,1)}, u32[]{:S(2)}, u32[]{:S(2)}) collective-permute-start(bf16[128,5504]{1,0:T(8,128)(2,1)} %constant_dynamic-update-slice_fusion.8.refs_1_.refs_7_), channel_id=1, source_target_pairs={{0,8},{1,33},{2,10},{3,35},{4,12},{5,37},{6,14},{7,39},{8,16},{9,4... | collective-permute-start | bytes 4227080 | tf_op jit(solution)/shard_map/ppermute | solution.py:62
  152.4 34.4 %collective-permute-start.35 = (bf16[128,5504]{1,0:T(8,128)(2,1)}, bf16[128,5504]{1,0:T(8,128)(2,1)}, u32[]{:S(2)}, u32[]{:S(2)}) collective-permute-start(bf16[128,5504]{1,0:T(8,128)(2,1)} %pad_maximum_fusion.refs_0_.refs_6_), channel_id=1, source_target_pairs={{0,8},{1,33},{2,10},{3,35},{4,12},{5,37},{6,14},{7,39},{8,16},{9,4... | collective-permute-start | bytes 4227080 | tf_op jit(solution)/shard_map/ppermute | solution.py:62
  152.4 34.4 %collective-permute-start.34 = (bf16[128,5504]{1,0:T(8,128)(2,1)}, bf16[128,5504]{1,0:T(8,128)(2,1)}, u32[]{:S(2)}, u32[]{:S(2)}) collective-permute-start(bf16[128,5504]{1,0:T(8,128)(2,1)} %constant_dynamic-update-slice_fusion.8.refs_1_.refs_7_), channel_id=1, source_target_pairs={{0,24},{1,97},{2,26},{3,99},{4,28},{5,101},{6,30},{7,103},{8,0},{9... | collective-permute-start | bytes 4227080 | tf_op jit(solution)/shard_map/ppermute | solution.py:62
  158.6 45.0 %collective-permute-start.27 = (bf16[128,5504]{1,0:T(8,128)(2,1)}, bf16[128,5504]{1,0:T(8,128)(2,1)S(1)}, u32[]{:S(2)}, u32[]{:S(2)}) collective-permute-start(bf16[128,5504]{1,0:T(8,128)(2,1)} %collective-permute-done.26.refs_2_.refs_8_), channel_id=1, source_target_pairs={{0,24},{1,97},{2,26},{3,99},{4,28},{5,101},{6,30},{7,103},{8,0},{9... | collective-permute-start | bytes 4227080 | tf_op jit(solution)/shard_map/ppermute | solution.py:62
  171.8 31.8 %collective-permute-start.33 = (bf16[128,5504]{1,0:T(8,128)(2,1)}, bf16[128,5504]{1,0:T(8,128)(2,1)S(1)}, u32[]{:S(2)}, u32[]{:S(2)}) collective-permute-start(bf16[128,5504]{1,0:T(8,128)(2,1)} %collective-permute-done.32.refs_5_.refs_11_), channel_id=1, source_target_pairs={{0,8},{1,33},{2,10},{3,35},{4,12},{5,37},{6,14},{7,39},{8,16},{9,4... | collective-permute-start | bytes 4227080 | tf_op jit(solution)/shard_map/ppermute | solution.py:62
  215.8 13.8 %collective-permute-start.40 = (bf16[256,3584]{1,0:T(8,128)(2,1)S(1)}, bf16[256,3584]{1,0:T(8,128)(2,1)S(1)}, u32[]{:S(2)}, u32[]{:S(2)}) collective-permute-start(bf16[256,3584]{1,0:T(8,128)(2,1)S(1)} %get-tuple-element.108), channel_id=1, source_target_pairs={{0,1},{1,0},{2,3},{3,2},{4,5},{5,4},{6,7},{7,6},{8,9},{9,8},{10,11... | collective-permute-start | bytes 5505032 | tf_op jit(solution)/shard_map/ppermute | solution.py:62
  223.1 8.6 %collective-permute-start.37 = (bf16[128,512]{1,0:T(8,128)(2,1)S(1)}, bf16[128,512]{1,0:T(8,128)(2,1)S(1)}, u32[]{:S(2)}, u32[]{:S(2)}) collective-permute-start(bf16[128,512]{1,0:T(8,128)(2,1)S(1)} %get-tuple-element.104), channel_id=1, source_target_pairs={{0,2},{1,3},{2,4},{3,5},{4,6},{5,7},{6,0},{7,1},{8,10},{9,11},{10,... | collective-permute-start | bytes 393224 | tf_op jit(solution)/shard_map/ppermute | solution.py:62
  223.5 8.2 %collective-permute-start.38 = (bf16[128,512]{1,0:T(8,128)(2,1)S(1)}, bf16[128,512]{1,0:T(8,128)(2,1)S(1)}, u32[]{:S(2)}, u32[]{:S(2)}) collective-permute-start(bf16[128,512]{1,0:T(8,128)(2,1)S(1)} %get-tuple-element.105), channel_id=1, source_target_pairs={{0,4},{1,5},{2,6},{3,7},{4,0},{5,1},{6,2},{7,3},{8,12},{9,13},{10,... | collective-permute-start | bytes 393224 | tf_op jit(solution)/shard_map/ppermute | solution.py:62
  (38 other events, 298.5 us)

commit v5 on v4

--- a/solution.py
+++ b/solution.py
@@ -325,7 +325,7 @@
             out_specs=[pl.BlockSpec((4 * h, depth), lambda i, s: (0, 0))] * 2,
             scratch_shapes=[pltpu.VMEM((8 * h, depth), F32)],
         ),
-        compiler_params=params(24),
+        compiler_params=params(54),
         name="input_product",
     )(source, top, bottom, turned_weight, near)
 
@@ -374,7 +374,7 @@
                 pl.BlockSpec((rows, tile), lambda i, s: (0, i)),
             ],
         ),
-        compiler_params=params(24),
+        compiler_params=params(54),
         name="weight_product",
     )(core[None], top, bottom, turned_inputs, near)
 

time: 234 us -> 239 us (1.021)
  Pallas kernels: 50.6 us -> 58.3 us
  local copies, waits for them, and re-layouts: 22.1 us -> 19.1 us
    pallas_call x1, Pallas kernels: 4.59 us -> 8.62 us  [weight_product(): pl.pallas_call(weight_kernel, out_shape=[jax.ShapeDtypeStruct((rows, widt...]
    pallas_call x1, Pallas kernels: 3.12 us -> 6.89 us  [input_product(): pl.pallas_call(input_kernel, out_shape=[jax.ShapeDtypeStruct((4 * h, dept...]
    unnamed x59 -> x65, local copies, waits for them, and re-layouts: 16.6 us -> 13.6 us
  transfers between devices with their start and end apart: 41 -> 41, of which waited for: 22 -> 22; matrix products, arithmetic and copies ran while one was open for 7% -> 7% of each run, Pallas kernels for 16% -> 15%
where the time goes in v5:
time: 239 us; the launch traced here: 238 us
  waiting for transfers between devices  83.4 us (35%)
  starting transfers between devices  64 us (27%)
  Pallas kernels  58.3 us (24%)
  local copies, waits for them, and re-layouts  19.1 us (8%)
  other arithmetic  8.21 us (3%)
  between operations  2.49 us (1%)
    ppermute x41, waiting for transfers between devices, move(): return lax.ppermute(value, AXES, links)  83.4 us
    ppermute x41, starting transfers between devices, move(): return lax.ppermute(value, AXES, links)  64 us
    pallas_call x1, Pallas kernels, near_products(): pl.pallas_call(near_kernel, out_shape=[jax.ShapeDtypeStruct((2 * tile, de...  16.5 us
    pallas_call x2, Pallas kernels, project(): pl.pallas_call(kernel, out_shape=[jax.ShapeDtypeStruct((h, 6 * tile + 128...  15.9 us
    unnamed x65, local copies, waits for them, and re-layouts  13.6 us
    pallas_call x1, Pallas kernels, weight_product(): pl.pallas_call(weight_kernel, out_shape=[jax.ShapeDtypeStruct((rows, widt...  8.62 us
    pallas_call x1, Pallas kernels, input_product(): pl.pallas_call(input_kernel, out_shape=[jax.ShapeDtypeStruct((4 * h, dept...  6.89 us
  transfers between devices with their start and end apart: 41, of which 22 were waited for; matrix products, arithmetic and copies ran while one was open for 7% of the time, Pallas kernels for 15%

profile of v5, /device:TPU:1, one launch (start us, length us, event | category | flops | bytes accessed | tf_op | source)
XLA Modules:
  0.0 237.6 jit_solution(12949373379892283113)
XLA Ops:
  0.7 4.7 %collective-permute-start = (bf16[128,512]{1,0:T(8,128)(2,1)}, bf16[128,512]{1,0:T(8,128)(2,1)S(1)}, u32[]{:S(2)}, u32[]{:S(2)}) collective-permute-start(bf16[128,512]{1,0:T(8,128)(2,1)} %param.8), channel_id=1, source_target_pairs={{0,6},{1,7},{2,0},{3,1},{4,2},{5,3},{6,4},{7,5},{8,14},{9,15},{10,... | collective-permute-start | bytes 393224 | tf_op jit(solution)/shard_map/ppermute | solution.py:62
  19.4 2.7 %collective-permute-start.7 = (bf16[512,512]{1,0:T(8,128)(2,1)S(1)}, bf16[512,512]{1,0:T(8,128)(2,1)S(1)}, u32[]{:S(2)}, u32[]{:S(2)}) collective-permute-start(bf16[512,512]{1,0:T(8,128)(2,1)S(1)} %constant_dynamic-update-slice_fusion.4), channel_id=1, source_target_pairs={{0,1},{1,0},{2,3},{3,2},{4,5},{5,4},{6,7},{7,6},{8,9},{9,8},{10,11... | collective-permute-start | bytes 1572872 | tf_op jit(solution)/shard_map/ppermute | solution.py:62
  29.1 4.8 %project_far.1 = (bf16[128,5504]{1,0:T(8,128)(2,1)S(1)}, bf16[128,5504]{1,0:T(8,128)(2,1)S(1)}) custom-call(s32[1]{0:T(128)} %bitcast.core_ref.core, bf16[1024,512]{1,0:T(8,128)(2,1)S(1)} %bitcast.38, bf16[1024,512]{1,0:T(8,128)(2,1)S(1)} %bitcast.34, bf16[512,3584]{1,0:T(8,128)(2,1)S(1)} %copy-done, bf16[512,3584]{1,0:T(8,128)(2,1)S(1)} %copy-done.2, ...), custom_call_target="tpu_custom_call" | custom-call | tf_op jit(solution)/shard_map/project_far/pallas_call | solution.py:118
  37.0 11.1 %project_rest.1 = (bf16[128,5504]{1,0:T(8,128)(2,1)S(1)}, bf16[128,5504]{1,0:T(8,128)(2,1)S(1)}, f32[128,5504]{1,0:T(8,128)S(1)}, f32[128,5504]{1,0:T(8,128)S(1)...) custom-call(s32[1]{0:T(128)} %bitcast.core_ref.core, bf16[1024,512]{1,0:T(8,128)(2,1)S(1)} %bitcast.39, ...), custom_call_target="tpu_custom_call" | custom-call | tf_op jit(solution)/shard_map/project_rest/pallas_call | solution.py:118
  48.1 5.0 %collective-permute-done.8.arrived_ref = bf16[128,5504]{1,0:T(8,128)(2,1)S(1)} collective-permute-done((bf16[128,5504]{1,0:T(8,128)(2,1)S(1)}, bf16[128,5504]{1,0:T(8,128)(2,1)S(1)}, u32[]{:S(2)}, u32[]{:S(2)}) %collective-permute-start.8) | collective-permute-done | bytes 1409056 | tf_op jit(solution)/shard_map/ppermute | solution.py:62
  60.1 29.4 %collective-permute-done.10 = bf16[256,5504]{1,0:T(8,128)(2,1)S(1)} collective-permute-done((bf16[256,5504]{1,0:T(8,128)(2,1)S(1)}, bf16[256,5504]{1,0:T(8,128)(2,1)S(1)}, u32[]{:S(2)}, u32[]{:S(2)}) %collective-permute-start.10) | collective-permute-done | bytes 2818080 | tf_op jit(solution)/shard_map/ppermute | solution.py:62
  95.3 4.7 %collective-permute-done.12 = bf16[32,5504]{1,0:T(8,128)(2,1)S(1)} collective-permute-done((bf16[32,5504]{1,0:T(8,128)(2,1)S(1)}, bf16[32,5504]{1,0:T(8,128)(2,1)S(1)}, u32[]{:S(2)}, u32[]{:S(2)}) %collective-permute-start.12) | collective-permute-done | bytes 352288 | tf_op jit(solution)/shard_map/ppermute | solution.py:62
  105.7 3.2 %collective-permute-done.17 = s32[2,128]{1,0:T(2,128)S(1)} collective-permute-done((s32[2,128]{1,0:T(2,128)S(1)}, s32[2,128]{1,0:T(2,128)S(1)}, u32[]{:S(2)}, u32[]{:S(2)}) %collective-permute-start.17) | collective-permute-done | bytes 1056 | tf_op jit(solution)/shard_map/ppermute | solution.py:62
  108.9 5.8 %collective-permute-start.19 = (s32[2,512]{1,0:T(2,128)S(1)}, s32[2,512]{1,0:T(2,128)S(1)}, u32[]{:S(2)}, u32[]{:S(2)}) collective-permute-start(s32[2,512]{1,0:T(2,128)S(1)} %pad_add_fusion), channel_id=1, source_target_pairs={{0,1},{1,0},{2,3},{3,2},{4,5},{5,4},{6,7},{7,6},{8,9},{9,8},{10,11... | collective-permute-start | bytes 12296 | tf_op jit(solution)/shard_map/ppermute | solution.py:62
  121.8 3.9 %collective-permute-start.23 = (f32[64]{0:T(128)S(1)}, f32[64]{0:T(128)S(1)}, u32[]{:S(2)}, u32[]{:S(2)}) collective-permute-start(f32[64]{0:T(128)S(1)} %add_add_fusion), channel_id=1, source_target_pairs={{0,1},{1,0},{2,3},{3,2},{4,5},{5,4},{6,7},{7,6},{8,9},{9,8},{10,11... | collective-permute-start | bytes 776 | tf_op jit(solution)/shard_map/ppermute | solution.py:62
  127.1 2.7 %collective-permute-start.24 = (bf16[32,5504]{1,0:T(8,128)(2,1)S(1)}, bf16[32,5504]{1,0:T(8,128)(2,1)S(1)}, u32[]{:S(2)}, u32[]{:S(2)}) collective-permute-start(bf16[32,5504]{1,0:T(8,128)(2,1)S(1)} %get-tuple-element.138), channel_id=1, source_target_pairs={{0,96},{1,25},{2,98},{3,27},{4,100},{5,29},{6,102},{7,31},{8,104},... | collective-permute-start | bytes 1056776 | tf_op jit(solution)/shard_map/ppermute | solution.py:62
  131.3 2.8 %collective-permute-done.24 = bf16[32,5504]{1,0:T(8,128)(2,1)S(1)} collective-permute-done((bf16[32,5504]{1,0:T(8,128)(2,1)S(1)}, bf16[32,5504]{1,0:T(8,128)(2,1)S(1)}, u32[]{:S(2)}, u32[]{:S(2)}) %collective-permute-start.24) | collective-permute-done | bytes 352288 | tf_op jit(solution)/shard_map/ppermute | solution.py:62
  134.1 3.1 %collective-permute-start.28 = (bf16[32,5504]{1,0:T(8,128)(2,1)S(1)}, bf16[32,5504]{1,0:T(8,128)(2,1)S(1)}, u32[]{:S(2)}, u32[]{:S(2)}) collective-permute-start(bf16[32,5504]{1,0:T(8,128)(2,1)S(1)} %collective-permute-done.24), channel_id=1, source_target_pairs={{0,96},{1,25},{2,98},{3,27},{4,100},{5,29},{6,102},{7,31},{8,104},... | collective-permute-start | bytes 1056776 | tf_op jit(solution)/shard_map/ppermute | solution.py:62
  142.9 7.2 %collective-permute-done.30 = bf16[32,5504]{1,0:T(8,128)(2,1)S(1)} collective-permute-done((bf16[32,5504]{1,0:T(8,128)(2,1)S(1)}, bf16[32,5504]{1,0:T(8,128)(2,1)S(1)}, u32[]{:S(2)}, u32[]{:S(2)}) %collective-permute-start.30) | collective-permute-done | bytes 352288 | tf_op jit(solution)/shard_map/ppermute | solution.py:62
  152.4 2.7 %collective-permute-start.34 = (bf16[128,5504]{1,0:T(8,128)(2,1)}, bf16[128,5504]{1,0:T(8,128)(2,1)}, u32[]{:S(2)}, u32[]{:S(2)}) collective-permute-start(bf16[128,5504]{1,0:T(8,128)(2,1)} %constant_dynamic-update-slice_fusion.8.refs_1_.refs_7_), channel_id=1, source_target_pairs={{0,24},{1,97},{2,26},{3,99},{4,28},{5,101},{6,30},{7,103},{8,0},{9... | collective-permute-start | bytes 4227080 | tf_op jit(solution)/shard_map/ppermute | solution.py:62
  155.1 3.4 %collective-permute-done.26.refs_2_.refs_8_ = bf16[128,5504]{1,0:T(8,128)(2,1)} collective-permute-done((bf16[128,5504]{1,0:T(8,128)(2,1)}, bf16[128,5504]{1,0:T(8,128)(2,1)}, u32[]{:S(2)}, u32[]{:S(2)}) %collective-permute-start.26) | collective-permute-done | bytes 1409056 | tf_op jit(solution)/shard_map/ppermute | solution.py:62
  158.6 3.4 %collective-permute-start.27 = (bf16[128,5504]{1,0:T(8,128)(2,1)}, bf16[128,5504]{1,0:T(8,128)(2,1)S(1)}, u32[]{:S(2)}, u32[]{:S(2)}) collective-permute-start(bf16[128,5504]{1,0:T(8,128)(2,1)} %collective-permute-done.26.refs_2_.refs_8_), channel_id=1, source_target_pairs={{0,24},{1,97},{2,26},{3,99},{4,28},{5,101},{6,30},{7,103},{8,0},{9... | collective-permute-start | bytes 4227080 | tf_op jit(solution)/shard_map/ppermute | solution.py:62
  162.0 9.8 %collective-permute-done.32.refs_5_.refs_11_ = bf16[128,5504]{1,0:T(8,128)(2,1)} collective-permute-done((bf16[128,5504]{1,0:T(8,128)(2,1)}, bf16[128,5504]{1,0:T(8,128)(2,1)}, u32[]{:S(2)}, u32[]{:S(2)}) %collective-permute-start.32) | collective-permute-done | bytes 1409056 | tf_op jit(solution)/shard_map/ppermute | solution.py:62
  182.2 4.7 %collective-permute-done.35.refs_4_.refs_10_ = bf16[128,5504]{1,0:T(8,128)(2,1)} collective-permute-done((bf16[128,5504]{1,0:T(8,128)(2,1)}, bf16[128,5504]{1,0:T(8,128)(2,1)}, u32[]{:S(2)}, u32[]{:S(2)}) %collective-permute-start.35) | collective-permute-done | bytes 1409056 | tf_op jit(solution)/shard_map/ppermute | solution.py:62
  186.9 16.5 %near_products.1 = (f32[1792,512]{1,0:T(8,128)}, f32[768,512]{1,0:T(8,128)}, f32[512,3584]{1,0:T(8,128)}) custom-call(bf16[128,5504]{1,0:T(8,128)(2,1)} %pad_maximum_fusion.refs_0_.refs_6_, bf16[128,5504]{1,0:T(8,128)(2,1)} %constant_dynamic-update-slice_fusion.8.refs_1_.refs_7_, bf16[128,5504]{1,0:T(8,128)(2,1)} %collective-permute-done.26.refs_2_.refs_8_, ...), custom_call_target="tpu_custom_call" | custom-call | tf_op jit(solution)/shard_map/near_products/pallas_call | solution.py:191
  204.9 6.9 %input_product.1 = (f32[512,512]{1,0:T(8,128)}, bf16[512,512]{1,0:T(8,128)(2,1)}) custom-call(s32[16]{0:T(128)} %copy-done.20, bf16[128,5504]{1,0:T(8,128)(2,1)} %copy-done.8, bf16[128,5504]{1,0:T(8,128)(2,1)} %copy-done.10, bf16[3584,512]{1,0:T(8,128)(2,1)} %copy-done.4, f32[768,512]{1,0:T(8,128)} %get-tuple-element.97.near), custom_call_target="tpu_custom_call" | custom-call | tf_op jit(solution)/shard_map/input_product/pallas_call | solution.py:311
  211.9 8.6 %weight_product.1 = (f32[256,3584]{1,0:T(8,128)}, f32[256,3584]{1,0:T(8,128)}, bf16[256,3584]{1,0:T(8,128)(2,1)}) custom-call(s32[1]{0:T(128)} %bitcast.core_ref.core, bf16[128,5504]{1,0:T(8,128)(2,1)} %copy-done.8, bf16[128,5504]{1,0:T(8,128)(2,1)} %copy-done.10, bf16[512,1024]{1,0:T(8,128)(2,1)} %bitcast.44, f32[512,3584]{1,0:T(8,128)} %get-tuple-element.107.near), custom_call_target="tpu_custom_call" | custom-call | tf_op jit(solution)/shard_map/weight_product/pallas_call | solution.py:356
  220.5 2.9 %collective-permute-start.40 = (bf16[256,3584]{1,0:T(8,128)(2,1)}, bf16[256,3584]{1,0:T(8,128)(2,1)S(1)}, u32[]{:S(2)}, u32[]{:S(2)}) collective-permute-start(bf16[256,3584]{1,0:T(8,128)(2,1)} %get-tuple-element.108), channel_id=1, source_target_pairs={{0,1},{1,0},{2,3},{3,2},{4,5},{5,4},{6,7},{7,6},{8,9},{9,8},{10,11... | collective-permute-start | bytes 5505032 | tf_op jit(solution)/shard_map/ppermute | solution.py:62
  231.6 2.7 %down_product.1 = f32[1792,512]{1,0:T(8,128)} custom-call(bf16[128,5504]{1,0:T(8,128)(2,1)S(1)} %copy-done.9, bf16[128,5504]{1,0:T(8,128)(2,1)S(1)} %copy-done.11, bf16[128,5504]{1,0:T(8,128)(2,1)S(1)} %copy-done.9, bf16[128,5504]{1,0:T(8,128)(2,1)S(1)} %copy-done.11, bf16[1024,512]{1,0:T(8,128)(2,1)S(1)} %bitcast.37, f32[1,512]{1,0:T(1,128)S(1)} %bitcast.42, ...), custom_call_target="tpu_custom_call" | custom-call | tf_op jit(solution)/shard_map/down_product/pallas_call | solution.py:231
  (192 shorter events, 82.5 us)
Async XLA Ops:
  0.7 11.9 %collective-permute-start = (bf16[128,512]{1,0:T(8,128)(2,1)}, bf16[128,512]{1,0:T(8,128)(2,1)S(1)}, u32[]{:S(2)}, u32[]{:S(2)}) collective-permute-start(bf16[128,512]{1,0:T(8,128)(2,1)} %param.8), channel_id=1, source_target_pairs={{0,6},{1,7},{2,0},{3,1},{4,2},{5,3},{6,4},{7,5},{8,14},{9,15},{10,... | collective-permute-start | bytes 393224 | tf_op jit(solution)/shard_map/ppermute | solution.py:62
  5.3 10.0 %collective-permute-start.2 = (bf16[128,512]{1,0:T(8,128)(2,1)}, bf16[128,512]{1,0:T(8,128)(2,1)S(1)}, u32[]{:S(2)}, u32[]{:S(2)}) collective-permute-start(bf16[128,512]{1,0:T(8,128)(2,1)} %param.8), channel_id=1, source_target_pairs={{0,2},{1,3},{2,4},{3,5},{4,6},{5,7},{6,0},{7,1},{8,10},{9,11},{10,... | collective-permute-start | bytes 393224 | tf_op jit(solution)/shard_map/ppermute | solution.py:62
  6.0 10.8 %collective-permute-start.4 = (bf16[128,512]{1,0:T(8,128)(2,1)}, bf16[128,512]{1,0:T(8,128)(2,1)S(1)}, u32[]{:S(2)}, u32[]{:S(2)}) collective-permute-start(bf16[128,512]{1,0:T(8,128)(2,1)} %param.13), channel_id=1, source_target_pairs={{0,6},{1,7},{2,0},{3,1},{4,2},{5,3},{6,4},{7,5},{8,14},{9,15},{10,... | collective-permute-start | bytes 393224 | tf_op jit(solution)/shard_map/ppermute | solution.py:62
  8.0 8.9 %collective-permute-start.5 = (bf16[128,512]{1,0:T(8,128)(2,1)}, bf16[128,512]{1,0:T(8,128)(2,1)S(1)}, u32[]{:S(2)}, u32[]{:S(2)}) collective-permute-start(bf16[128,512]{1,0:T(8,128)(2,1)} %param.13), channel_id=1, source_target_pairs={{0,4},{1,5},{2,6},{3,7},{4,0},{5,1},{6,2},{7,3},{8,12},{9,13},{10,... | collective-permute-start | bytes 393224 | tf_op jit(solution)/shard_map/ppermute | solution.py:62
  33.9 19.1 %collective-permute-start.8 = (bf16[128,5504]{1,0:T(8,128)(2,1)S(1)}, bf16[128,5504]{1,0:T(8,128)(2,1)S(1)}, u32[]{:S(2)}, u32[]{:S(2)}) collective-permute-start(bf16[128,5504]{1,0:T(8,128)(2,1)S(1)} %get-tuple-element.67), channel_id=1, source_target_pairs={{0,8},{1,33},{2,10},{3,35},{4,12},{5,37},{6,14},{7,39},{8,16},{9,4... | collective-permute-start | bytes 4227080 | tf_op jit(solution)/shard_map/ppermute | solution.py:62
  35.3 17.8 %collective-permute-start.9 = (bf16[128,5504]{1,0:T(8,128)(2,1)S(1)}, bf16[128,5504]{1,0:T(8,128)(2,1)S(1)}, u32[]{:S(2)}, u32[]{:S(2)}) collective-permute-start(bf16[128,5504]{1,0:T(8,128)(2,1)S(1)} %get-tuple-element.68), channel_id=1, source_target_pairs={{0,24},{1,97},{2,26},{3,99},{4,28},{5,101},{6,30},{7,103},{8,0},{9... | collective-permute-start | bytes 4227080 | tf_op jit(solution)/shard_map/ppermute | solution.py:62
  55.1 34.4 %collective-permute-start.10 = (bf16[256,5504]{1,0:T(8,128)(2,1)S(1)}, bf16[256,5504]{1,0:T(8,128)(2,1)S(1)}, u32[]{:S(2)}, u32[]{:S(2)}) collective-permute-start(bf16[256,5504]{1,0:T(8,128)(2,1)S(1)} %add_halves.2), channel_id=1, source_target_pairs={{0,8},{1,33},{2,10},{3,35},{4,12},{5,37},{6,14},{7,39},{8,16},{9,4... | collective-permute-start | bytes 8454152 | tf_op jit(solution)/shard_map/ppermute | solution.py:62
  58.4 33.0 %collective-permute-start.11 = (bf16[256,5504]{1,0:T(8,128)(2,1)S(1)}, bf16[256,5504]{1,0:T(8,128)(2,1)S(1)}, u32[]{:S(2)}, u32[]{:S(2)}) collective-permute-start(bf16[256,5504]{1,0:T(8,128)(2,1)S(1)} %add_halves.3), channel_id=1, source_target_pairs={{0,24},{1,97},{2,26},{3,99},{4,28},{5,101},{6,30},{7,103},{8,0},{9... | collective-permute-start | bytes 8454152 | tf_op jit(solution)/shard_map/ppermute | solution.py:62
  100.2 15.3 %collective-permute-start.14 = (bf16[64,5504]{1,0:T(8,128)(2,1)S(1)}, bf16[64,5504]{1,0:T(8,128)(2,1)S(1)}, u32[]{:S(2)}, u32[]{:S(2)}) collective-permute-start(bf16[64,5504]{1,0:T(8,128)(2,1)S(1)} %pad_maximum_fusion.1), channel_id=1, source_target_pairs={{0,32},{1,9},{2,34},{3,11},{4,36},{5,13},{6,38},{7,15},{8,40},{9,1... | collective-permute-start | bytes 2113544 | tf_op jit(solution)/shard_map/ppermute | solution.py:62
  101.6 14.0 %collective-permute-start.15 = (bf16[64,5504]{1,0:T(8,128)(2,1)S(1)}, bf16[64,5504]{1,0:T(8,128)(2,1)}, u32[]{:S(2)}, u32[]{:S(2)}) collective-permute-start(bf16[64,5504]{1,0:T(8,128)(2,1)S(1)} %pad_maximum_fusion.2), channel_id=1, source_target_pairs={{0,96},{1,25},{2,98},{3,27},{4,100},{5,29},{6,102},{7,31},{8,104},... | collective-permute-start | bytes 2113544 | tf_op jit(solution)/shard_map/ppermute | solution.py:62
  129.8 8.1 %collective-permute-start.25 = (bf16[32,5504]{1,0:T(8,128)(2,1)S(1)}, bf16[32,5504]{1,0:T(8,128)(2,1)S(1)}, u32[]{:S(2)}, u32[]{:S(2)}) collective-permute-start(bf16[32,5504]{1,0:T(8,128)(2,1)S(1)} %get-tuple-element.139), channel_id=1, source_target_pairs={{0,96},{1,25},{2,98},{3,27},{4,100},{5,29},{6,102},{7,31},{8,104},... | collective-permute-start | bytes 1056776 | tf_op jit(solution)/shard_map/ppermute | solution.py:62
  130.1 11.6 %collective-permute-start.29 = (bf16[32,5504]{1,0:T(8,128)(2,1)S(1)}, bf16[32,5504]{1,0:T(8,128)(2,1)S(1)}, u32[]{:S(2)}, u32[]{:S(2)}) collective-permute-start(bf16[32,5504]{1,0:T(8,128)(2,1)S(1)} %get-tuple-element.139), channel_id=1, source_target_pairs={{0,32},{1,9},{2,34},{3,11},{4,36},{5,13},{6,38},{7,15},{8,40},{9,1... | collective-permute-start | bytes 1056776 | tf_op jit(solution)/shard_map/ppermute | solution.py:62
  131.3 19.6 %collective-permute-start.31 = (bf16[32,5504]{1,0:T(8,128)(2,1)S(1)}, bf16[32,5504]{1,0:T(8,128)(2,1)S(1)}, u32[]{:S(2)}, u32[]{:S(2)}) collective-permute-start(bf16[32,5504]{1,0:T(8,128)(2,1)S(1)} %get-tuple-element.138), channel_id=1, source_target_pairs={{0,32},{1,9},{2,34},{3,11},{4,36},{5,13},{6,38},{7,15},{8,40},{9,1... | collective-permute-start | bytes 1056776 | tf_op jit(solution)/shard_map/ppermute | solution.py:62
  134.1 8.0 %collective-permute-start.28 = (bf16[32,5504]{1,0:T(8,128)(2,1)S(1)}, bf16[32,5504]{1,0:T(8,128)(2,1)S(1)}, u32[]{:S(2)}, u32[]{:S(2)}) collective-permute-start(bf16[32,5504]{1,0:T(8,128)(2,1)S(1)} %collective-permute-done.24), channel_id=1, source_target_pairs={{0,96},{1,25},{2,98},{3,27},{4,100},{5,29},{6,102},{7,31},{8,104},... | collective-permute-start | bytes 1056776 | tf_op jit(solution)/shard_map/ppermute | solution.py:62
  139.1 19.5 %collective-permute-start.26 = (bf16[128,5504]{1,0:T(8,128)(2,1)}, bf16[128,5504]{1,0:T(8,128)(2,1)}, u32[]{:S(2)}, u32[]{:S(2)}) collective-permute-start(bf16[128,5504]{1,0:T(8,128)(2,1)} %pad_maximum_fusion.refs_0_.refs_6_), channel_id=1, source_target_pairs={{0,24},{1,97},{2,26},{3,99},{4,28},{5,101},{6,30},{7,103},{8,0},{9... | collective-permute-start | bytes 4227080 | tf_op jit(solution)/shard_map/ppermute | solution.py:62
  141.7 8.4 %collective-permute-start.30 = (bf16[32,5504]{1,0:T(8,128)(2,1)S(1)}, bf16[32,5504]{1,0:T(8,128)(2,1)S(1)}, u32[]{:S(2)}, u32[]{:S(2)}) collective-permute-start(bf16[32,5504]{1,0:T(8,128)(2,1)S(1)} %collective-permute-done.29), channel_id=1, source_target_pairs={{0,32},{1,9},{2,34},{3,11},{4,36},{5,13},{6,38},{7,15},{8,40},{9,1... | collective-permute-start | bytes 1056776 | tf_op jit(solution)/shard_map/ppermute | solution.py:62
  152.4 19.3 %collective-permute-start.32 = (bf16[128,5504]{1,0:T(8,128)(2,1)}, bf16[128,5504]{1,0:T(8,128)(2,1)}, u32[]{:S(2)}, u32[]{:S(2)}) collective-permute-start(bf16[128,5504]{1,0:T(8,128)(2,1)} %constant_dynamic-update-slice_fusion.8.refs_1_.refs_7_), channel_id=1, source_target_pairs={{0,8},{1,33},{2,10},{3,35},{4,12},{5,37},{6,14},{7,39},{8,16},{9,4... | collective-permute-start | bytes 4227080 | tf_op jit(solution)/shard_map/ppermute | solution.py:62
  152.4 34.4 %collective-permute-start.35 = (bf16[128,5504]{1,0:T(8,128)(2,1)}, bf16[128,5504]{1,0:T(8,128)(2,1)}, u32[]{:S(2)}, u32[]{:S(2)}) collective-permute-start(bf16[128,5504]{1,0:T(8,128)(2,1)} %pad_maximum_fusion.refs_0_.refs_6_), channel_id=1, source_target_pairs={{0,8},{1,33},{2,10},{3,35},{4,12},{5,37},{6,14},{7,39},{8,16},{9,4... | collective-permute-start | bytes 4227080 | tf_op jit(solution)/shard_map/ppermute | solution.py:62
  152.4 34.4 %collective-permute-start.34 = (bf16[128,5504]{1,0:T(8,128)(2,1)}, bf16[128,5504]{1,0:T(8,128)(2,1)}, u32[]{:S(2)}, u32[]{:S(2)}) collective-permute-start(bf16[128,5504]{1,0:T(8,128)(2,1)} %constant_dynamic-update-slice_fusion.8.refs_1_.refs_7_), channel_id=1, source_target_pairs={{0,24},{1,97},{2,26},{3,99},{4,28},{5,101},{6,30},{7,103},{8,0},{9... | collective-permute-start | bytes 4227080 | tf_op jit(solution)/shard_map/ppermute | solution.py:62
  158.6 44.9 %collective-permute-start.27 = (bf16[128,5504]{1,0:T(8,128)(2,1)}, bf16[128,5504]{1,0:T(8,128)(2,1)S(1)}, u32[]{:S(2)}, u32[]{:S(2)}) collective-permute-start(bf16[128,5504]{1,0:T(8,128)(2,1)} %collective-permute-done.26.refs_2_.refs_8_), channel_id=1, source_target_pairs={{0,24},{1,97},{2,26},{3,99},{4,28},{5,101},{6,30},{7,103},{8,0},{9... | collective-permute-start | bytes 4227080 | tf_op jit(solution)/shard_map/ppermute | solution.py:62
  171.8 31.7 %collective-permute-start.33 = (bf16[128,5504]{1,0:T(8,128)(2,1)}, bf16[128,5504]{1,0:T(8,128)(2,1)S(1)}, u32[]{:S(2)}, u32[]{:S(2)}) collective-permute-start(bf16[128,5504]{1,0:T(8,128)(2,1)} %collective-permute-done.32.refs_5_.refs_11_), channel_id=1, source_target_pairs={{0,8},{1,33},{2,10},{3,35},{4,12},{5,37},{6,14},{7,39},{8,16},{9,4... | collective-permute-start | bytes 4227080 | tf_op jit(solution)/shard_map/ppermute | solution.py:62
  220.5 13.8 %collective-permute-start.40 = (bf16[256,3584]{1,0:T(8,128)(2,1)}, bf16[256,3584]{1,0:T(8,128)(2,1)S(1)}, u32[]{:S(2)}, u32[]{:S(2)}) collective-permute-start(bf16[256,3584]{1,0:T(8,128)(2,1)} %get-tuple-element.108), channel_id=1, source_target_pairs={{0,1},{1,0},{2,3},{3,2},{4,5},{5,4},{6,7},{7,6},{8,9},{9,8},{10,11... | collective-permute-start | bytes 5505032 | tf_op jit(solution)/shard_map/ppermute | solution.py:62
  227.8 8.6 %collective-permute-start.37 = (bf16[128,512]{1,0:T(8,128)(2,1)S(1)}, bf16[128,512]{1,0:T(8,128)(2,1)S(1)}, u32[]{:S(2)}, u32[]{:S(2)}) collective-permute-start(bf16[128,512]{1,0:T(8,128)(2,1)S(1)} %get-tuple-element.104), channel_id=1, source_target_pairs={{0,2},{1,3},{2,4},{3,5},{4,6},{5,7},{6,0},{7,1},{8,10},{9,11},{10,... | collective-permute-start | bytes 393224 | tf_op jit(solution)/shard_map/ppermute | solution.py:62
  228.2 8.2 %collective-permute-start.38 = (bf16[128,512]{1,0:T(8,128)(2,1)S(1)}, bf16[128,512]{1,0:T(8,128)(2,1)S(1)}, u32[]{:S(2)}, u32[]{:S(2)}) collective-permute-start(bf16[128,512]{1,0:T(8,128)(2,1)S(1)} %get-tuple-element.105), channel_id=1, source_target_pairs={{0,4},{1,5},{2,6},{3,7},{4,0},{5,1},{6,2},{7,3},{8,12},{9,13},{10,... | collective-permute-start | bytes 393224 | tf_op jit(solution)/shard_map/ppermute | solution.py:62
  (41 other events, 360.8 us)
